TPU v7x, 32 devices: a whole 2x2x4 slice. The times are simulated.
32 devices in a mesh: groups: 2 (over x), seq: 8 (over z, y), sub: 2 (over core).
Axes of the slice: x: 2, y: 2, z: 4, core: 2. Of those that a mesh axis runs over, the one named last changes fastest.
Arguments:
- frames: bfloat16 [2048, 1024], P(('groups', 'seq', 'sub')), parts along dimension 0, may hold values from -6 to 6
- fine_gain: float32 [1024], replicated, may hold values from 0.1 to 1.9
- dw_kernel: bfloat16 [5, 1024], replicated, may hold values from -3 to 3
- w_down: bfloat16 [4096, 4096], P(None, 'seq'), may hold values from -0.21875 to 0.21875
- coarse_gain: float32 [4096], replicated, may hold values from 0.1 to 1.9
- w_qkv: bfloat16 [3, 4096, 4096], P(None, None, 'seq'), may hold values from -1.609375 to 1.609375
- w_out: bfloat16 [4096, 4096], P('seq'), may hold values from -0.09375 to 0.09375
- w_up: bfloat16 [4096, 4096], P('seq'), may hold values from -0.09375 to 0.09375
Outputs:
- denoised: bfloat16 [2048, 1024], P(('groups', 'seq', 'sub')), parts along dimension 0
There are 2 independent parts, one for each index of `groups`. A program takes and returns all parts, laid end to end along the dimension named above; an argument that names none is the same for every part. Nothing has to cross between parts.
All inputs are finite; a program needn't handle non-finite values.
Results may differ from a plain program's by a relative error of at most 0.012.
Values may be sent and summed in bfloat16 or wider, within the bound.
No kernel may reach another device: no remote copies, remote signals or barrier semaphores. Data moves between devices by JAX's collectives and lax.ppermute only.
A program may use at most 128 MiB of HBM per device.

v0:
```python
import math

import jax
import jax.numpy as jnp
from jax import lax
from jax.sharding import PartitionSpec as P

DF = 1024
HD = 128
KW = 5


epsilon = 1e-06


def padded_2(array, sides, width):
    for axis, dim in sides:
        size, length = (lax.axis_size(axis), array.shape[dim])
        up = [(i, (i + 1) % size) for i in range(size - 1)]
        down = [(j, i) for i, j in up]
        last = lax.slice_in_dim(array, length - width, length, axis=dim)
        leading = lax.slice_in_dim(array, 0, width, axis=dim)
        before = lax.ppermute(last, axis, up)
        after = lax.ppermute(leading, axis, down)
        array = jnp.concatenate([before, array, after], axis=dim)
    return array


def partner(value, axis, bit):
    mask = 2**bit
    pairs = [(source, source ^ mask) for source in range(lax.axis_size(axis))]
    return lax.ppermute(value, axis, pairs)


def attend(queries, keys_all, values_all, heads_here):
    row_total = queries.shape[0]
    block_rows = min(row_total, 512)
    key_heads = keys_all.reshape(keys_all.shape[0], heads_here, HD)
    value_heads = values_all.reshape(values_all.shape[0], heads_here, HD)
    query_blocks = queries.reshape(row_total // block_rows, block_rows, heads_here, HD)
    score_scale = 1.0 / math.sqrt(HD)

    def one_block(query_block):
        scores = (
            jnp.einsum("qhd,khd->hqk", query_block, key_heads, preferred_element_type=jnp.float32)
            * score_scale
        )
        peak = jnp.max(scores, axis=2, keepdims=True)
        weights = jnp.exp(scores - peak)
        weights = (weights / jnp.sum(weights, axis=2, keepdims=True)).astype(jnp.bfloat16)
        return jnp.einsum(
            "hqk,khd->qhd", weights, value_heads, preferred_element_type=jnp.float32
        ).astype(jnp.bfloat16)

    outputs = lax.map(one_block, query_blocks)
    return outputs.reshape(row_total, heads_here * HD)


def per_device(frames, fine_gain, dw_kernel, w_down, coarse_gain, w_qkv, w_out, w_up):
    frame_rows = frames.shape[0]
    heads_here = w_qkv.shape[2] // HD
    frames_f32 = frames.astype(jnp.float32)
    normed_fine = (
        frames_f32
        * lax.rsqrt(jnp.mean(frames_f32 * frames_f32, axis=1, keepdims=True) + epsilon)
        * fine_gain
    ).astype(jnp.bfloat16)
    padded = padded_2(normed_fine, ((("seq", "sub"), 0),), KW // 2)
    convolved = jnp.zeros((frame_rows, DF), jnp.float32)
    for offset in range(KW):
        convolved = convolved + padded[offset : offset + frame_rows].astype(
            jnp.float32
        ) * dw_kernel[offset].astype(jnp.float32)
    patches = convolved.astype(jnp.bfloat16).reshape(frame_rows // 4, 4 * DF)
    coarse = jnp.dot(
        lax.all_gather(patches, "seq", axis=0, tiled=True),
        w_down,
        preferred_element_type=jnp.float32,
    ).astype(jnp.bfloat16)
    coarse_f32 = coarse.astype(jnp.float32)
    whole = lax.all_gather(coarse, "seq", axis=1, tiled=True).astype(jnp.float32)
    normed_coarse = (
        whole * lax.rsqrt(jnp.mean(whole * whole, axis=1, keepdims=True) + epsilon) * coarse_gain
    ).astype(jnp.bfloat16)
    queries = jnp.dot(normed_coarse, w_qkv[0], preferred_element_type=jnp.float32).astype(
        jnp.bfloat16
    )
    own_keys = jnp.dot(normed_coarse, w_qkv[1], preferred_element_type=jnp.float32).astype(
        jnp.bfloat16
    )
    own_values = jnp.dot(normed_coarse, w_qkv[2], preferred_element_type=jnp.float32).astype(
        jnp.bfloat16
    )
    other_keys, other_values = partner((own_keys, own_values), "sub", 0)
    keys_all = jnp.concatenate([own_keys, other_keys], axis=0)
    values_all = jnp.concatenate([own_values, other_values], axis=0)
    attended = attend(queries, keys_all, values_all, heads_here)
    partial_out = jnp.dot(attended, w_out, preferred_element_type=jnp.float32)
    projected = lax.psum_scatter(
        partial_out.astype(jnp.bfloat16), "seq", scatter_dimension=1, tiled=True
    ).astype(jnp.float32)
    mixed = (coarse_f32 + projected).astype(jnp.bfloat16)
    lifted = lax.psum_scatter(
        jnp.dot(mixed, w_up, preferred_element_type=jnp.float32),
        "seq",
        scatter_dimension=0,
        tiled=True,
    )
    return (frames_f32 + lifted.reshape(frame_rows, DF)).astype(jnp.bfloat16)


def solution(mesh):
    placed = (
        P(("groups", "seq", "sub"), None),
        P(),
        P(),
        P(None, "seq"),
        P(),
        P(None, None, "seq"),
        P("seq", None),
        P("seq", None),
    )
    return jax.shard_map(
        per_device,
        mesh=mesh,
        in_specs=placed,
        out_specs=P(("groups", "seq", "sub"), None),
        check_vma=False,
    )
```

profile of v0, /device:TPU:0, one launch (start us, length us, event | category | flops | bytes accessed | tf_op | source)
XLA Modules:
  0.0 262.8 jit_solution(18423422648642373346)
XLA Ops:
  6.5 0.0 copy-start.3
  6.5 0.0 all-gather.3.cloned.1.call-start
  6.5 1.0 fusion.27
  7.6 1.0 fusion.29
  8.6 2.4 collective-permute-start
  11.0 1.3 collective-permute-start.1
  12.3 0.9 slice_convert_fusion.4
  13.2 0.0 collective-permute-done
  13.2 3.0 %collective-permute-done.1 = bf16[2,1024]{1,0:T(2,128)(2,1)S(1)} collective-permute-done((bf16[2,1024]{1,0:T(2,128)(2,1)S(1)}, bf16[2,1024]{1,0:T(2,128)(2,1)S(1)}, u32[]{:S(2)}, u32[]{:S(2)}) %collective-permute-start.1) | collective-permute-done | bytes 4128 | tf_op jit(solution)/shard_map/ppermute | solution.py:24
  16.2 0.2 add_convert_fusion.1
  16.4 0.7 reshape.38
  17.1 0.0 all-gather.3.cloned.1.call-update
  17.1 0.0 all-gather.5.cloned.1.call-start
  17.2 43.4 %all-gather.3.cloned.1.call-done = bf16[128,4096]{1,0:T(8,128)(2,1)} async-done(((bf16[16,4096]{1,0:T(8,128)(2,1)}), bf16[128,4096]{1,0:T(8,128)(2,1)}) %all-gather.3.cloned.1.call-update) | async-done | bytes 1048592 | tf_op jit(solution)/shard_map/all_gather | solution.py:76
  60.6 3.9 %convolution_convert_fusion.2 = bf16[128,512]{1,0:T(8,128)(2,1)} fusion(bf16[128,4096]{1,0:T(8,128)(2,1)} %all-gather.3.cloned.1.call-done, bf16[4096,512]{1,0:T(8,128)(2,1)} %param.11), kind=kOutput, calls=%fused_computation.23 | convolution fusion | flops 536936448 | bytes 5373952 | tf_op jit(solution)/shard_map/dot_general | solution.py:75
  64.5 0.0 all-gather.5.cloned.1.call-update
  64.5 0.0 reduce-scatter.3.cloned.1.call-start
  64.6 38.4 %all-gather.5.cloned.1.call-done = bf16[128,4096]{1,0:T(8,128)(2,1)} async-done(((bf16[128,512]{1,0:T(8,128)(2,1)}), bf16[128,4096]{1,0:T(8,128)(2,1)}) %all-gather.5.cloned.1.call-update) | async-done | bytes 1048592 | tf_op jit(solution)/shard_map/all_gather | solution.py:81
  103.0 0.0 copy-start.2
  103.0 1.6 fusion.10
  104.6 0.0 copy-done.3
  104.6 3.3 %fusion.15 = bf16[128,512]{1,0:T(8,128)(2,1)S(1)} fusion(bf16[3,4096,512]{2,1,0:T(8,128)(2,1)} %param.13, bf16[128,4096]{1,0:T(8,128)(2,1)} %all-gather.5.cloned.1.call-done, f32[4096]{0:T(1024)S(1)} %copy-done.3, f32[128]{0:T(128)S(1)} %add_rsqrt_fusion), kind=kOutput, calls=%fused_computation.19 | convolution fusion | flops 539033600 | bytes 5390848 | tf_op jit(solution)/shard_map/dot_general | solution.py:91
  107.9 0.1 collective-permute-start.2
  107.9 0.0 copy-done.2
  107.9 3.0 %fusion.21 = bf16[128,512]{1,0:T(8,128)(2,1)S(1)} fusion(bf16[3,4096,512]{2,1,0:T(8,128)(2,1)} %param.13, bf16[128,4096]{1,0:T(8,128)(2,1)S(1)} %copy-done.2, f32[4096]{0:T(1024)S(1)} %copy-done.3, f32[128]{0:T(128)S(1)} %add_rsqrt_fusion), kind=kOutput, calls=%fused_computation.21 | convolution fusion | flops 539033600 | bytes 5390848 | tf_op jit(solution)/shard_map/dot_general | solution.py:88
  110.9 0.6 collective-permute-start.3
  111.5 2.9 %fusion.24 = bf16[16,4,8,128]{3,2,1,0:T(8,128)(2,1)S(1)} fusion(bf16[3,4096,512]{2,1,0:T(8,128)(2,1)} %param.13, bf16[128,4096]{1,0:T(8,128)(2,1)S(1)} %copy-done.2, f32[4096]{0:T(1024)S(1)} %copy-done.3, f32[128]{0:T(128)S(1)} %add_rsqrt_fusion), kind=kOutput, calls=%fused_computation.24 | convolution fusion | flops 539033600 | bytes 5390848 | tf_op jit(solution)/shard_map/dot_general | solution.py:85
  114.4 0.0 collective-permute-done.2
  114.5 0.1 copy.12
  114.6 0.0 collective-permute-done.3
  114.6 0.4 fusion.49
  115.0 0.2 convolution_multiply_fusion
  115.3 0.0 copy-start.1
  115.3 1.0 convolution_convert_fusion.1
  116.3 3.9 %convolution_convert_fusion = bf16[128,4096]{1,0:T(8,128)(2,1)} fusion(bf16[128,512]{0,1:T(8,128)(2,1)S(1)} %bitcast.57, bf16[512,4096]{1,0:T(8,128)(2,1)} %param.14), kind=kOutput, calls=%fused_computation.1 | convolution fusion | flops 537395200 | bytes 5373952 | tf_op jit(solution)/shard_map/dot_general | solution.py:98
  120.2 0.0 reduce-scatter.3.cloned.1.call-update
  120.3 0.0 copy-start
  120.3 0.0 reduce-scatter.5.cloned.1.call-start
  120.3 62.8 %reduce-scatter.3.cloned.1.call-done = bf16[128,512]{1,0:T(8,128)(2,1)} async-done(((bf16[128,4096]{1,0:T(8,128)(2,1)}), bf16[128,512]{1,0:T(8,128)(2,1)}) %reduce-scatter.3.cloned.1.call-update) | async-done | bytes 131088 | tf_op jit(solution)/shard_map/reduce_scatter | solution.py:99
  183.2 0.0 copy-done.1
  183.2 4.3 %fusion.36 = f32[128,4096]{1,0:T(8,128)} fusion(bf16[512,4096]{1,0:T(8,128)(2,1)} %param.15, bf16[128,512]{1,0:T(8,128)(2,1)} %reduce-scatter.3.cloned.1.call-done, bf16[128,512]{1,0:T(8,128)(2,1)S(1)} %copy-done.1), kind=kOutput, calls=%fused_computation.46 | convolution fusion | flops 537133056 | bytes 6553600 | tf_op jit(solution)/shard_map/dot_general | solution.py:104
  187.5 0.0 reduce-scatter.5.cloned.1.call-update
  187.5 67.0 %reduce-scatter.5.cloned.1.call-done = f32[16,4096]{1,0:T(8,128)} async-done(((f32[128,4096]{1,0:T(8,128)}), f32[16,4096]{1,0:T(8,128)}) %reduce-scatter.5.cloned.1.call-update) | async-done | bytes 262160 | tf_op jit(solution)/shard_map/reduce_scatter | solution.py:103
  254.5 1.0 reshape.42
  255.5 0.0 copy-done
  255.5 0.7 fusion.30
  (4 shorter events, 0.0 us)
Async XLA Ops:
  6.5 98.0 %copy-start.3 = (f32[4096]{0:T(1024)S(1)}, f32[4096]{0:T(1024)}, u32[]{:S(2)}) copy-start(f32[4096]{0:T(1024)} %param.12) | copy-start | bytes 49156
  6.5 54.1 %all-gather.3.cloned.1.call-start = ((), (), s32[]{:S(2)}) async-start(), calls=%async_computation.2 | async-start | bytes 1179648 | tf_op jit(solution)/shard_map/all_gather | solution.py:76
  8.6 4.6 %collective-permute-start = (bf16[2,1024]{1,0:T(2,128)(2,1)S(1)}, bf16[2,1024]{1,0:T(2,128)(2,1)S(1)}, u32[]{:S(2)}, u32[]{:S(2)}) collective-permute-start(bf16[2,1024]{1,0:T(2,128)(2,1)S(1)} %get-tuple-element.13), channel_id=1, source_target_pairs={{0,1},{1,2},{2,3},{3,4},{4,5},{5,6},{6,7},{7,8},{8,9},{9,10},{10,1... | collective-permute-start | bytes 12296 | tf_op jit(solution)/shard_map/ppermute | solution.py:23
  11.0 5.2 %collective-permute-start.1 = (bf16[2,1024]{1,0:T(2,128)(2,1)S(1)}, bf16[2,1024]{1,0:T(2,128)(2,1)S(1)}, u32[]{:S(2)}, u32[]{:S(2)}) collective-permute-start(bf16[2,1024]{1,0:T(2,128)(2,1)S(1)} %get-tuple-element.14), channel_id=1, source_target_pairs={{1,0},{2,1},{3,2},{4,3},{5,4},{6,5},{7,6},{8,7},{9,8},{10,9},{11,1... | collective-permute-start | bytes 12296 | tf_op jit(solution)/shard_map/ppermute | solution.py:24
  17.1 85.8 %all-gather.5.cloned.1.call-start = ((), (), s32[]{:S(2)}) async-start(), calls=%async_computation.3 | async-start | bytes 1179648 | tf_op jit(solution)/shard_map/all_gather | solution.py:81
  64.5 118.6 %reduce-scatter.3.cloned.1.call-start = ((), (), s32[]{:S(2)}) async-start(), calls=%async_computation.4 | async-start | bytes 1179648 | tf_op jit(solution)/shard_map/reduce_scatter | solution.py:99
  103.0 5.0 %copy-start.2 = (bf16[128,4096]{1,0:T(8,128)(2,1)S(1)}, bf16[128,4096]{1,0:T(8,128)(2,1)}, u32[]{:S(2)}) copy-start(bf16[128,4096]{1,0:T(8,128)(2,1)} %all-gather.5.cloned.1.call-done) | copy-start | bytes 3145732
  107.9 6.6 %collective-permute-start.2 = (bf16[128,512]{1,0:T(8,128)(2,1)S(1)}, bf16[128,512]{1,0:T(8,128)(2,1)S(1)}, u32[]{:S(2)}, u32[]{:S(2)}) collective-permute-start(bf16[128,512]{1,0:T(8,128)(2,1)S(1)} %fusion.15), channel_id=1, source_target_pairs={{0,1},{1,0},{2,3},{3,2},{4,5},{5,4},{6,7},{7,6},{8,9},{9,8},{10,11... | collective-permute-start | bytes 393224 | tf_op jit(solution)/shard_map/ppermute | solution.py:32
  110.9 3.7 %collective-permute-start.3 = (bf16[128,512]{1,0:T(8,128)(2,1)S(1)}, bf16[128,512]{1,0:T(8,128)(2,1)S(1)}, u32[]{:S(2)}, u32[]{:S(2)}) collective-permute-start(bf16[128,512]{1,0:T(8,128)(2,1)S(1)} %fusion.21), channel_id=1, source_target_pairs={{0,1},{1,0},{2,3},{3,2},{4,5},{5,4},{6,7},{7,6},{8,9},{9,8},{10,11... | collective-permute-start | bytes 393224 | tf_op jit(solution)/shard_map/ppermute | solution.py:32
  115.3 67.9 %copy-start.1 = (bf16[128,512]{1,0:T(8,128)(2,1)S(1)}, bf16[128,512]{1,0:T(8,128)(2,1)}, u32[]{:S(2)}) copy-start(bf16[128,512]{1,0:T(8,128)(2,1)} %convolution_convert_fusion.2) | copy-start | bytes 393220
  120.3 135.3 %copy-start = (bf16[64,1024]{1,0:T(8,128)(2,1)S(1)}, bf16[64,1024]{1,0:T(8,128)(2,1)}, u32[]{:S(2)}) copy-start(bf16[64,1024]{1,0:T(8,128)(2,1)} %param.8) | copy-start | bytes 393220
  120.3 134.2 %reduce-scatter.5.cloned.1.call-start = ((), (), s32[]{:S(2)}) async-start(), calls=%async_computation.5 | async-start | bytes 2359296 | tf_op jit(solution)/shard_map/reduce_scatter | solution.py:103
Sparse Core Ops, SparseCore 0:
  17.3 43.2 all-gather.2
  64.6 38.2 all-gather.4
  120.4 62.7 reduce-scatter.2
  187.6 66.8 reduce-scatter.4
where the time goes:
time: 263 us
  waiting for transfers between devices  215 us (82%)
  matrix products  23 us (9%)
  between operations  13.3 us (5%)
  other arithmetic  5.48 us (2%)
  starting transfers between devices  4.4 us (2%)
    reduce_scatter x1, waiting for transfers between devices, per_device(): lax.psum_scatter(jnp.dot(mixed, w_up, preferred_element_type=jnp.float32)...  67 us
    reduce_scatter x1, waiting for transfers between devices, per_device(): lax.psum_scatter(partial_out.astype(jnp.bfloat16), 'seq', scatter_dimensi...  62.8 us
    all_gather x1, waiting for transfers between devices, per_device(): lax.all_gather(patches, 'seq', axis=0, tiled=True)  43.4 us
    all_gather x1, waiting for transfers between devices, per_device(): lax.all_gather(coarse, 'seq', axis=1, tiled=True).astype(jnp.float32)  38.4 us
  transfers between devices with their start and end apart: 8, of which 5 were waited for; matrix products, arithmetic and copies ran while one was open for 3% of the time, Pallas kernels for 0%

commit v1 on v0

v1 whole, which is shorter than its diff:
```python
import math

import jax
import jax.numpy as jnp
from jax import lax
from jax.sharding import PartitionSpec as P

DF = 1024
HD = 128
KW = 5


epsilon = 1e-06


def padded_2(array, sides, width):
    for axis, dim in sides:
        size, length = (lax.axis_size(axis), array.shape[dim])
        up = [(i, (i + 1) % size) for i in range(size - 1)]
        down = [(j, i) for i, j in up]
        last = lax.slice_in_dim(array, length - width, length, axis=dim)
        leading = lax.slice_in_dim(array, 0, width, axis=dim)
        before = lax.ppermute(last, axis, up)
        after = lax.ppermute(leading, axis, down)
        array = jnp.concatenate([before, array, after], axis=dim)
    return array


def flip(value, axis, mask):
    pairs = [(source, source ^ mask) for source in range(lax.axis_size(axis))]
    return lax.ppermute(value, axis, pairs)


def relayed(mask, size):
    return mask & 1 == 1 and mask >= max(size // 2, 2)


def gather_flips(value, axis):
    size = lax.axis_size(axis)
    blocks = [value] + [None] * (size - 1)
    order = sorted(range(1, size), reverse=True)
    for mask in order:
        if not relayed(mask, size):
            blocks[mask] = flip(value, axis, mask)
    for mask in order:
        if relayed(mask, size):
            blocks[mask] = flip(blocks[mask ^ 1], axis, 1)
    return blocks


def scatter_flips(chunk_of, axis):
    size = lax.axis_size(axis)
    order = sorted(range(1, size), reverse=True)
    passed = {}
    for mask in order:
        if relayed(mask, size):
            passed[mask ^ 1] = flip(chunk_of(mask).astype(jnp.bfloat16), axis, 1)
    total = chunk_of(0)
    arrived = []
    for mask in order:
        if not relayed(mask, size):
            chunk = chunk_of(mask)
            if mask in passed:
                chunk = chunk + passed[mask].astype(jnp.float32)
            arrived.append(flip(chunk.astype(jnp.bfloat16), axis, mask))
    for value in arrived:
        total = total + value.astype(jnp.float32)
    return total


def in_index_order(stacked, axis):
    me, size = lax.axis_index(axis), lax.axis_size(axis)
    bit = 1
    while bit < size:
        shape = stacked.shape
        split = stacked.reshape((size // (2 * bit), 2, bit) + shape[1:])
        stacked = jnp.where((me & bit) != 0, split[:, ::-1], split).reshape(shape)
        bit *= 2
    return stacked


def attend(queries, keys_all, values_all, heads_here):
    row_total = queries.shape[0]
    query_heads = queries.reshape(row_total, heads_here, HD)
    key_heads = keys_all.reshape(keys_all.shape[0], heads_here, HD)
    value_heads = values_all.reshape(values_all.shape[0], heads_here, HD)
    scores = jnp.einsum(
        "qhd,khd->hqk", query_heads, key_heads, preferred_element_type=jnp.float32
    ) * (1.0 / math.sqrt(HD))
    peak = jnp.max(scores, axis=2, keepdims=True)
    weights = jnp.exp(scores - peak)
    weights = (weights / jnp.sum(weights, axis=2, keepdims=True)).astype(jnp.bfloat16)
    return (
        jnp.einsum("hqk,khd->qhd", weights, value_heads, preferred_element_type=jnp.float32)
        .astype(jnp.bfloat16)
        .reshape(row_total, heads_here * HD)
    )


def per_device(frames, fine_gain, dw_kernel, w_down, coarse_gain, w_qkv, w_out, w_up):
    frame_rows = frames.shape[0]
    columns = w_qkv.shape[2]
    heads_here = columns // HD
    me, size = lax.axis_index("seq"), lax.axis_size("seq")
    frames_f32 = frames.astype(jnp.float32)
    normed_fine = (
        frames_f32
        * lax.rsqrt(jnp.mean(frames_f32 * frames_f32, axis=1, keepdims=True) + epsilon)
        * fine_gain
    ).astype(jnp.bfloat16)
    padded = padded_2(normed_fine, ((("seq", "sub"), 0),), KW // 2)
    convolved = jnp.zeros((frame_rows, DF), jnp.float32)
    for offset in range(KW):
        convolved = convolved + padded[offset : offset + frame_rows].astype(
            jnp.float32
        ) * dw_kernel[offset].astype(jnp.float32)
    own_tokens = frame_rows // 4
    tokens = own_tokens * size
    patches = convolved.astype(jnp.bfloat16).reshape(own_tokens, 4 * DF)
    all_patches = jnp.concatenate(gather_flips(patches, "seq"), axis=0)
    coarse = jnp.dot(all_patches, w_down, preferred_element_type=jnp.float32).astype(jnp.bfloat16)
    coarse = in_index_order(coarse.reshape(size, own_tokens, columns), "seq").reshape(
        tokens, columns
    )

    coarse_f32 = coarse.astype(jnp.float32)
    blocks = gather_flips(coarse, "seq")
    squares = jnp.zeros((tokens, 1), jnp.float32)
    products = [jnp.zeros((tokens, columns), jnp.float32) for _ in range(3)]
    for mask in sorted(range(size), key=lambda m: (relayed(m, size), m)):
        start = (me ^ mask) * columns
        block = blocks[mask].astype(jnp.float32)
        squares = squares + jnp.sum(block * block, axis=1, keepdims=True)
        gained = (block * lax.dynamic_slice_in_dim(coarse_gain, start, columns)).astype(jnp.bfloat16)
        for which in range(3):
            piece = lax.dynamic_slice(w_qkv, (which, start, 0), (1, columns, columns))[0]
            products[which] = products[which] + jnp.dot(
                gained, piece, preferred_element_type=jnp.float32
            )
    scale = lax.rsqrt(squares / (columns * size) + epsilon)
    queries, own_keys, own_values = [(p * scale).astype(jnp.bfloat16) for p in products]
    other_keys, other_values = flip(own_keys, "sub", 1), flip(own_values, "sub", 1)
    keys_all = jnp.concatenate([own_keys, other_keys], axis=0)
    values_all = jnp.concatenate([own_values, other_values], axis=0)
    attended = attend(queries, keys_all, values_all, heads_here)

    def out_chunk(mask):
        piece = lax.dynamic_slice_in_dim(w_out, (me ^ mask) * columns, columns, axis=1)
        return jnp.dot(attended, piece, preferred_element_type=jnp.float32)

    mixed = (coarse_f32 + scatter_flips(out_chunk, "seq")).astype(jnp.bfloat16)
    lifted_part = jnp.dot(mixed, w_up, preferred_element_type=jnp.float32)

    def up_chunk(mask):
        return lax.dynamic_slice_in_dim(lifted_part, (me ^ mask) * own_tokens, own_tokens, axis=0)

    lifted = scatter_flips(up_chunk, "seq")
    return (frames_f32 + lifted.reshape(frame_rows, DF)).astype(jnp.bfloat16)


def solution(mesh):
    placed = (
        P(("groups", "seq", "sub"), None),
        P(),
        P(),
        P(None, "seq"),
        P(),
        P(None, None, "seq"),
        P("seq", None),
        P("seq", None),
    )
    return jax.shard_map(
        per_device,
        mesh=mesh,
        in_specs=placed,
        out_specs=P(("groups", "seq", "sub"), None),
        check_vma=False,
    )
```

time: 263 us -> 138 us (0.52)
  waiting for transfers between devices: 215 us -> 37.6 us
  starting transfers between devices: 4.4 us -> 42.6 us
  matrix products: 23 us -> 47.8 us
  between operations: 13.3 us -> 0.64 us
    reduce_scatter x2 -> x0, waiting for transfers between devices: 130 us -> none  [the longest x1 67 us: per_device(): lax.psum_scatter(jnp.dot(mixed, w_up, preferred_element_type=jnp.float32)...]
    all_gather x2 -> x0, waiting for transfers between devices: 81.8 us -> none  [the longest x1 43.4 us: per_device(): lax.all_gather(patches, 'seq', axis=0, tiled=True)]
    ppermute x2 -> x30, starting transfers between devices: 0.62 us -> 39 us  [flip(): return lax.ppermute(value, axis, pairs)]
    ppermute x2 -> x30, waiting for transfers between devices: 0.01 us -> 35.7 us  [flip(): return lax.ppermute(value, axis, pairs)]
    dot_general x8 -> x35, matrix products: 22.6 us -> 47.4 us  [the longest x24 30.7 us: per_device(): jnp.dot(gained, piece, preferred_element_type=jnp.float32)]
  transfers between devices with their start and end apart: 8 -> 32, of which waited for: 5 -> 12; matrix products, arithmetic and copies ran while one was open for 3% -> 26% of each run, Pallas kernels for 0% -> 0%
where the time goes in v1:
time: 138 us; the launch traced here: 136 us
  matrix products  47.8 us (35%)
  starting transfers between devices  42.6 us (31%)
  waiting for transfers between devices  37.6 us (27%)
  other arithmetic  5.65 us (4%)
  local copies, waits for them, and re-layouts  1.46 us (1%)
    ppermute x30, starting transfers between devices, flip(): return lax.ppermute(value, axis, pairs)  39 us
    ppermute x30, waiting for transfers between devices, flip(): return lax.ppermute(value, axis, pairs)  35.7 us
    dot_general x24, matrix products, per_device(): jnp.dot(gained, piece, preferred_element_type=jnp.float32)  30.7 us
    dot_general x7, matrix products, out_chunk(): return jnp.dot(attended, piece, preferred_element_type=jnp.float32)  9.06 us
    dot_general x1, matrix products, per_device(): lifted_part = jnp.dot(mixed, w_up, preferred_element_type=jnp.float32)  3.35 us
    dot_general x1, matrix products, per_device(): jnp.dot(all_patches, w_down, preferred_element_type=jnp.float32)  2.97 us
  transfers between devices with their start and end apart: 32, of which 12 were waited for; matrix products, arithmetic and copies ran while one was open for 26% of the time, Pallas kernels for 0%

profile of v1, /device:TPU:0, one launch (start us, length us, event | category | flops | bytes accessed | tf_op | source)
XLA Modules:
  0.0 135.8 jit_solution(17529488746773717417)
XLA Ops:
  2.1 2.4 %collective-permute-start = (bf16[2,1024]{1,0:T(2,128)(2,1)S(1)}, bf16[2,1024]{1,0:T(2,128)(2,1)S(1)}, u32[]{:S(2)}, u32[]{:S(2)}) collective-permute-start(bf16[2,1024]{1,0:T(2,128)(2,1)S(1)} %get-tuple-element.14), channel_id=1, source_target_pairs={{0,1},{1,2},{2,3},{3,4},{4,5},{5,6},{6,7},{7,8},{8,9},{9,10},{10,1... | collective-permute-start | bytes 12296 | tf_op jit(solution)/shard_map/ppermute | solution.py:23
  4.4 1.3 collective-permute-start.1
  7.7 2.0 %collective-permute-done.1 = bf16[2,1024]{1,0:T(2,128)(2,1)S(1)} collective-permute-done((bf16[2,1024]{1,0:T(2,128)(2,1)S(1)}, bf16[2,1024]{1,0:T(2,128)(2,1)S(1)}, u32[]{:S(2)}, u32[]{:S(2)}) %collective-permute-start.1) | collective-permute-done | bytes 4128 | tf_op jit(solution)/shard_map/ppermute | solution.py:24
  9.9 3.0 %collective-permute-start.2 = (bf16[16,4096]{1,0:T(8,128)(2,1)S(1)}, bf16[16,4096]{1,0:T(8,128)(2,1)S(1)}, u32[]{:S(2)}, u32[]{:S(2)}) collective-permute-start(bf16[16,4096]{1,0:T(8,128)(2,1)S(1)} %reshape.93), channel_id=1, source_target_pairs={{0,2},{2,0},{4,6},{6,4},{8,10},{10,8},{12,14},{14,12},{1,3},{3,1},... | collective-permute-start | bytes 393224 | tf_op jit(solution)/shard_map/ppermute | solution.py:31
  12.9 2.6 %collective-permute-start.5 = (bf16[16,4096]{1,0:T(8,128)(2,1)S(1)}, bf16[16,4096]{1,0:T(8,128)(2,1)S(1)}, u32[]{:S(2)}, u32[]{:S(2)}) collective-permute-start(bf16[16,4096]{1,0:T(8,128)(2,1)S(1)} %reshape.93), channel_id=1, source_target_pairs={{0,8},{2,10},{4,12},{6,14},{8,0},{10,2},{12,4},{14,6},{1,9},{3,11}... | collective-permute-start | bytes 393224 | tf_op jit(solution)/shard_map/ppermute | solution.py:31
  15.5 1.6 %collective-permute-start.3 = (bf16[16,4096]{1,0:T(8,128)(2,1)S(1)}, bf16[16,4096]{1,0:T(8,128)(2,1)S(1)}, u32[]{:S(2)}, u32[]{:S(2)}) collective-permute-start(bf16[16,4096]{1,0:T(8,128)(2,1)S(1)} %reshape.93), channel_id=1, source_target_pairs={{0,4},{2,6},{4,0},{6,2},{8,12},{10,14},{12,8},{14,10},{1,5},{3,7},... | collective-permute-start | bytes 393224 | tf_op jit(solution)/shard_map/ppermute | solution.py:31
  17.2 1.3 collective-permute-start.4
  18.5 1.3 collective-permute-start.7
  19.8 2.7 %collective-permute-done.5 = bf16[16,4096]{1,0:T(8,128)(2,1)S(1)} collective-permute-done((bf16[16,4096]{1,0:T(8,128)(2,1)S(1)}, bf16[16,4096]{1,0:T(8,128)(2,1)S(1)}, u32[]{:S(2)}, u32[]{:S(2)}) %collective-permute-start.5) | collective-permute-done | bytes 131104 | tf_op jit(solution)/shard_map/ppermute | solution.py:31
  22.6 1.6 %collective-permute-start.6 = (bf16[16,4096]{1,0:T(8,128)(2,1)S(1)}, bf16[16,4096]{1,0:T(8,128)(2,1)S(1)}, u32[]{:S(2)}, u32[]{:S(2)}) collective-permute-start(bf16[16,4096]{1,0:T(8,128)(2,1)S(1)} %collective-permute-done.5), channel_id=1, source_target_pairs={{0,2},{2,0},{4,6},{6,4},{8,10},{10,8},{12,14},{14,12},{1,3},{3,1},... | collective-permute-start | bytes 393224 | tf_op jit(solution)/shard_map/ppermute | solution.py:31
  24.2 2.5 %collective-permute-done.4 = bf16[16,4096]{1,0:T(8,128)(2,1)S(1)} collective-permute-done((bf16[16,4096]{1,0:T(8,128)(2,1)S(1)}, bf16[16,4096]{1,0:T(8,128)(2,1)S(1)}, u32[]{:S(2)}, u32[]{:S(2)}) %collective-permute-start.4) | collective-permute-done | bytes 131104 | tf_op jit(solution)/shard_map/ppermute | solution.py:31
  26.7 2.5 %collective-permute-done.7 = bf16[16,4096]{1,0:T(8,128)(2,1)S(1)} collective-permute-done((bf16[16,4096]{1,0:T(8,128)(2,1)S(1)}, bf16[16,4096]{1,0:T(8,128)(2,1)S(1)}, u32[]{:S(2)}, u32[]{:S(2)}) %collective-permute-start.7) | collective-permute-done | bytes 131104 | tf_op jit(solution)/shard_map/ppermute | solution.py:31
  29.2 1.5 %collective-permute-start.8 = (bf16[16,4096]{1,0:T(8,128)(2,1)S(1)}, bf16[16,4096]{1,0:T(8,128)(2,1)S(1)}, u32[]{:S(2)}, u32[]{:S(2)}) collective-permute-start(bf16[16,4096]{1,0:T(8,128)(2,1)S(1)} %collective-permute-done.7), channel_id=1, source_target_pairs={{0,2},{2,0},{4,6},{6,4},{8,10},{10,8},{12,14},{14,12},{1,3},{3,1},... | collective-permute-start | bytes 393224 | tf_op jit(solution)/shard_map/ppermute | solution.py:31
  30.7 4.2 %collective-permute-done.8 = bf16[16,4096]{1,0:T(8,128)(2,1)S(1)} collective-permute-done((bf16[16,4096]{1,0:T(8,128)(2,1)S(1)}, bf16[16,4096]{1,0:T(8,128)(2,1)S(1)}, u32[]{:S(2)}, u32[]{:S(2)}) %collective-permute-start.8) | collective-permute-done | bytes 131104 | tf_op jit(solution)/shard_map/ppermute | solution.py:31
  35.0 3.0 %convolution_convert_fusion.6 = bf16[128,512]{1,0:T(8,128)(2,1)S(1)} fusion(bf16[128,4096]{1,0:T(8,128)(2,1)S(1)} %constant_dynamic-update-slice_fusion, bf16[4096,512]{1,0:T(8,128)(2,1)} %param.11), kind=kOutput, calls=%fused_computation.34 | convolution fusion | flops 536936448 | bytes 5373952 | tf_op jit(solution)/shard_map/dot_general | solution.py:121
  39.1 2.5 %collective-permute-start.13 = (bf16[128,512]{1,0:T(8,128)(2,1)S(1)}, bf16[128,512]{1,0:T(8,128)(2,1)S(1)}, u32[]{:S(2)}, u32[]{:S(2)}) collective-permute-start(bf16[128,512]{1,0:T(8,128)(2,1)S(1)} %bitcast.137), channel_id=1, source_target_pairs={{0,12},{2,14},{4,8},{6,10},{8,4},{10,6},{12,0},{14,2},{1,13},{3,15... | collective-permute-start | bytes 393224 | tf_op jit(solution)/shard_map/ppermute | solution.py:31
  41.6 2.5 %collective-permute-start.11 = (bf16[128,512]{1,0:T(8,128)(2,1)S(1)}, bf16[128,512]{1,0:T(8,128)(2,1)S(1)}, u32[]{:S(2)}, u32[]{:S(2)}) collective-permute-start(bf16[128,512]{1,0:T(8,128)(2,1)S(1)} %bitcast.139), channel_id=1, source_target_pairs={{0,6},{2,4},{4,2},{6,0},{8,14},{10,12},{12,10},{14,8},{1,7},{3,5},... | collective-permute-start | bytes 393224 | tf_op jit(solution)/shard_map/ppermute | solution.py:31
  44.2 1.3 fusion.33
  45.5 1.3 fusion.46
  46.8 1.3 fusion.59
  49.1 1.3 fusion.25
  50.4 1.3 fusion.38
  51.6 1.2 collective-permute-start.14
  52.8 1.3 fusion.27
  54.1 1.3 fusion.40
  55.4 1.3 fusion.29
  56.7 1.3 fusion.42
  58.0 1.3 fusion.51
  59.2 1.3 fusion.53
  60.5 1.3 fusion.55
  62.2 1.3 convolution_add_fusion.2
  63.5 1.3 convolution_add_fusion.5
  64.7 1.3 convolution_add_fusion.8
  66.0 1.3 fusion.11
  67.3 1.3 fusion.14
  68.7 1.3 fusion.17
  70.5 1.3 fusion.22
  71.7 1.3 fusion.20
  73.1 1.3 fusion.48
  74.4 1.3 fusion.18
  76.2 1.3 fusion.35
  77.5 1.3 fusion.21
  80.7 1.3 convolution_convert_fusion.4
  82.0 1.3 convolution_convert_fusion.3
  83.3 1.3 convolution_convert_fusion.2
  84.6 1.3 convolution_convert_fusion.1
  88.0 2.2 %collective-permute-start.22 = (bf16[128,512]{1,0:T(8,128)(2,1)S(1)}, bf16[128,512]{1,0:T(8,128)(2,1)S(1)}, u32[]{:S(2)}, u32[]{:S(2)}) collective-permute-start(bf16[128,512]{1,0:T(8,128)(2,1)S(1)} %convolution_convert_fusion.2), channel_id=1, source_target_pairs={{0,6},{2,4},{4,2},{6,0},{8,14},{10,12},{12,10},{14,8},{1,7},{3,5},... | collective-permute-start | bytes 393224 | tf_op jit(solution)/shard_map/ppermute | solution.py:31
  90.4 1.3 convolution_convert_fusion
  91.7 1.2 collective-permute-start.24
  92.9 2.3 %collective-permute-done.18 = bf16[128,512]{1,0:T(8,128)(2,1)S(1)} collective-permute-done((bf16[128,512]{1,0:T(8,128)(2,1)S(1)}, bf16[128,512]{1,0:T(8,128)(2,1)S(1)}, u32[]{:S(2)}, u32[]{:S(2)}) %collective-permute-start.18) | collective-permute-done | bytes 131104 | tf_op jit(solution)/shard_map/ppermute | solution.py:31
  95.1 1.3 add_convert_fusion.4
  96.4 2.4 %collective-permute-start.19 = (bf16[128,512]{1,0:T(8,128)(2,1)S(1)}, bf16[128,512]{1,0:T(8,128)(2,1)S(1)}, u32[]{:S(2)}, u32[]{:S(2)}) collective-permute-start(bf16[128,512]{1,0:T(8,128)(2,1)S(1)} %add_convert_fusion.4), channel_id=1, source_target_pairs={{0,12},{2,14},{4,8},{6,10},{8,4},{10,6},{12,0},{14,2},{1,13},{3,15... | collective-permute-start | bytes 393224 | tf_op jit(solution)/shard_map/ppermute | solution.py:31
  98.9 1.3 add_convert_fusion.3
  100.2 2.1 %collective-permute-start.21 = (bf16[128,512]{1,0:T(8,128)(2,1)S(1)}, bf16[128,512]{1,0:T(8,128)(2,1)S(1)}, u32[]{:S(2)}, u32[]{:S(2)}) collective-permute-start(bf16[128,512]{1,0:T(8,128)(2,1)S(1)} %add_convert_fusion.3), channel_id=1, source_target_pairs={{0,8},{2,10},{4,12},{6,14},{8,0},{10,2},{12,4},{14,6},{1,9},{3,11}... | collective-permute-start | bytes 393224 | tf_op jit(solution)/shard_map/ppermute | solution.py:31
  102.3 2.0 %collective-permute-done.19 = bf16[128,512]{1,0:T(8,128)(2,1)S(1)} collective-permute-done((bf16[128,512]{1,0:T(8,128)(2,1)S(1)}, bf16[128,512]{1,0:T(8,128)(2,1)S(1)}, u32[]{:S(2)}, u32[]{:S(2)}) %collective-permute-start.19) | collective-permute-done | bytes 131104 | tf_op jit(solution)/shard_map/ppermute | solution.py:31
  104.3 5.4 %collective-permute-done.21 = bf16[128,512]{1,0:T(8,128)(2,1)S(1)} collective-permute-done((bf16[128,512]{1,0:T(8,128)(2,1)S(1)}, bf16[128,512]{1,0:T(8,128)(2,1)S(1)}, u32[]{:S(2)}, u32[]{:S(2)}) %collective-permute-start.21) | collective-permute-done | bytes 131104 | tf_op jit(solution)/shard_map/ppermute | solution.py:31
  109.6 3.3 %fusion.121 = f32[128,4096]{1,0:T(8,128)S(1)} fusion(bf16[512,4096]{1,0:T(8,128)(2,1)} %param.15, bf16[128,512]{1,0:T(8,128)(2,1)S(1)} %collective-permute-done.24, bf16[128,512]{1,0:T(8,128)(2,1)S(1)} %collective-permute-done.23, bf16[128,512]{1,0:T(8,128)(2,1)S(1)} %collective-permute-done.22, bf16[128,512]{1,0:T(8,128)(2,1)S(1)} %collective-permute-done.21, ...), kind=kOutput, calls=%fused_computation.179 | convolution fusion | flops 604831744 | bytes 7733252 | tf_op jit(solution)/shard_map/dot_general | solution.py:152
  115.2 2.3 %collective-permute-start.30 = (bf16[16,4096]{1,0:T(8,128)(2,1)S(1)}, bf16[16,4096]{1,0:T(8,128)(2,1)S(1)}, u32[]{:S(2)}, u32[]{:S(2)}) collective-permute-start(bf16[16,4096]{1,0:T(8,128)(2,1)S(1)} %get-tuple-element.11), channel_id=1, source_target_pairs={{0,4},{2,6},{4,0},{6,2},{8,12},{10,14},{12,8},{14,10},{1,5},{3,7},... | collective-permute-start | bytes 393224 | tf_op jit(solution)/shard_map/ppermute | solution.py:31
  117.5 1.2 collective-permute-start.31
  118.7 3.7 %collective-permute-done.25 = bf16[16,4096]{1,0:T(8,128)(2,1)S(1)} collective-permute-done((bf16[16,4096]{1,0:T(8,128)(2,1)S(1)}, bf16[16,4096]{1,0:T(8,128)(2,1)S(1)}, u32[]{:S(2)}, u32[]{:S(2)}) %collective-permute-start.25) | collective-permute-done | bytes 131104 | tf_op jit(solution)/shard_map/ppermute | solution.py:31
  122.4 2.0 %collective-permute-done.27 = bf16[16,4096]{1,0:T(8,128)(2,1)S(1)} collective-permute-done((bf16[16,4096]{1,0:T(8,128)(2,1)S(1)}, bf16[16,4096]{1,0:T(8,128)(2,1)S(1)}, u32[]{:S(2)}, u32[]{:S(2)}) %collective-permute-start.27) | collective-permute-done | bytes 131104 | tf_op jit(solution)/shard_map/ppermute | solution.py:31
  125.1 1.5 %collective-permute-start.26 = (bf16[16,4096]{1,0:T(8,128)(2,1)}, bf16[16,4096]{1,0:T(8,128)(2,1)S(1)}, u32[]{:S(2)}, u32[]{:S(2)}) collective-permute-start(bf16[16,4096]{1,0:T(8,128)(2,1)} %get-tuple-element.7), channel_id=1, source_target_pairs={{0,12},{2,14},{4,8},{6,10},{8,4},{10,6},{12,0},{14,2},{1,13},{3,15... | collective-permute-start | bytes 393224 | tf_op jit(solution)/shard_map/ppermute | solution.py:31
  126.7 5.5 %collective-permute-done.26 = bf16[16,4096]{1,0:T(8,128)(2,1)S(1)} collective-permute-done((bf16[16,4096]{1,0:T(8,128)(2,1)}, bf16[16,4096]{1,0:T(8,128)(2,1)S(1)}, u32[]{:S(2)}, u32[]{:S(2)}) %collective-permute-start.26) | collective-permute-done | bytes 131104 | tf_op jit(solution)/shard_map/ppermute | solution.py:31
  132.2 2.7 %collective-permute-done.28 = bf16[16,4096]{1,0:T(8,128)(2,1)S(1)} collective-permute-done((bf16[16,4096]{1,0:T(8,128)(2,1)S(1)}, bf16[16,4096]{1,0:T(8,128)(2,1)S(1)}, u32[]{:S(2)}, u32[]{:S(2)}) %collective-permute-start.28) | collective-permute-done | bytes 131104 | tf_op jit(solution)/shard_map/ppermute | solution.py:31
  (74 shorter events, 15.8 us)
Async XLA Ops:
  2.1 5.6 %collective-permute-start = (bf16[2,1024]{1,0:T(2,128)(2,1)S(1)}, bf16[2,1024]{1,0:T(2,128)(2,1)S(1)}, u32[]{:S(2)}, u32[]{:S(2)}) collective-permute-start(bf16[2,1024]{1,0:T(2,128)(2,1)S(1)} %get-tuple-element.14), channel_id=1, source_target_pairs={{0,1},{1,2},{2,3},{3,4},{4,5},{5,6},{6,7},{7,8},{8,9},{9,10},{10,1... | collective-permute-start | bytes 12296 | tf_op jit(solution)/shard_map/ppermute | solution.py:23
  4.4 5.2 %collective-permute-start.1 = (bf16[2,1024]{1,0:T(2,128)(2,1)S(1)}, bf16[2,1024]{1,0:T(2,128)(2,1)S(1)}, u32[]{:S(2)}, u32[]{:S(2)}) collective-permute-start(bf16[2,1024]{1,0:T(2,128)(2,1)S(1)} %get-tuple-element.15), channel_id=1, source_target_pairs={{1,0},{2,1},{3,2},{4,3},{5,4},{6,5},{7,6},{8,7},{9,8},{10,9},{11,1... | collective-permute-start | bytes 12296 | tf_op jit(solution)/shard_map/ppermute | solution.py:24
  9.9 14.2 %collective-permute-start.2 = (bf16[16,4096]{1,0:T(8,128)(2,1)S(1)}, bf16[16,4096]{1,0:T(8,128)(2,1)S(1)}, u32[]{:S(2)}, u32[]{:S(2)}) collective-permute-start(bf16[16,4096]{1,0:T(8,128)(2,1)S(1)} %reshape.93), channel_id=1, source_target_pairs={{0,2},{2,0},{4,6},{6,4},{8,10},{10,8},{12,14},{14,12},{1,3},{3,1},... | collective-permute-start | bytes 393224 | tf_op jit(solution)/shard_map/ppermute | solution.py:31
  12.9 9.6 %collective-permute-start.5 = (bf16[16,4096]{1,0:T(8,128)(2,1)S(1)}, bf16[16,4096]{1,0:T(8,128)(2,1)S(1)}, u32[]{:S(2)}, u32[]{:S(2)}) collective-permute-start(bf16[16,4096]{1,0:T(8,128)(2,1)S(1)} %reshape.93), channel_id=1, source_target_pairs={{0,8},{2,10},{4,12},{6,14},{8,0},{10,2},{12,4},{14,6},{1,9},{3,11}... | collective-permute-start | bytes 393224 | tf_op jit(solution)/shard_map/ppermute | solution.py:31
  15.5 8.6 %collective-permute-start.3 = (bf16[16,4096]{1,0:T(8,128)(2,1)S(1)}, bf16[16,4096]{1,0:T(8,128)(2,1)S(1)}, u32[]{:S(2)}, u32[]{:S(2)}) collective-permute-start(bf16[16,4096]{1,0:T(8,128)(2,1)S(1)} %reshape.93), channel_id=1, source_target_pairs={{0,4},{2,6},{4,0},{6,2},{8,12},{10,14},{12,8},{14,10},{1,5},{3,7},... | collective-permute-start | bytes 393224 | tf_op jit(solution)/shard_map/ppermute | solution.py:31
  17.2 9.5 %collective-permute-start.4 = (bf16[16,4096]{1,0:T(8,128)(2,1)S(1)}, bf16[16,4096]{1,0:T(8,128)(2,1)S(1)}, u32[]{:S(2)}, u32[]{:S(2)}) collective-permute-start(bf16[16,4096]{1,0:T(8,128)(2,1)S(1)} %reshape.93), channel_id=1, source_target_pairs={{0,6},{2,4},{4,2},{6,0},{8,14},{10,12},{12,10},{14,8},{1,7},{3,5},... | collective-permute-start | bytes 393224 | tf_op jit(solution)/shard_map/ppermute | solution.py:31
  18.5 10.7 %collective-permute-start.7 = (bf16[16,4096]{1,0:T(8,128)(2,1)S(1)}, bf16[16,4096]{1,0:T(8,128)(2,1)S(1)}, u32[]{:S(2)}, u32[]{:S(2)}) collective-permute-start(bf16[16,4096]{1,0:T(8,128)(2,1)S(1)} %reshape.93), channel_id=1, source_target_pairs={{0,12},{2,14},{4,8},{6,10},{8,4},{10,6},{12,0},{14,2},{1,13},{3,15... | collective-permute-start | bytes 393224 | tf_op jit(solution)/shard_map/ppermute | solution.py:31
  22.6 8.1 %collective-permute-start.6 = (bf16[16,4096]{1,0:T(8,128)(2,1)S(1)}, bf16[16,4096]{1,0:T(8,128)(2,1)S(1)}, u32[]{:S(2)}, u32[]{:S(2)}) collective-permute-start(bf16[16,4096]{1,0:T(8,128)(2,1)S(1)} %collective-permute-done.5), channel_id=1, source_target_pairs={{0,2},{2,0},{4,6},{6,4},{8,10},{10,8},{12,14},{14,12},{1,3},{3,1},... | collective-permute-start | bytes 393224 | tf_op jit(solution)/shard_map/ppermute | solution.py:31
  29.2 5.8 %collective-permute-start.8 = (bf16[16,4096]{1,0:T(8,128)(2,1)S(1)}, bf16[16,4096]{1,0:T(8,128)(2,1)S(1)}, u32[]{:S(2)}, u32[]{:S(2)}) collective-permute-start(bf16[16,4096]{1,0:T(8,128)(2,1)S(1)} %collective-permute-done.7), channel_id=1, source_target_pairs={{0,2},{2,0},{4,6},{6,4},{8,10},{10,8},{12,14},{14,12},{1,3},{3,1},... | collective-permute-start | bytes 393224 | tf_op jit(solution)/shard_map/ppermute | solution.py:31
  38.1 24.0 %collective-permute-start.9 = (bf16[128,512]{1,0:T(8,128)(2,1)S(1)}, bf16[128,512]{1,0:T(8,128)(2,1)S(1)}, u32[]{:S(2)}, u32[]{:S(2)}) collective-permute-start(bf16[128,512]{1,0:T(8,128)(2,1)S(1)} %bitcast.136), channel_id=1, source_target_pairs={{0,2},{2,0},{4,6},{6,4},{8,10},{10,8},{12,14},{14,12},{1,3},{3,1},... | collective-permute-start | bytes 393224 | tf_op jit(solution)/shard_map/ppermute | solution.py:31
  39.1 9.1 %collective-permute-start.13 = (bf16[128,512]{1,0:T(8,128)(2,1)S(1)}, bf16[128,512]{1,0:T(8,128)(2,1)S(1)}, u32[]{:S(2)}, u32[]{:S(2)}) collective-permute-start(bf16[128,512]{1,0:T(8,128)(2,1)S(1)} %bitcast.137), channel_id=1, source_target_pairs={{0,12},{2,14},{4,8},{6,10},{8,4},{10,6},{12,0},{14,2},{1,13},{3,15... | collective-permute-start | bytes 393224 | tf_op jit(solution)/shard_map/ppermute | solution.py:31
  41.6 10.1 %collective-permute-start.12 = (bf16[128,512]{1,0:T(8,128)(2,1)S(1)}, bf16[128,512]{1,0:T(8,128)(2,1)S(1)}, u32[]{:S(2)}, u32[]{:S(2)}) collective-permute-start(bf16[128,512]{1,0:T(8,128)(2,1)S(1)} %bitcast.138), channel_id=1, source_target_pairs={{0,8},{2,10},{4,12},{6,14},{8,0},{10,2},{12,4},{14,6},{1,9},{3,11}... | collective-permute-start | bytes 393224 | tf_op jit(solution)/shard_map/ppermute | solution.py:31
  41.6 13.8 %collective-permute-start.11 = (bf16[128,512]{1,0:T(8,128)(2,1)S(1)}, bf16[128,512]{1,0:T(8,128)(2,1)S(1)}, u32[]{:S(2)}, u32[]{:S(2)}) collective-permute-start(bf16[128,512]{1,0:T(8,128)(2,1)S(1)} %bitcast.139), channel_id=1, source_target_pairs={{0,6},{2,4},{4,2},{6,0},{8,14},{10,12},{12,10},{14,8},{1,7},{3,5},... | collective-permute-start | bytes 393224 | tf_op jit(solution)/shard_map/ppermute | solution.py:31
  44.0 18.0 %collective-permute-start.10 = (bf16[128,512]{1,0:T(8,128)(2,1)S(1)}, bf16[128,512]{1,0:T(8,128)(2,1)S(1)}, u32[]{:S(2)}, u32[]{:S(2)}) collective-permute-start(bf16[128,512]{1,0:T(8,128)(2,1)S(1)} %bitcast.140), channel_id=1, source_target_pairs={{0,4},{2,6},{4,0},{6,2},{8,12},{10,14},{12,8},{14,10},{1,5},{3,7},... | collective-permute-start | bytes 393224 | tf_op jit(solution)/shard_map/ppermute | solution.py:31
  48.1 22.2 %collective-permute-start.15 = (bf16[128,512]{1,0:T(8,128)(2,1)S(1)}, bf16[128,512]{1,0:T(8,128)(2,1)S(1)}, u32[]{:S(2)}, u32[]{:S(2)}) collective-permute-start(bf16[128,512]{1,0:T(8,128)(2,1)S(1)} %collective-permute-done.13), channel_id=1, source_target_pairs={{0,2},{2,0},{4,6},{6,4},{8,10},{10,8},{12,14},{14,12},{1,3},{3,1},... | collective-permute-start | bytes 393224 | tf_op jit(solution)/shard_map/ppermute | solution.py:31
  51.6 18.6 %collective-permute-start.14 = (bf16[128,512]{1,0:T(8,128)(2,1)S(1)}, bf16[128,512]{1,0:T(8,128)(2,1)S(1)}, u32[]{:S(2)}, u32[]{:S(2)}) collective-permute-start(bf16[128,512]{1,0:T(8,128)(2,1)S(1)} %collective-permute-done.12), channel_id=1, source_target_pairs={{0,2},{2,0},{4,6},{6,4},{8,10},{10,8},{12,14},{14,12},{1,3},{3,1},... | collective-permute-start | bytes 393224 | tf_op jit(solution)/shard_map/ppermute | solution.py:31
  73.0 6.0 %collective-permute-start.17 = (bf16[128,512]{1,0:T(8,128)(2,1)S(1)}, bf16[128,512]{1,0:T(8,128)(2,1)S(1)}, u32[]{:S(2)}, u32[]{:S(2)}) collective-permute-start(bf16[128,512]{1,0:T(8,128)(2,1)S(1)} %fusion.20), channel_id=1, source_target_pairs={{0,1},{1,0},{2,3},{3,2},{4,5},{5,4},{6,7},{7,6},{8,9},{9,8},{10,11... | collective-permute-start | bytes 393224 | tf_op jit(solution)/shard_map/ppermute | solution.py:31
  75.7 59.4 %copy-start = (bf16[64,1024]{1,0:T(8,128)(2,1)S(1)}, bf16[64,1024]{1,0:T(8,128)(2,1)}, u32[]{:S(2)}) copy-start(bf16[64,1024]{1,0:T(8,128)(2,1)} %param.8) | copy-start | bytes 393220
  75.7 3.1 %collective-permute-start.16 = (bf16[128,512]{1,0:T(8,128)(2,1)S(1)}, bf16[128,512]{1,0:T(8,128)(2,1)S(1)}, u32[]{:S(2)}, u32[]{:S(2)}) collective-permute-start(bf16[128,512]{1,0:T(8,128)(2,1)S(1)} %fusion.18), channel_id=1, source_target_pairs={{0,1},{1,0},{2,3},{3,2},{4,5},{5,4},{6,7},{7,6},{8,9},{9,8},{10,11... | collective-permute-start | bytes 393224 | tf_op jit(solution)/shard_map/ppermute | solution.py:31
  85.9 9.2 %collective-permute-start.18 = (bf16[128,512]{1,0:T(8,128)(2,1)S(1)}, bf16[128,512]{1,0:T(8,128)(2,1)S(1)}, u32[]{:S(2)}, u32[]{:S(2)}) collective-permute-start(bf16[128,512]{1,0:T(8,128)(2,1)S(1)} %convolution_convert_fusion.4), channel_id=1, source_target_pairs={{0,2},{2,0},{4,6},{6,4},{8,10},{10,8},{12,14},{14,12},{1,3},{3,1},... | collective-permute-start | bytes 393224 | tf_op jit(solution)/shard_map/ppermute | solution.py:31
  86.9 12.0 %collective-permute-start.20 = (bf16[128,512]{1,0:T(8,128)(2,1)S(1)}, bf16[128,512]{1,0:T(8,128)(2,1)S(1)}, u32[]{:S(2)}, u32[]{:S(2)}) collective-permute-start(bf16[128,512]{1,0:T(8,128)(2,1)S(1)} %convolution_convert_fusion.3), channel_id=1, source_target_pairs={{0,2},{2,0},{4,6},{6,4},{8,10},{10,8},{12,14},{14,12},{1,3},{3,1},... | collective-permute-start | bytes 393224 | tf_op jit(solution)/shard_map/ppermute | solution.py:31
  88.0 14.2 %collective-permute-start.22 = (bf16[128,512]{1,0:T(8,128)(2,1)S(1)}, bf16[128,512]{1,0:T(8,128)(2,1)S(1)}, u32[]{:S(2)}, u32[]{:S(2)}) collective-permute-start(bf16[128,512]{1,0:T(8,128)(2,1)S(1)} %convolution_convert_fusion.2), channel_id=1, source_target_pairs={{0,6},{2,4},{4,2},{6,0},{8,14},{10,12},{12,10},{14,8},{1,7},{3,5},... | collective-permute-start | bytes 393224 | tf_op jit(solution)/shard_map/ppermute | solution.py:31
  90.2 12.0 %collective-permute-start.23 = (bf16[128,512]{1,0:T(8,128)(2,1)S(1)}, bf16[128,512]{1,0:T(8,128)(2,1)S(1)}, u32[]{:S(2)}, u32[]{:S(2)}) collective-permute-start(bf16[128,512]{1,0:T(8,128)(2,1)S(1)} %convolution_convert_fusion.1), channel_id=1, source_target_pairs={{0,4},{2,6},{4,0},{6,2},{8,12},{10,14},{12,8},{14,10},{1,5},{3,7},... | collective-permute-start | bytes 393224 | tf_op jit(solution)/shard_map/ppermute | solution.py:31
  91.7 10.6 %collective-permute-start.24 = (bf16[128,512]{1,0:T(8,128)(2,1)S(1)}, bf16[128,512]{1,0:T(8,128)(2,1)S(1)}, u32[]{:S(2)}, u32[]{:S(2)}) collective-permute-start(bf16[128,512]{1,0:T(8,128)(2,1)S(1)} %convolution_convert_fusion), channel_id=1, source_target_pairs={{0,2},{2,0},{4,6},{6,4},{8,10},{10,8},{12,14},{14,12},{1,3},{3,1},... | collective-permute-start | bytes 393224 | tf_op jit(solution)/shard_map/ppermute | solution.py:31
  96.4 7.8 %collective-permute-start.19 = (bf16[128,512]{1,0:T(8,128)(2,1)S(1)}, bf16[128,512]{1,0:T(8,128)(2,1)S(1)}, u32[]{:S(2)}, u32[]{:S(2)}) collective-permute-start(bf16[128,512]{1,0:T(8,128)(2,1)S(1)} %add_convert_fusion.4), channel_id=1, source_target_pairs={{0,12},{2,14},{4,8},{6,10},{8,4},{10,6},{12,0},{14,2},{1,13},{3,15... | collective-permute-start | bytes 393224 | tf_op jit(solution)/shard_map/ppermute | solution.py:31
  100.2 9.5 %collective-permute-start.21 = (bf16[128,512]{1,0:T(8,128)(2,1)S(1)}, bf16[128,512]{1,0:T(8,128)(2,1)S(1)}, u32[]{:S(2)}, u32[]{:S(2)}) collective-permute-start(bf16[128,512]{1,0:T(8,128)(2,1)S(1)} %add_convert_fusion.3), channel_id=1, source_target_pairs={{0,8},{2,10},{4,12},{6,14},{8,0},{10,2},{12,4},{14,6},{1,9},{3,11}... | collective-permute-start | bytes 393224 | tf_op jit(solution)/shard_map/ppermute | solution.py:31
  113.1 9.3 %collective-permute-start.25 = (bf16[16,4096]{1,0:T(8,128)(2,1)S(1)}, bf16[16,4096]{1,0:T(8,128)(2,1)S(1)}, u32[]{:S(2)}, u32[]{:S(2)}) collective-permute-start(bf16[16,4096]{1,0:T(8,128)(2,1)S(1)} %get-tuple-element.9), channel_id=1, source_target_pairs={{0,2},{2,0},{4,6},{6,4},{8,10},{10,8},{12,14},{14,12},{1,3},{3,1},... | collective-permute-start | bytes 393224 | tf_op jit(solution)/shard_map/ppermute | solution.py:31
  114.0 10.4 %collective-permute-start.27 = (bf16[16,4096]{1,0:T(8,128)(2,1)S(1)}, bf16[16,4096]{1,0:T(8,128)(2,1)S(1)}, u32[]{:S(2)}, u32[]{:S(2)}) collective-permute-start(bf16[16,4096]{1,0:T(8,128)(2,1)S(1)} %get-tuple-element.13), channel_id=1, source_target_pairs={{0,2},{2,0},{4,6},{6,4},{8,10},{10,8},{12,14},{14,12},{1,3},{3,1},... | collective-permute-start | bytes 393224 | tf_op jit(solution)/shard_map/ppermute | solution.py:31
  115.2 11.5 %collective-permute-start.29 = (bf16[16,4096]{1,0:T(8,128)(2,1)S(1)}, bf16[16,4096]{1,0:T(8,128)(2,1)S(1)}, u32[]{:S(2)}, u32[]{:S(2)}) collective-permute-start(bf16[16,4096]{1,0:T(8,128)(2,1)S(1)} %get-tuple-element.12), channel_id=1, source_target_pairs={{0,6},{2,4},{4,2},{6,0},{8,14},{10,12},{12,10},{14,8},{1,7},{3,5},... | collective-permute-start | bytes 393224 | tf_op jit(solution)/shard_map/ppermute | solution.py:31
  115.2 11.5 %collective-permute-start.30 = (bf16[16,4096]{1,0:T(8,128)(2,1)S(1)}, bf16[16,4096]{1,0:T(8,128)(2,1)S(1)}, u32[]{:S(2)}, u32[]{:S(2)}) collective-permute-start(bf16[16,4096]{1,0:T(8,128)(2,1)S(1)} %get-tuple-element.11), channel_id=1, source_target_pairs={{0,4},{2,6},{4,0},{6,2},{8,12},{10,14},{12,8},{14,10},{1,5},{3,7},... | collective-permute-start | bytes 393224 | tf_op jit(solution)/shard_map/ppermute | solution.py:31
  117.5 9.2 %collective-permute-start.31 = (bf16[16,4096]{1,0:T(8,128)(2,1)S(1)}, bf16[16,4096]{1,0:T(8,128)(2,1)S(1)}, u32[]{:S(2)}, u32[]{:S(2)}) collective-permute-start(bf16[16,4096]{1,0:T(8,128)(2,1)S(1)} %get-tuple-element.10), channel_id=1, source_target_pairs={{0,2},{2,0},{4,6},{6,4},{8,10},{10,8},{12,14},{14,12},{1,3},{3,1},... | collective-permute-start | bytes 393224 | tf_op jit(solution)/shard_map/ppermute | solution.py:31
  125.1 7.1 %collective-permute-start.26 = (bf16[16,4096]{1,0:T(8,128)(2,1)}, bf16[16,4096]{1,0:T(8,128)(2,1)S(1)}, u32[]{:S(2)}, u32[]{:S(2)}) collective-permute-start(bf16[16,4096]{1,0:T(8,128)(2,1)} %get-tuple-element.7), channel_id=1, source_target_pairs={{0,12},{2,14},{4,8},{6,10},{8,4},{10,6},{12,0},{14,2},{1,13},{3,15... | collective-permute-start | bytes 393224 | tf_op jit(solution)/shard_map/ppermute | solution.py:31
  126.7 8.2 %collective-permute-start.28 = (bf16[16,4096]{1,0:T(8,128)(2,1)S(1)}, bf16[16,4096]{1,0:T(8,128)(2,1)S(1)}, u32[]{:S(2)}, u32[]{:S(2)}) collective-permute-start(bf16[16,4096]{1,0:T(8,128)(2,1)S(1)} %get-tuple-element.8), channel_id=1, source_target_pairs={{0,8},{2,10},{4,12},{6,14},{8,0},{10,2},{12,4},{14,6},{1,9},{3,11}... | collective-permute-start | bytes 393224 | tf_op jit(solution)/shard_map/ppermute | solution.py:31

commit v2 on v0

v2 whole, which is shorter than its diff:
```python
import functools
import math

import jax
import jax.numpy as jnp
from jax import lax
from jax.experimental import pallas as pl
from jax.experimental.pallas import tpu as pltpu
from jax.sharding import PartitionSpec as P

DF = 1024
HD = 128
KW = 5
VMEM = pltpu.VMEM


epsilon = 1e-06


def flip(value, axis, mask):
    pairs = [(source, source ^ mask) for source in range(lax.axis_size(axis))]
    return lax.ppermute(value, axis, pairs)


def relayed(mask, size):
    return mask & 1 == 1 and mask >= max(size // 2, 2)


def far_first(size):
    return sorted(range(1, size), reverse=True)


def gather_flips(value, axis):
    size = lax.axis_size(axis)
    blocks = [value] + [None] * (size - 1)
    for mask in far_first(size):
        if not relayed(mask, size):
            blocks[mask] = flip(value, axis, mask)
    for mask in far_first(size):
        if relayed(mask, size):
            blocks[mask] = flip(blocks[mask ^ 1], axis, 1)
    return blocks


def scatter_flips(relay_chunks, direct_chunks, axis):
    size = lax.axis_size(axis)
    passed = {mask ^ 1: flip(chunk, axis, 1) for mask, chunk in relay_chunks.items()}
    arrived = []
    for mask in far_first(size):
        if mask in direct_chunks:
            chunk = direct_chunks[mask]
            if mask in passed:
                chunk = (chunk + passed[mask].astype(jnp.float32)).astype(jnp.bfloat16)
            arrived.append(flip(chunk, axis, mask))
    return arrived


def call(body, outs, scratch, in_memory, *operands):
    specs = [
        pl.BlockSpec(memory_space=pl.ANY if where == "h" else VMEM) for where in in_memory
    ]
    return pl.pallas_call(
        body,
        out_shape=outs,
        in_specs=specs,
        out_specs=jax.tree.map(lambda _: pl.BlockSpec(memory_space=VMEM), outs),
        scratch_shapes=scratch,
        compiler_params=pltpu.CompilerParams(vmem_limit_bytes=48 * 2**20),
    )(*operands)


def sds(shape, dtype):
    return jax.ShapeDtypeStruct(shape, dtype)


def dot(left, right):
    return jnp.dot(left, right, preferred_element_type=jnp.float32)


def offset(mask, width):
    return pl.multiple_of((lax.axis_index("seq") ^ mask) * width, width)


def start_all(copies):
    for copy in copies:
        copy.start()
    return copies


def down_kernel(size, own_tokens, pieces, *refs):
    blocks, w_ref, out_ref, held, sems = refs[:size], *refs[size:]
    depth = w_ref.shape[0] // pieces
    copies = start_all(
        [
            pltpu.make_async_copy(w_ref.at[pl.ds(p * depth, depth)], held.at[p], sems.at[p])
            for p in range(pieces)
        ]
    )
    total = None
    for p in range(pieces):
        rows = jnp.concatenate([b[:, p * depth : (p + 1) * depth] for b in blocks], axis=0)
        copies[p].wait()
        product = dot(rows, held[p])
        total = product if total is None else total + product
    total = total.astype(jnp.bfloat16)
    for mask in range(size):
        out_ref[pl.ds(offset(mask, own_tokens), own_tokens), :] = total[
            mask * own_tokens : (mask + 1) * own_tokens
        ]


def qkv_steps(masks, blocks, gain_ref, w_ref, held, sems, totals, squares):
    columns = blocks[0].shape[1]
    copies = start_all(
        [
            pltpu.make_async_copy(
                w_ref.at[:, pl.ds(offset(mask, columns), columns), :], held.at[i], sems.at[i]
            )
            for i, mask in enumerate(masks)
        ]
    )
    for i, mask in enumerate(masks):
        block = blocks[i][...].astype(jnp.float32)
        part = jnp.sum(block * block, axis=1, keepdims=True)
        squares = part if squares is None else squares + part
        gained = (block * gain_ref[:, pl.ds(offset(mask, columns), columns)]).astype(jnp.bfloat16)
        copies[i].wait()
        products = [dot(gained, held[i, which]) for which in range(3)]
        totals = products if totals is None else [t + p for t, p in zip(totals, products)]
    return totals, squares


def qkv_early(masks, *refs):
    count = len(masks)
    blocks, (gain_ref, w_ref, totals_ref, squares_ref, held, sems) = refs[:count], refs[count:]
    totals, squares = qkv_steps(masks, blocks, gain_ref, w_ref, held, sems, None, None)
    for which in range(3):
        totals_ref[which] = totals[which]
    squares_ref[...] = jnp.broadcast_to(squares, squares_ref.shape)


def qkv_late(masks, features, *refs):
    count = len(masks)
    blocks = refs[:count]
    gain_ref, w_ref, totals_ref, squares_ref, q_ref, kv_ref, held, sems = refs[count:]
    totals, squares = qkv_steps(
        masks,
        blocks,
        gain_ref,
        w_ref,
        held,
        sems,
        [totals_ref[which] for which in range(3)],
        squares_ref[:, :1],
    )
    scale = lax.rsqrt(squares / features + epsilon)
    q_ref[...] = (totals[0] * scale).astype(jnp.bfloat16)
    kv_ref[0] = (totals[1] * scale).astype(jnp.bfloat16)
    kv_ref[1] = (totals[2] * scale).astype(jnp.bfloat16)


def out_copies(masks, columns, w_ref, held, sems):
    return start_all(
        [
            pltpu.make_async_copy(
                w_ref.at[:, pl.ds(offset(mask, columns), columns)], held.at[i], sems.at[i]
            )
            for i, mask in enumerate(masks)
        ]
    )


def attend_kernel(masks, q_ref, own_ref, other_ref, w_ref, *refs):
    attended_ref, chunk_refs, held, sems = refs[0], refs[1:-2], refs[-2], refs[-1]
    columns = q_ref.shape[1]
    copies = out_copies(masks, columns, w_ref, held, sems)
    contract = (((1,), (1,)), ((), ()))
    for head in range(columns // HD):
        here = slice(head * HD, (head + 1) * HD)
        query = q_ref[:, here]
        scores = [
            lax.dot_general(query, kv[0, :, here], contract, preferred_element_type=jnp.float32)
            * (1.0 / math.sqrt(HD))
            for kv in (own_ref, other_ref)
        ]
        peak = jnp.maximum(*[jnp.max(s, axis=1, keepdims=True) for s in scores])
        weights = [jnp.exp(s - peak) for s in scores]
        norm = sum(jnp.sum(w, axis=1, keepdims=True) for w in weights)
        attended_ref[:, here] = sum(
            dot((w / norm).astype(jnp.bfloat16), kv[1, :, here])
            for w, kv in zip(weights, (own_ref, other_ref))
        ).astype(jnp.bfloat16)
    for i, chunk_ref in enumerate(chunk_refs):
        copies[i].wait()
        chunk_ref[...] = dot(attended_ref[...], held[i]).astype(chunk_ref.dtype)


def out_kernel(masks, attended_ref, w_ref, *refs):
    chunk_refs, held, sems = refs[:-2], refs[-2], refs[-1]
    copies = out_copies(masks, attended_ref.shape[1], w_ref, held, sems)
    for i, chunk_ref in enumerate(chunk_refs):
        copies[i].wait()
        chunk_ref[...] = dot(attended_ref[...], held[i]).astype(chunk_ref.dtype)


def up_kernel(size, arrivals, pieces, coarse_ref, own_ref, *refs):
    arrived, w_ref = refs[:arrivals], refs[arrivals]
    chunk_refs, (held, sums, sems) = refs[arrivals + 1 : -3], refs[-3:]
    own_tokens, width = chunk_refs[0].shape[0], w_ref.shape[1] // pieces
    copies = start_all(
        [
            pltpu.make_async_copy(w_ref.at[:, pl.ds(p * width, width)], held.at[p], sems.at[p])
            for p in range(pieces)
        ]
    )
    mixed = own_ref[...]
    for value in arrived:
        mixed = mixed + value[...].astype(jnp.float32)
    mixed = (coarse_ref[...].astype(jnp.float32) + mixed).astype(jnp.bfloat16)
    for p in range(pieces):
        copies[p].wait()
        sums[...] = dot(mixed, held[p])
        for mask, chunk_ref in enumerate(chunk_refs):
            chunk_ref[:, p * width : (p + 1) * width] = sums[
                pl.ds(offset(mask, own_tokens), own_tokens), :
            ].astype(chunk_ref.dtype)


def edge_rows(frames, width):
    size, inner = lax.axis_size("seq"), lax.axis_size("sub")
    position = lax.axis_index("seq") * inner + lax.axis_index("sub")
    total = size * inner
    first, last = frames[:width], frames[-width:]
    even = (position & 1) == 0
    inside = [(i, i ^ 1) for i in range(total)]
    across = [(i, ((i + 1) ^ 1) - 1) for i in range(1, total - 1)]
    near = lax.ppermute(jnp.where(even, last, first), ("seq", "sub"), inside)
    far = lax.ppermute(jnp.where(even, first, last), ("seq", "sub"), across)
    return jnp.where(even, far, near), jnp.where(even, near, far)


def per_device(frames, fine_gain, dw_kernel, w_down, coarse_gain, w_qkv, w_out, w_up):
    frame_rows = frames.shape[0]
    columns = w_qkv.shape[2]
    size = lax.axis_size("seq")
    features = columns * size
    own_tokens = frame_rows // 4
    tokens = own_tokens * size
    bf16, f32 = jnp.bfloat16, jnp.float32
    direct = [m for m in range(1, size) if not relayed(m, size)]
    relay = [m for m in range(1, size) if relayed(m, size)]
    via = [m ^ 1 for m in relay]

    before, after = edge_rows(frames, KW // 2)
    frames_f32 = frames.astype(f32)

    def normed(rows):
        return (
            rows * lax.rsqrt(jnp.mean(rows * rows, axis=1, keepdims=True) + epsilon) * fine_gain
        ).astype(bf16)

    padded = jnp.concatenate(
        [normed(before.astype(f32)), normed(frames_f32), normed(after.astype(f32))], axis=0
    )
    convolved = jnp.zeros((frame_rows, DF), f32)
    for tap in range(KW):
        convolved = convolved + padded[tap : tap + frame_rows].astype(f32) * dw_kernel[tap].astype(
            f32
        )
    patches = convolved.astype(bf16).reshape(own_tokens, 4 * DF)

    pieces = 8
    coarse = call(
        functools.partial(down_kernel, size, own_tokens, pieces),
        sds((tokens, columns), bf16),
        [VMEM((pieces, 4 * DF // pieces, columns), bf16), pltpu.SemaphoreType.DMA((pieces,))],
        "v" * size + "h",
        *gather_flips(patches, "seq"),
        w_down,
    )

    blocks = gather_flips(coarse, "seq")
    gain_row = coarse_gain.reshape(1, features)
    early = [0] + direct

    def weight_scratch(masks):
        count = len(masks)
        return [VMEM((count, 3, columns, columns), bf16), pltpu.SemaphoreType.DMA((count,))]

    totals, squares = call(
        functools.partial(qkv_early, early),
        (sds((3, tokens, columns), f32), sds((tokens, 128), f32)),
        weight_scratch(early),
        "v" * len(early) + "vh",
        *[blocks[m] for m in early],
        gain_row,
        w_qkv,
    )
    queries, own_kv = call(
        functools.partial(qkv_late, relay, features),
        (sds((tokens, columns), bf16), sds((2, tokens, columns), bf16)),
        weight_scratch(relay),
        "v" * len(relay) + "vhvv",
        *[blocks[m] for m in relay],
        gain_row,
        w_qkv,
        totals,
        squares,
    )
    other_kv = flip(own_kv, "sub", 1)

    def out_scratch(masks):
        count = len(masks)
        return [VMEM((count, columns, columns), bf16), pltpu.SemaphoreType.DMA((count,))]

    attended, *relay_chunks = call(
        functools.partial(attend_kernel, relay),
        (sds((tokens, columns), bf16),) * (1 + len(relay)),
        out_scratch(relay),
        "vvvh",
        queries,
        own_kv,
        other_kv,
        w_out,
    )
    rest = via + [m for m in direct if m not in via] + [0]

    def kind(mask):
        return f32 if mask == 0 or mask in via else bf16

    chunks = call(
        functools.partial(out_kernel, rest),
        tuple(sds((tokens, columns), kind(m)) for m in rest),
        out_scratch(rest),
        "vh",
        attended,
        w_out,
    )
    chunks = dict(zip(rest, chunks))
    own_part = chunks.pop(0)
    arrived = scatter_flips(dict(zip(relay, relay_chunks)), chunks, "seq")

    def up_kind(mask):
        return bf16 if mask in relay else kind(mask)

    lifted = call(
        functools.partial(up_kernel, size, len(arrived), pieces),
        tuple(sds((own_tokens, 4 * DF), up_kind(m)) for m in range(size)),
        [
            VMEM((pieces, columns, 4 * DF // pieces), bf16),
            VMEM((tokens, 4 * DF // pieces), f32),
            pltpu.SemaphoreType.DMA((pieces,)),
        ],
        "vv" + "v" * len(arrived) + "h",
        coarse,
        own_part,
        *arrived,
        w_up,
    )
    arrived = scatter_flips(
        {m: lifted[m] for m in relay}, {m: lifted[m] for m in direct}, "seq"
    )
    total = lifted[0]
    for value in arrived:
        total = total + value.astype(f32)
    return (frames_f32 + total.reshape(frame_rows, DF)).astype(bf16)


def solution(mesh):
    placed = (
        P(("groups", "seq", "sub"), None),
        P(),
        P(),
        P(None, "seq"),
        P(),
        P(None, None, "seq"),
        P("seq", None),
        P("seq", None),
    )
    return jax.shard_map(
        per_device,
        mesh=mesh,
        in_specs=placed,
        out_specs=P(("groups", "seq", "sub"), None),
        check_vma=False,
    )
```

time: 263 us -> 105 us (0.40)
  waiting for transfers between devices: 215 us -> 39.6 us
  starting transfers between devices: 4.4 us -> 41 us
  matrix products: 23 us -> 0 us
  Pallas kernels: 0 us -> 15.4 us
  between operations: 13.3 us -> 0.25 us
    reduce_scatter x2 -> x0, waiting for transfers between devices: 130 us -> none  [the longest x1 67 us: per_device(): lax.psum_scatter(jnp.dot(mixed, w_up, preferred_element_type=jnp.float32)...]
    all_gather x2 -> x0, waiting for transfers between devices: 81.8 us -> none  [the longest x1 43.4 us: per_device(): lax.all_gather(patches, 'seq', axis=0, tiled=True)]
    ppermute x4 -> x31, starting transfers between devices: 4.27 us -> 41 us  [the longest x29 39.8 us: flip(): return lax.ppermute(value, axis, pairs)]
    ppermute x4 -> x31, waiting for transfers between devices: 2.97 us -> 39.6 us  [the longest x29 39.6 us: flip(): return lax.ppermute(value, axis, pairs)]
    dot_general x8 -> x0, matrix products: 22.6 us -> none  [the longest x1 4.33 us: per_device(): jnp.dot(mixed, w_up, preferred_element_type=jnp.float32)]
    pallas_call x0 -> x6, Pallas kernels: none -> 15.4 us  [call(): pl.pallas_call(body, out_shape=outs, in_specs=specs, out_specs=jax.tree.m...]
  transfers between devices with their start and end apart: 8 -> 31, of which waited for: 5 -> 15; matrix products, arithmetic and copies ran while one was open for 3% -> 3% of each run, Pallas kernels for 0% -> 6%
where the time goes in v2:
time: 105 us; the launch traced here: 104 us
  starting transfers between devices  41 us (39%)
  waiting for transfers between devices  39.6 us (38%)
  Pallas kernels  15.4 us (15%)
  other arithmetic  5.73 us (5%)
  local copies, waits for them, and re-layouts  2.37 us (2%)
    ppermute x29, starting transfers between devices, flip(): return lax.ppermute(value, axis, pairs)  39.8 us
    ppermute x29, waiting for transfers between devices, flip(): return lax.ppermute(value, axis, pairs)  39.6 us
    pallas_call x6, Pallas kernels, call(): pl.pallas_call(body, out_shape=outs, in_specs=specs, out_specs=jax.tree.m...  15.4 us
    unnamed x8, local copies, waits for them, and re-layouts  2.2 us
  transfers between devices with their start and end apart: 31, of which 15 were waited for; matrix products, arithmetic and copies ran while one was open for 3% of the time, Pallas kernels for 6%

profile of v2, /device:TPU:0, one launch (start us, length us, event | category | flops | bytes accessed | tf_op | source)
XLA Modules:
  0.0 104.4 jit_solution(10018387160075146118)
XLA Ops:
  0.0 0.8 broadcast_select_fusion.2
  0.8 0.5 collective-permute-start.1
  1.3 0.6 collective-permute-start
  1.9 1.0 fusion
  3.0 1.0 fusion.2
  4.0 0.9 slice_convert_fusion.4
  4.9 0.0 collective-permute-done.1
  4.9 0.0 collective-permute-done
  5.0 0.2 fusion.6
  5.1 0.8 fusion.8
  5.9 0.2 add_convert_fusion.4
  6.1 0.1 reshape.34.refs_0_
  6.2 7.4 %collective-permute-start.7 = (bf16[16,4096]{1,0:T(8,128)(2,1)S(1)}, bf16[16,4096]{1,0:T(8,128)(2,1)S(1)}, u32[]{:S(2)}, u32[]{:S(2)}) collective-permute-start(bf16[16,4096]{1,0:T(8,128)(2,1)S(1)} %reshape.34.refs_0_), channel_id=1, source_target_pairs={{0,12},{2,14},{4,8},{6,10},{8,4},{10,6},{12,0},{14,2},{1,13},{3,15... | collective-permute-start | bytes 393224 | tf_op jit(solution)/shard_map/ppermute | solution.py:22
  13.6 0.7 collective-permute-start.4
  14.3 1.4 %collective-permute-start.3 = (bf16[16,4096]{1,0:T(8,128)(2,1)S(1)}, bf16[16,4096]{1,0:T(8,128)(2,1)S(1)}, u32[]{:S(2)}, u32[]{:S(2)}) collective-permute-start(bf16[16,4096]{1,0:T(8,128)(2,1)S(1)} %reshape.34.refs_0_), channel_id=1, source_target_pairs={{0,4},{2,6},{4,0},{6,2},{8,12},{10,14},{12,8},{14,10},{1,5},{3,7},... | collective-permute-start | bytes 393224 | tf_op jit(solution)/shard_map/ppermute | solution.py:22
  15.7 1.4 %collective-permute-start.2 = (bf16[16,4096]{1,0:T(8,128)(2,1)S(1)}, bf16[16,4096]{1,0:T(8,128)(2,1)S(1)}, u32[]{:S(2)}, u32[]{:S(2)}) collective-permute-start(bf16[16,4096]{1,0:T(8,128)(2,1)S(1)} %reshape.34.refs_0_), channel_id=1, source_target_pairs={{0,2},{2,0},{4,6},{6,4},{8,10},{10,8},{12,14},{14,12},{1,3},{3,1},... | collective-permute-start | bytes 393224 | tf_op jit(solution)/shard_map/ppermute | solution.py:22
  17.1 0.9 collective-permute-done.7.refs_6_
  18.0 0.5 collective-permute-start.8
  18.5 6.6 %collective-permute-done.5.refs_4_ = bf16[16,4096]{1,0:T(8,128)(2,1)S(1)} collective-permute-done((bf16[16,4096]{1,0:T(8,128)(2,1)S(1)}, bf16[16,4096]{1,0:T(8,128)(2,1)S(1)}, u32[]{:S(2)}, u32[]{:S(2)}) %collective-permute-start.5) | collective-permute-done | bytes 131104 | tf_op jit(solution)/shard_map/ppermute | solution.py:22
  25.1 1.4 %collective-permute-start.6 = (bf16[16,4096]{1,0:T(8,128)(2,1)S(1)}, bf16[16,4096]{1,0:T(8,128)(2,1)S(1)}, u32[]{:S(2)}, u32[]{:S(2)}) collective-permute-start(bf16[16,4096]{1,0:T(8,128)(2,1)S(1)} %collective-permute-done.5.refs_4_), channel_id=1, source_target_pairs={{0,2},{2,0},{4,6},{6,4},{8,10},{10,8},{12,14},{14,12},{1,3},{3,1},... | collective-permute-start | bytes 393224 | tf_op jit(solution)/shard_map/ppermute | solution.py:22
  26.5 0.0 collective-permute-done.4.refs_3_
  26.5 3.7 %collective-permute-done.6.refs_5_ = bf16[16,4096]{1,0:T(8,128)(2,1)S(1)} collective-permute-done((bf16[16,4096]{1,0:T(8,128)(2,1)S(1)}, bf16[16,4096]{1,0:T(8,128)(2,1)S(1)}, u32[]{:S(2)}, u32[]{:S(2)}) %collective-permute-start.6) | collective-permute-done | bytes 131104 | tf_op jit(solution)/shard_map/ppermute | solution.py:22
  30.2 2.2 %copy-done.1 = bf16[4096,512]{1,0:T(8,128)(2,1)S(1)} copy-done((bf16[4096,512]{1,0:T(8,128)(2,1)S(1)}, bf16[4096,512]{1,0:T(8,128)(2,1)}, u32[]{:S(2)}) %copy-start.1) | copy-done | bytes 4194328
  32.4 1.5 %shard_map.82.refs_0_.coarse_ref = bf16[128,512]{1,0:T(8,128)(2,1)S(1)} custom-call(bf16[16,4096]{1,0:T(8,128)(2,1)S(1)} %reshape.34.refs_0_, bf16[16,4096]{1,0:T(8,128)(2,1)S(1)} %collective-permute-done.2.refs_1_, bf16[16,4096]{1,0:T(8,128)(2,1)S(1)} %collective-permute-done.3.refs_2_, bf16[16,4096]{1,0:T(8,128)(2,1)S(1)} %collective-permute-done.4.refs_3_, ...), custom_call_target="tpu_custom_call" | custom-call | tf_op jit(solution)/shard_map/pallas_call | solution.py:62
  33.9 2.4 %collective-permute-start.11 = (bf16[128,512]{1,0:T(8,128)(2,1)S(1)}, bf16[128,512]{1,0:T(8,128)(2,1)S(1)}, u32[]{:S(2)}, u32[]{:S(2)}) collective-permute-start(bf16[128,512]{1,0:T(8,128)(2,1)S(1)} %shard_map.82.refs_0_.coarse_ref), channel_id=1, source_target_pairs={{0,12},{2,14},{4,8},{6,10},{8,4},{10,6},{12,0},{14,2},{1,13},{3,15... | collective-permute-start | bytes 393224 | tf_op jit(solution)/shard_map/ppermute | solution.py:22
  36.3 3.2 %collective-permute-start.15 = (bf16[128,512]{1,0:T(8,128)(2,1)S(1)}, bf16[128,512]{1,0:T(8,128)(2,1)S(1)}, u32[]{:S(2)}, u32[]{:S(2)}) collective-permute-start(bf16[128,512]{1,0:T(8,128)(2,1)S(1)} %shard_map.82.refs_0_.coarse_ref), channel_id=1, source_target_pairs={{0,6},{2,4},{4,2},{6,0},{8,14},{10,12},{12,10},{14,8},{1,7},{3,5},... | collective-permute-start | bytes 393224 | tf_op jit(solution)/shard_map/ppermute | solution.py:22
  39.5 0.6 collective-permute-start.13
  40.1 1.8 %collective-permute-done.11.refs_5_ = bf16[128,512]{1,0:T(8,128)(2,1)S(1)} collective-permute-done((bf16[128,512]{1,0:T(8,128)(2,1)S(1)}, bf16[128,512]{1,0:T(8,128)(2,1)S(1)}, u32[]{:S(2)}, u32[]{:S(2)}) %collective-permute-start.11) | collective-permute-done | bytes 131104 | tf_op jit(solution)/shard_map/ppermute | solution.py:22
  41.8 2.1 %collective-permute-start.12 = (bf16[128,512]{1,0:T(8,128)(2,1)S(1)}, bf16[128,512]{1,0:T(8,128)(2,1)S(1)}, u32[]{:S(2)}, u32[]{:S(2)}) collective-permute-start(bf16[128,512]{1,0:T(8,128)(2,1)S(1)} %collective-permute-done.11.refs_5_), channel_id=1, source_target_pairs={{0,2},{2,0},{4,6},{6,4},{8,10},{10,8},{12,14},{14,12},{1,3},{3,1},... | collective-permute-start | bytes 393224 | tf_op jit(solution)/shard_map/ppermute | solution.py:22
  43.9 3.0 %collective-permute-done.9.refs_4_ = bf16[128,512]{1,0:T(8,128)(2,1)S(1)} collective-permute-done((bf16[128,512]{1,0:T(8,128)(2,1)S(1)}, bf16[128,512]{1,0:T(8,128)(2,1)S(1)}, u32[]{:S(2)}, u32[]{:S(2)}) %collective-permute-start.9) | collective-permute-done | bytes 131104 | tf_op jit(solution)/shard_map/ppermute | solution.py:22
  47.0 2.2 %collective-permute-start.10 = (bf16[128,512]{1,0:T(8,128)(2,1)S(1)}, bf16[128,512]{1,0:T(8,128)(2,1)S(1)}, u32[]{:S(2)}, u32[]{:S(2)}) collective-permute-start(bf16[128,512]{1,0:T(8,128)(2,1)S(1)} %collective-permute-done.9.refs_4_), channel_id=1, source_target_pairs={{0,2},{2,0},{4,6},{6,4},{8,10},{10,8},{12,14},{14,12},{1,3},{3,1},... | collective-permute-start | bytes 393224 | tf_op jit(solution)/shard_map/ppermute | solution.py:22
  49.2 4.2 %shard_map.83 = (f32[3,128,512]{2,1,0:T(8,128)S(1)}, f32[128,128]{1,0:T(8,128)S(1)}) custom-call(bf16[128,512]{1,0:T(8,128)(2,1)S(1)} %shard_map.82.refs_0_.coarse_ref, bf16[128,512]{1,0:T(8,128)(2,1)S(1)} %collective-permute-done.13.refs_1_, bf16[128,512]{1,0:T(8,128)(2,1)S(1)} %collective-permute-done.14.refs_2_, ...), custom_call_target="tpu_custom_call" | custom-call | tf_op jit(solution)/shard_map/pallas_call | solution.py:62
  53.4 0.0 copy-start
  53.5 2.5 %shard_map.84 = (bf16[128,512]{1,0:T(8,128)(2,1)S(1)}, bf16[2,128,512]{2,1,0:T(8,128)(2,1)S(1)}) custom-call(bf16[128,512]{1,0:T(8,128)(2,1)S(1)} %collective-permute-done.10.refs_0_, bf16[128,512]{1,0:T(8,128)(2,1)S(1)} %collective-permute-done.12.refs_1_, f32[1,4096]{1,0:T(1,128)S(1)} %bitcast.7, bf16[3,4096,512]{2,1,0:T(8,128)(2,1)} %refs_3_.1, ...), custom_call_target="tpu_custom_call" | custom-call | tf_op jit(solution)/shard_map/pallas_call | solution.py:62
  55.9 0.1 collective-permute-start.16
  56.0 1.5 %collective-permute-done.16.other_ref = bf16[2,128,512]{2,1,0:T(8,128)(2,1)S(1)} collective-permute-done((bf16[2,128,512]{2,1,0:T(8,128)(2,1)S(1)}, bf16[2,128,512]{2,1,0:T(8,128)(2,1)S(1)}, u32[]{:S(2)}, u32[]{:S(2)}) %collective-permute-start.16) | collective-permute-done | bytes 262176 | tf_op jit(solution)/shard_map/ppermute | solution.py:22
  57.5 2.2 %shard_map.85 = (bf16[128,512]{1,0:T(8,128)(2,1)S(1)}, bf16[128,512]{1,0:T(8,128)(2,1)S(1)}, bf16[128,512]{1,0:T(8,128)(2,1)S(1)}) custom-call(bf16[128,512]{1,0:T(8,128)(2,1)S(1)} %get-tuple-element.28.q_ref, bf16[2,128,512]{2,1,0:T(8,128)(2,1)S(1)} %get-tuple-element.29.own_ref, bf16[2,128,512]{2,1,0:T(8,128)(2,1)S(1)} %collective-permute-done.16.other_ref, ...), custom_call_target="tpu_custom_call" | custom-call | tf_op jit(solution)/shard_map/pallas_call | solution.py:62
  59.8 1.4 %collective-permute-start.17 = (bf16[128,512]{1,0:T(8,128)(2,1)S(1)}, bf16[128,512]{1,0:T(8,128)(2,1)S(1)}, u32[]{:S(2)}, u32[]{:S(2)}) collective-permute-start(bf16[128,512]{1,0:T(8,128)(2,1)S(1)} %get-tuple-element.33), channel_id=1, source_target_pairs={{0,2},{2,0},{4,6},{6,4},{8,10},{10,8},{12,14},{14,12},{1,3},{3,1},... | collective-permute-start | bytes 393224 | tf_op jit(solution)/shard_map/ppermute | solution.py:22
  61.2 0.7 collective-permute-start.19
  61.8 1.9 %shard_map.86 = (f32[128,512]{1,0:T(8,128)S(1)}, f32[128,512]{1,0:T(8,128)S(1)}, bf16[128,512]{1,0:T(8,128)(2,1)S(1)}, bf16[128,512]{1,0:T(8,128)(2,1)S(1)}, bf1...) custom-call(bf16[128,512]{1,0:T(8,128)(2,1)S(1)} %get-tuple-element.30.attended_ref, bf16[512,4096]{1,0:T(8,128)(2,1)S(1)} %copy-done), custom_call_target="tpu_custom_call" | custom-call | tf_op jit(solution)/shard_map/pallas_call | solution.py:62
  63.8 1.2 %collective-permute-start.21 = (bf16[128,512]{1,0:T(8,128)(2,1)S(1)}, bf16[128,512]{1,0:T(8,128)(2,1)S(1)}, u32[]{:S(2)}, u32[]{:S(2)}) collective-permute-start(bf16[128,512]{1,0:T(8,128)(2,1)S(1)} %get-tuple-element.36), channel_id=1, source_target_pairs={{0,6},{2,4},{4,2},{6,0},{8,14},{10,12},{12,10},{14,8},{1,7},{3,5},... | collective-permute-start | bytes 393224 | tf_op jit(solution)/shard_map/ppermute | solution.py:22
  65.0 1.7 %collective-permute-start.22 = (bf16[128,512]{1,0:T(8,128)(2,1)S(1)}, bf16[128,512]{1,0:T(8,128)(2,1)S(1)}, u32[]{:S(2)}, u32[]{:S(2)}) collective-permute-start(bf16[128,512]{1,0:T(8,128)(2,1)S(1)} %get-tuple-element.37), channel_id=1, source_target_pairs={{0,4},{2,6},{4,0},{6,2},{8,12},{10,14},{12,8},{14,10},{1,5},{3,7},... | collective-permute-start | bytes 393224 | tf_op jit(solution)/shard_map/ppermute | solution.py:22
  66.7 0.7 collective-permute-start.23
  67.4 2.1 %collective-permute-start.18 = (bf16[128,512]{1,0:T(8,128)(2,1)S(1)}, bf16[128,512]{1,0:T(8,128)(2,1)S(1)}, u32[]{:S(2)}, u32[]{:S(2)}) collective-permute-start(bf16[128,512]{1,0:T(8,128)(2,1)S(1)} %add_convert_fusion.3), channel_id=1, source_target_pairs={{0,12},{2,14},{4,8},{6,10},{8,4},{10,6},{12,0},{14,2},{1,13},{3,15... | collective-permute-start | bytes 393224 | tf_op jit(solution)/shard_map/ppermute | solution.py:22
  69.5 2.3 %collective-permute-done.19 = bf16[128,512]{1,0:T(8,128)(2,1)S(1)} collective-permute-done((bf16[128,512]{1,0:T(8,128)(2,1)S(1)}, bf16[128,512]{1,0:T(8,128)(2,1)S(1)}, u32[]{:S(2)}, u32[]{:S(2)}) %collective-permute-start.19) | collective-permute-done | bytes 131104 | tf_op jit(solution)/shard_map/ppermute | solution.py:22
  71.8 1.0 collective-permute-start.20
  72.8 1.8 %collective-permute-done.22.refs_3_ = bf16[128,512]{1,0:T(8,128)(2,1)S(1)} collective-permute-done((bf16[128,512]{1,0:T(8,128)(2,1)S(1)}, bf16[128,512]{1,0:T(8,128)(2,1)S(1)}, u32[]{:S(2)}, u32[]{:S(2)}) %collective-permute-start.22) | collective-permute-done | bytes 131104 | tf_op jit(solution)/shard_map/ppermute | solution.py:22
  74.7 1.8 %collective-permute-done.18.refs_0_ = bf16[128,512]{1,0:T(8,128)(2,1)S(1)} collective-permute-done((bf16[128,512]{1,0:T(8,128)(2,1)S(1)}, bf16[128,512]{1,0:T(8,128)(2,1)S(1)}, u32[]{:S(2)}, u32[]{:S(2)}) %collective-permute-start.18) | collective-permute-done | bytes 131104 | tf_op jit(solution)/shard_map/ppermute | solution.py:22
  76.4 4.3 %collective-permute-done.20.refs_1_ = bf16[128,512]{1,0:T(8,128)(2,1)S(1)} collective-permute-done((bf16[128,512]{1,0:T(8,128)(2,1)S(1)}, bf16[128,512]{1,0:T(8,128)(2,1)S(1)}, u32[]{:S(2)}, u32[]{:S(2)}) %collective-permute-start.20) | collective-permute-done | bytes 131104 | tf_op jit(solution)/shard_map/ppermute | solution.py:22
  80.8 3.1 %shard_map.87 = (f32[16,4096]{1,0:T(8,128)S(1)}, bf16[16,4096]{1,0:T(8,128)(2,1)S(1)}, bf16[16,4096]{1,0:T(8,128)(2,1)S(1)}, bf16[16,4096]{1,0:T(8,128)(2,1)S(1)...) custom-call(bf16[128,512]{1,0:T(8,128)(2,1)S(1)} %shard_map.82.refs_, ...), custom_call_target="tpu_custom_call" | custom-call | tf_op jit(solution)/shard_map/pallas_call | solution.py:62
  83.9 1.3 %collective-permute-start.24 = (bf16[16,4096]{1,0:T(8,128)(2,1)S(1)}, bf16[16,4096]{1,0:T(8,128)(2,1)S(1)}, u32[]{:S(2)}, u32[]{:S(2)}) collective-permute-start(bf16[16,4096]{1,0:T(8,128)(2,1)S(1)} %get-tuple-element.41), channel_id=1, source_target_pairs={{0,2},{2,0},{4,6},{6,4},{8,10},{10,8},{12,14},{14,12},{1,3},{3,1},... | collective-permute-start | bytes 393224 | tf_op jit(solution)/shard_map/ppermute | solution.py:22
  85.2 0.8 collective-permute-start.26
  86.0 2.7 %collective-permute-start.29 = (bf16[16,4096]{1,0:T(8,128)(2,1)S(1)}, bf16[16,4096]{1,0:T(8,128)(2,1)S(1)}, u32[]{:S(2)}, u32[]{:S(2)}) collective-permute-start(bf16[16,4096]{1,0:T(8,128)(2,1)S(1)} %get-tuple-element.45), channel_id=1, source_target_pairs={{0,4},{2,6},{4,0},{6,2},{8,12},{10,14},{12,8},{14,10},{1,5},{3,7},... | collective-permute-start | bytes 393224 | tf_op jit(solution)/shard_map/ppermute | solution.py:22
  88.7 0.8 collective-permute-start.30
  89.5 3.7 %collective-permute-done.24 = bf16[16,4096]{1,0:T(8,128)(2,1)S(1)} collective-permute-done((bf16[16,4096]{1,0:T(8,128)(2,1)S(1)}, bf16[16,4096]{1,0:T(8,128)(2,1)S(1)}, u32[]{:S(2)}, u32[]{:S(2)}) %collective-permute-start.24) | collective-permute-done | bytes 131104 | tf_op jit(solution)/shard_map/ppermute | solution.py:22
  93.2 2.0 %collective-permute-start.25 = (bf16[16,4096]{1,0:T(8,128)(2,1)S(1)}, bf16[16,4096]{1,0:T(8,128)(2,1)S(1)}, u32[]{:S(2)}, u32[]{:S(2)}) collective-permute-start(bf16[16,4096]{1,0:T(8,128)(2,1)S(1)} %add_convert_fusion.1), channel_id=1, source_target_pairs={{0,12},{2,14},{4,8},{6,10},{8,4},{10,6},{12,0},{14,2},{1,13},{3,15... | collective-permute-start | bytes 393224 | tf_op jit(solution)/shard_map/ppermute | solution.py:22
  95.2 0.8 collective-permute-done.26
  96.0 0.1 collective-permute-start.27
  96.1 1.6 %collective-permute-done.30 = bf16[16,4096]{1,0:T(8,128)(2,1)S(1)} collective-permute-done((bf16[16,4096]{1,0:T(8,128)(2,1)S(1)}, bf16[16,4096]{1,0:T(8,128)(2,1)S(1)}, u32[]{:S(2)}, u32[]{:S(2)}) %collective-permute-start.30) | collective-permute-done | bytes 131104 | tf_op jit(solution)/shard_map/ppermute | solution.py:22
  97.7 2.5 %collective-permute-done.25 = bf16[16,4096]{1,0:T(8,128)(2,1)S(1)} collective-permute-done((bf16[16,4096]{1,0:T(8,128)(2,1)S(1)}, bf16[16,4096]{1,0:T(8,128)(2,1)S(1)}, u32[]{:S(2)}, u32[]{:S(2)}) %collective-permute-start.25) | collective-permute-done | bytes 131104 | tf_op jit(solution)/shard_map/ppermute | solution.py:22
  100.1 3.4 %collective-permute-done.27 = bf16[16,4096]{1,0:T(8,128)(2,1)S(1)} collective-permute-done((bf16[16,4096]{1,0:T(8,128)(2,1)S(1)}, bf16[16,4096]{1,0:T(8,128)(2,1)S(1)}, u32[]{:S(2)}, u32[]{:S(2)}) %collective-permute-start.27) | collective-permute-done | bytes 131104 | tf_op jit(solution)/shard_map/ppermute | solution.py:22
  103.5 0.1 convert_add_fusion.1
  103.6 0.1 reshape.36
  103.7 0.7 fusion.3
  (29 shorter events, 0.2 us)
Async XLA Ops:
  0.0 49.2 %copy-start.2 = (f32[4096]{0:T(1024)S(1)}, f32[4096]{0:T(1024)}, u32[]{:S(2)}) copy-start(f32[4096]{0:T(1024)} %param.12) | copy-start | bytes 49156
  0.8 4.2 %collective-permute-start.1 = (bf16[2,1024]{1,0:T(2,128)(2,1)S(1)}, bf16[2,1024]{1,0:T(2,128)(2,1)S(1)}, u32[]{:S(2)}, u32[]{:S(2)}) collective-permute-start(bf16[2,1024]{1,0:T(2,128)(2,1)S(1)} %get-tuple-element.49), channel_id=1, source_target_pairs={{0,1},{1,0},{2,3},{3,2},{4,5},{5,4},{6,7},{7,6},{8,9},{9,8},{10,11... | collective-permute-start | bytes 12296 | tf_op jit(solution)/shard_map/ppermute | solution.py:237
  1.3 3.7 %collective-permute-start = (bf16[2,1024]{1,0:T(2,128)(2,1)S(1)}, bf16[2,1024]{1,0:T(2,128)(2,1)S(1)}, u32[]{:S(2)}, u32[]{:S(2)}) collective-permute-start(bf16[2,1024]{1,0:T(2,128)(2,1)S(1)} %get-tuple-element.50), channel_id=1, source_target_pairs={{1,2},{2,1},{3,4},{4,3},{5,6},{6,5},{7,8},{8,7},{9,10},{10,9},{11,... | collective-permute-start | bytes 12296 | tf_op jit(solution)/shard_map/ppermute | solution.py:238
  6.2 11.8 %collective-permute-start.7 = (bf16[16,4096]{1,0:T(8,128)(2,1)S(1)}, bf16[16,4096]{1,0:T(8,128)(2,1)S(1)}, u32[]{:S(2)}, u32[]{:S(2)}) collective-permute-start(bf16[16,4096]{1,0:T(8,128)(2,1)S(1)} %reshape.34.refs_0_), channel_id=1, source_target_pairs={{0,12},{2,14},{4,8},{6,10},{8,4},{10,6},{12,0},{14,2},{1,13},{3,15... | collective-permute-start | bytes 393224 | tf_op jit(solution)/shard_map/ppermute | solution.py:22
  13.6 11.5 %collective-permute-start.5 = (bf16[16,4096]{1,0:T(8,128)(2,1)S(1)}, bf16[16,4096]{1,0:T(8,128)(2,1)S(1)}, u32[]{:S(2)}, u32[]{:S(2)}) collective-permute-start(bf16[16,4096]{1,0:T(8,128)(2,1)S(1)} %reshape.34.refs_0_), channel_id=1, source_target_pairs={{0,8},{2,10},{4,12},{6,14},{8,0},{10,2},{12,4},{14,6},{1,9},{3,11}... | collective-permute-start | bytes 393224 | tf_op jit(solution)/shard_map/ppermute | solution.py:22
  13.6 12.9 %collective-permute-start.4 = (bf16[16,4096]{1,0:T(8,128)(2,1)S(1)}, bf16[16,4096]{1,0:T(8,128)(2,1)S(1)}, u32[]{:S(2)}, u32[]{:S(2)}) collective-permute-start(bf16[16,4096]{1,0:T(8,128)(2,1)S(1)} %reshape.34.refs_0_), channel_id=1, source_target_pairs={{0,6},{2,4},{4,2},{6,0},{8,14},{10,12},{12,10},{14,8},{1,7},{3,5},... | collective-permute-start | bytes 393224 | tf_op jit(solution)/shard_map/ppermute | solution.py:22
  14.3 12.2 %collective-permute-start.3 = (bf16[16,4096]{1,0:T(8,128)(2,1)S(1)}, bf16[16,4096]{1,0:T(8,128)(2,1)S(1)}, u32[]{:S(2)}, u32[]{:S(2)}) collective-permute-start(bf16[16,4096]{1,0:T(8,128)(2,1)S(1)} %reshape.34.refs_0_), channel_id=1, source_target_pairs={{0,4},{2,6},{4,0},{6,2},{8,12},{10,14},{12,8},{14,10},{1,5},{3,7},... | collective-permute-start | bytes 393224 | tf_op jit(solution)/shard_map/ppermute | solution.py:22
  15.7 10.8 %collective-permute-start.2 = (bf16[16,4096]{1,0:T(8,128)(2,1)S(1)}, bf16[16,4096]{1,0:T(8,128)(2,1)S(1)}, u32[]{:S(2)}, u32[]{:S(2)}) collective-permute-start(bf16[16,4096]{1,0:T(8,128)(2,1)S(1)} %reshape.34.refs_0_), channel_id=1, source_target_pairs={{0,2},{2,0},{4,6},{6,4},{8,10},{10,8},{12,14},{14,12},{1,3},{3,1},... | collective-permute-start | bytes 393224 | tf_op jit(solution)/shard_map/ppermute | solution.py:22
  18.0 8.5 %collective-permute-start.8 = (bf16[16,4096]{1,0:T(8,128)(2,1)S(1)}, bf16[16,4096]{1,0:T(8,128)(2,1)S(1)}, u32[]{:S(2)}, u32[]{:S(2)}) collective-permute-start(bf16[16,4096]{1,0:T(8,128)(2,1)S(1)} %collective-permute-done.7.refs_6_), channel_id=1, source_target_pairs={{0,2},{2,0},{4,6},{6,4},{8,10},{10,8},{12,14},{14,12},{1,3},{3,1},... | collective-permute-start | bytes 393224 | tf_op jit(solution)/shard_map/ppermute | solution.py:22
  25.1 5.1 %collective-permute-start.6 = (bf16[16,4096]{1,0:T(8,128)(2,1)S(1)}, bf16[16,4096]{1,0:T(8,128)(2,1)S(1)}, u32[]{:S(2)}, u32[]{:S(2)}) collective-permute-start(bf16[16,4096]{1,0:T(8,128)(2,1)S(1)} %collective-permute-done.5.refs_4_), channel_id=1, source_target_pairs={{0,2},{2,0},{4,6},{6,4},{8,10},{10,8},{12,14},{14,12},{1,3},{3,1},... | collective-permute-start | bytes 393224 | tf_op jit(solution)/shard_map/ppermute | solution.py:22
  30.2 2.2 %copy-start.1 = (bf16[4096,512]{1,0:T(8,128)(2,1)S(1)}, bf16[4096,512]{1,0:T(8,128)(2,1)}, u32[]{:S(2)}) copy-start(bf16[4096,512]{1,0:T(8,128)(2,1)} %refs_8_.1) | copy-start | bytes 12582916
  33.9 8.0 %collective-permute-start.11 = (bf16[128,512]{1,0:T(8,128)(2,1)S(1)}, bf16[128,512]{1,0:T(8,128)(2,1)S(1)}, u32[]{:S(2)}, u32[]{:S(2)}) collective-permute-start(bf16[128,512]{1,0:T(8,128)(2,1)S(1)} %shard_map.82.refs_0_.coarse_ref), channel_id=1, source_target_pairs={{0,12},{2,14},{4,8},{6,10},{8,4},{10,6},{12,0},{14,2},{1,13},{3,15... | collective-permute-start | bytes 393224 | tf_op jit(solution)/shard_map/ppermute | solution.py:22
  36.3 10.7 %collective-permute-start.9 = (bf16[128,512]{1,0:T(8,128)(2,1)S(1)}, bf16[128,512]{1,0:T(8,128)(2,1)S(1)}, u32[]{:S(2)}, u32[]{:S(2)}) collective-permute-start(bf16[128,512]{1,0:T(8,128)(2,1)S(1)} %shard_map.82.refs_0_.coarse_ref), channel_id=1, source_target_pairs={{0,8},{2,10},{4,12},{6,14},{8,0},{10,2},{12,4},{14,6},{1,9},{3,11}... | collective-permute-start | bytes 393224 | tf_op jit(solution)/shard_map/ppermute | solution.py:22
  36.3 12.9 %collective-permute-start.15 = (bf16[128,512]{1,0:T(8,128)(2,1)S(1)}, bf16[128,512]{1,0:T(8,128)(2,1)S(1)}, u32[]{:S(2)}, u32[]{:S(2)}) collective-permute-start(bf16[128,512]{1,0:T(8,128)(2,1)S(1)} %shard_map.82.refs_0_.coarse_ref), channel_id=1, source_target_pairs={{0,6},{2,4},{4,2},{6,0},{8,14},{10,12},{12,10},{14,8},{1,7},{3,5},... | collective-permute-start | bytes 393224 | tf_op jit(solution)/shard_map/ppermute | solution.py:22
  39.5 9.7 %collective-permute-start.14 = (bf16[128,512]{1,0:T(8,128)(2,1)S(1)}, bf16[128,512]{1,0:T(8,128)(2,1)S(1)}, u32[]{:S(2)}, u32[]{:S(2)}) collective-permute-start(bf16[128,512]{1,0:T(8,128)(2,1)S(1)} %shard_map.82.refs_0_.coarse_ref), channel_id=1, source_target_pairs={{0,4},{2,6},{4,0},{6,2},{8,12},{10,14},{12,8},{14,10},{1,5},{3,7},... | collective-permute-start | bytes 393224 | tf_op jit(solution)/shard_map/ppermute | solution.py:22
  39.5 9.7 %collective-permute-start.13 = (bf16[128,512]{1,0:T(8,128)(2,1)S(1)}, bf16[128,512]{1,0:T(8,128)(2,1)S(1)}, u32[]{:S(2)}, u32[]{:S(2)}) collective-permute-start(bf16[128,512]{1,0:T(8,128)(2,1)S(1)} %shard_map.82.refs_0_.coarse_ref), channel_id=1, source_target_pairs={{0,2},{2,0},{4,6},{6,4},{8,10},{10,8},{12,14},{14,12},{1,3},{3,1},... | collective-permute-start | bytes 393224 | tf_op jit(solution)/shard_map/ppermute | solution.py:22
  41.8 11.6 %collective-permute-start.12 = (bf16[128,512]{1,0:T(8,128)(2,1)S(1)}, bf16[128,512]{1,0:T(8,128)(2,1)S(1)}, u32[]{:S(2)}, u32[]{:S(2)}) collective-permute-start(bf16[128,512]{1,0:T(8,128)(2,1)S(1)} %collective-permute-done.11.refs_5_), channel_id=1, source_target_pairs={{0,2},{2,0},{4,6},{6,4},{8,10},{10,8},{12,14},{14,12},{1,3},{3,1},... | collective-permute-start | bytes 393224 | tf_op jit(solution)/shard_map/ppermute | solution.py:22
  47.0 6.5 %collective-permute-start.10 = (bf16[128,512]{1,0:T(8,128)(2,1)S(1)}, bf16[128,512]{1,0:T(8,128)(2,1)S(1)}, u32[]{:S(2)}, u32[]{:S(2)}) collective-permute-start(bf16[128,512]{1,0:T(8,128)(2,1)S(1)} %collective-permute-done.9.refs_4_), channel_id=1, source_target_pairs={{0,2},{2,0},{4,6},{6,4},{8,10},{10,8},{12,14},{14,12},{1,3},{3,1},... | collective-permute-start | bytes 393224 | tf_op jit(solution)/shard_map/ppermute | solution.py:22
  53.4 4.1 %copy-start = (bf16[512,4096]{1,0:T(8,128)(2,1)S(1)}, bf16[512,4096]{1,0:T(8,128)(2,1)}, u32[]{:S(2)}) copy-start(bf16[512,4096]{1,0:T(8,128)(2,1)} %w_ref.3) | copy-start | bytes 12582916
  55.9 1.6 %collective-permute-start.16 = (bf16[2,128,512]{2,1,0:T(8,128)(2,1)S(1)}, bf16[2,128,512]{2,1,0:T(8,128)(2,1)S(1)}, u32[]{:S(2)}, u32[]{:S(2)}) collective-permute-start(bf16[2,128,512]{2,1,0:T(8,128)(2,1)S(1)} %get-tuple-element.29.own_ref), channel_id=1, source_target_pairs={{0,1},{1,0},{2,3},{3,2},{4,5},{5,4},{6,7},{7,6},{8,9},{9,8},{10,11... | collective-permute-start | bytes 786440 | tf_op jit(solution)/shard_map/ppermute | solution.py:22
  59.8 7.6 %collective-permute-start.17 = (bf16[128,512]{1,0:T(8,128)(2,1)S(1)}, bf16[128,512]{1,0:T(8,128)(2,1)S(1)}, u32[]{:S(2)}, u32[]{:S(2)}) collective-permute-start(bf16[128,512]{1,0:T(8,128)(2,1)S(1)} %get-tuple-element.33), channel_id=1, source_target_pairs={{0,2},{2,0},{4,6},{6,4},{8,10},{10,8},{12,14},{14,12},{1,3},{3,1},... | collective-permute-start | bytes 393224 | tf_op jit(solution)/shard_map/ppermute | solution.py:22
  61.2 10.6 %collective-permute-start.19 = (bf16[128,512]{1,0:T(8,128)(2,1)S(1)}, bf16[128,512]{1,0:T(8,128)(2,1)S(1)}, u32[]{:S(2)}, u32[]{:S(2)}) collective-permute-start(bf16[128,512]{1,0:T(8,128)(2,1)S(1)} %get-tuple-element.35), channel_id=1, source_target_pairs={{0,2},{2,0},{4,6},{6,4},{8,10},{10,8},{12,14},{14,12},{1,3},{3,1},... | collective-permute-start | bytes 393224 | tf_op jit(solution)/shard_map/ppermute | solution.py:22
  63.8 9.0 %collective-permute-start.21 = (bf16[128,512]{1,0:T(8,128)(2,1)S(1)}, bf16[128,512]{1,0:T(8,128)(2,1)S(1)}, u32[]{:S(2)}, u32[]{:S(2)}) collective-permute-start(bf16[128,512]{1,0:T(8,128)(2,1)S(1)} %get-tuple-element.36), channel_id=1, source_target_pairs={{0,6},{2,4},{4,2},{6,0},{8,14},{10,12},{12,10},{14,8},{1,7},{3,5},... | collective-permute-start | bytes 393224 | tf_op jit(solution)/shard_map/ppermute | solution.py:22
  65.0 9.6 %collective-permute-start.22 = (bf16[128,512]{1,0:T(8,128)(2,1)S(1)}, bf16[128,512]{1,0:T(8,128)(2,1)S(1)}, u32[]{:S(2)}, u32[]{:S(2)}) collective-permute-start(bf16[128,512]{1,0:T(8,128)(2,1)S(1)} %get-tuple-element.37), channel_id=1, source_target_pairs={{0,4},{2,6},{4,0},{6,2},{8,12},{10,14},{12,8},{14,10},{1,5},{3,7},... | collective-permute-start | bytes 393224 | tf_op jit(solution)/shard_map/ppermute | solution.py:22
  66.7 8.0 %collective-permute-start.23 = (bf16[128,512]{1,0:T(8,128)(2,1)S(1)}, bf16[128,512]{1,0:T(8,128)(2,1)S(1)}, u32[]{:S(2)}, u32[]{:S(2)}) collective-permute-start(bf16[128,512]{1,0:T(8,128)(2,1)S(1)} %get-tuple-element.38), channel_id=1, source_target_pairs={{0,2},{2,0},{4,6},{6,4},{8,10},{10,8},{12,14},{14,12},{1,3},{3,1},... | collective-permute-start | bytes 393224 | tf_op jit(solution)/shard_map/ppermute | solution.py:22
  67.4 9.1 %collective-permute-start.18 = (bf16[128,512]{1,0:T(8,128)(2,1)S(1)}, bf16[128,512]{1,0:T(8,128)(2,1)S(1)}, u32[]{:S(2)}, u32[]{:S(2)}) collective-permute-start(bf16[128,512]{1,0:T(8,128)(2,1)S(1)} %add_convert_fusion.3), channel_id=1, source_target_pairs={{0,12},{2,14},{4,8},{6,10},{8,4},{10,6},{12,0},{14,2},{1,13},{3,15... | collective-permute-start | bytes 393224 | tf_op jit(solution)/shard_map/ppermute | solution.py:22
  71.8 31.9 %copy-start.3 = (bf16[64,1024]{1,0:T(8,128)(2,1)S(1)}, bf16[64,1024]{1,0:T(8,128)(2,1)}, u32[]{:S(2)}) copy-start(bf16[64,1024]{1,0:T(8,128)(2,1)} %param.8) | copy-start | bytes 393220
  71.8 9.0 %collective-permute-start.20 = (bf16[128,512]{1,0:T(8,128)(2,1)S(1)}, bf16[128,512]{1,0:T(8,128)(2,1)S(1)}, u32[]{:S(2)}, u32[]{:S(2)}) collective-permute-start(bf16[128,512]{1,0:T(8,128)(2,1)S(1)} %add_convert_fusion.2), channel_id=1, source_target_pairs={{0,8},{2,10},{4,12},{6,14},{8,0},{10,2},{12,4},{14,6},{1,9},{3,11}... | collective-permute-start | bytes 393224 | tf_op jit(solution)/shard_map/ppermute | solution.py:22
  83.9 9.3 %collective-permute-start.24 = (bf16[16,4096]{1,0:T(8,128)(2,1)S(1)}, bf16[16,4096]{1,0:T(8,128)(2,1)S(1)}, u32[]{:S(2)}, u32[]{:S(2)}) collective-permute-start(bf16[16,4096]{1,0:T(8,128)(2,1)S(1)} %get-tuple-element.41), channel_id=1, source_target_pairs={{0,2},{2,0},{4,6},{6,4},{8,10},{10,8},{12,14},{14,12},{1,3},{3,1},... | collective-permute-start | bytes 393224 | tf_op jit(solution)/shard_map/ppermute | solution.py:22
  85.2 10.8 %collective-permute-start.26 = (bf16[16,4096]{1,0:T(8,128)(2,1)S(1)}, bf16[16,4096]{1,0:T(8,128)(2,1)S(1)}, u32[]{:S(2)}, u32[]{:S(2)}) collective-permute-start(bf16[16,4096]{1,0:T(8,128)(2,1)S(1)} %get-tuple-element.43), channel_id=1, source_target_pairs={{0,2},{2,0},{4,6},{6,4},{8,10},{10,8},{12,14},{14,12},{1,3},{3,1},... | collective-permute-start | bytes 393224 | tf_op jit(solution)/shard_map/ppermute | solution.py:22
  86.0 10.1 %collective-permute-start.28 = (bf16[16,4096]{1,0:T(8,128)(2,1)S(1)}, bf16[16,4096]{1,0:T(8,128)(2,1)S(1)}, u32[]{:S(2)}, u32[]{:S(2)}) collective-permute-start(bf16[16,4096]{1,0:T(8,128)(2,1)S(1)} %get-tuple-element.44), channel_id=1, source_target_pairs={{0,6},{2,4},{4,2},{6,0},{8,14},{10,12},{12,10},{14,8},{1,7},{3,5},... | collective-permute-start | bytes 393224 | tf_op jit(solution)/shard_map/ppermute | solution.py:22
  86.0 10.1 %collective-permute-start.29 = (bf16[16,4096]{1,0:T(8,128)(2,1)S(1)}, bf16[16,4096]{1,0:T(8,128)(2,1)S(1)}, u32[]{:S(2)}, u32[]{:S(2)}) collective-permute-start(bf16[16,4096]{1,0:T(8,128)(2,1)S(1)} %get-tuple-element.45), channel_id=1, source_target_pairs={{0,4},{2,6},{4,0},{6,2},{8,12},{10,14},{12,8},{14,10},{1,5},{3,7},... | collective-permute-start | bytes 393224 | tf_op jit(solution)/shard_map/ppermute | solution.py:22
  88.7 9.0 %collective-permute-start.30 = (bf16[16,4096]{1,0:T(8,128)(2,1)S(1)}, bf16[16,4096]{1,0:T(8,128)(2,1)S(1)}, u32[]{:S(2)}, u32[]{:S(2)}) collective-permute-start(bf16[16,4096]{1,0:T(8,128)(2,1)S(1)} %get-tuple-element.46), channel_id=1, source_target_pairs={{0,2},{2,0},{4,6},{6,4},{8,10},{10,8},{12,14},{14,12},{1,3},{3,1},... | collective-permute-start | bytes 393224 | tf_op jit(solution)/shard_map/ppermute | solution.py:22
  93.2 6.9 %collective-permute-start.25 = (bf16[16,4096]{1,0:T(8,128)(2,1)S(1)}, bf16[16,4096]{1,0:T(8,128)(2,1)S(1)}, u32[]{:S(2)}, u32[]{:S(2)}) collective-permute-start(bf16[16,4096]{1,0:T(8,128)(2,1)S(1)} %add_convert_fusion.1), channel_id=1, source_target_pairs={{0,12},{2,14},{4,8},{6,10},{8,4},{10,6},{12,0},{14,2},{1,13},{3,15... | collective-permute-start | bytes 393224 | tf_op jit(solution)/shard_map/ppermute | solution.py:22
  96.0 7.5 %collective-permute-start.27 = (bf16[16,4096]{1,0:T(8,128)(2,1)S(1)}, bf16[16,4096]{1,0:T(8,128)(2,1)S(1)}, u32[]{:S(2)}, u32[]{:S(2)}) collective-permute-start(bf16[16,4096]{1,0:T(8,128)(2,1)S(1)} %add_convert_fusion), channel_id=1, source_target_pairs={{0,8},{2,10},{4,12},{6,14},{8,0},{10,2},{12,4},{14,6},{1,9},{3,11}... | collective-permute-start | bytes 393224 | tf_op jit(solution)/shard_map/ppermute | solution.py:22

commit v3 on v2

v3 whole, which is shorter than its diff:
```python
import functools
import math

import jax
import jax.numpy as jnp
from jax import lax
from jax.experimental import pallas as pl
from jax.experimental.pallas import tpu as pltpu
from jax.sharding import PartitionSpec as P

DF = 1024
HD = 128
KW = 5
VMEM = pltpu.VMEM


epsilon = 1e-06


def flip(value, axis, mask):
    pairs = [(source, source ^ mask) for source in range(lax.axis_size(axis))]
    return lax.ppermute(value, axis, pairs)


def relayed(mask, size):
    return mask & 1 == 1 and mask >= max(size // 2, 2)


def far_first(size):
    return sorted(range(1, size), reverse=True)


def after_all(values, others):
    return lax.optimization_barrier((tuple(values), tuple(others)))[0]


def gather_flips(value, axis, fetched):
    size, rows = lax.axis_size(axis), value.shape[0]
    arrays = [value] + [None] * (size - 1)
    for mask in far_first(size):
        if not relayed(mask, size):
            arrays[mask] = flip(value, axis, mask)
    for mask in far_first(size):
        if relayed(mask, size):
            arrays[mask] = flip(after_all((arrays[mask ^ 1],), fetched)[0], axis, 1)
    return arrays, {mask: [(mask, 0, rows)] for mask in range(size)}


def late_masks(size):
    return [m for m in range(size) if relayed(m, size)]


def early_masks(size):
    return [m for m in range(size) if m not in late_masks(size)]


def scatter_plan(size, rows):
    relays = [m for m in far_first(size) if relayed(m, size)]
    via = [m ^ 1 for m in relays]
    rest = via + [m for m in far_first(size) if m not in via and m not in relays]
    first = [(m, [(m, 0, rows)], False) for m in relays]
    second = [(m, [(m, 0, rows)], m in via) for m in rest] + [("own", [(0, 0, rows)], True)]
    return first, second


def scatter_flips(parts, axis):
    size, rows = lax.axis_size(axis), parts["own"].shape[0]

    def plus(part, *others):
        return sum([o.astype(jnp.float32) for o in others], part).astype(jnp.bfloat16)

    arrived = []
    passed = {m ^ 1: flip(parts[m], axis, 1) for m in far_first(size) if relayed(m, size)}
    for mask in far_first(size):
        if not relayed(mask, size):
            part = plus(parts[mask], passed[mask]) if mask in passed else parts[mask]
            arrived.append((flip(part, axis, mask), 0, 0, rows))
    return arrived


def call(body, outs, scratch, in_memory, *operands, aliases=None):
    specs = [
        pl.BlockSpec(memory_space=pl.ANY if where == "h" else VMEM) for where in in_memory
    ]
    return pl.pallas_call(
        body,
        out_shape=outs,
        in_specs=specs,
        out_specs=jax.tree.map(lambda _: pl.BlockSpec(memory_space=VMEM), outs),
        scratch_shapes=scratch,
        input_output_aliases=aliases or {},
        compiler_params=pltpu.CompilerParams(vmem_limit_bytes=20 * 2**20),
    )(
        *[
            pltpu.with_memory_space_constraint(o, pltpu.HBM) if where == "h" else o
            for where, o in zip(in_memory, operands)
        ]
    )


def sds(shape, dtype):
    return jax.ShapeDtypeStruct(shape, dtype)


def dot(left, right):
    return jnp.dot(left, right, preferred_element_type=jnp.float32)


def offset(mask, width):
    return pl.multiple_of((lax.axis_index("seq") ^ mask) * width, width)


def start_all(copies):
    for copy in copies:
        copy.start()
    return copies


def rows_of(refs, place):
    parts = [refs[i][first : first + rows] for i, first, rows in place]
    return parts[0] if len(parts) == 1 else jnp.concatenate(parts, axis=0)


def needed(places, masks):
    which = sorted({i for mask in masks for i, _, _ in places[mask]})
    number = {i: n for n, i in enumerate(which)}
    return which, {m: [(number[i], f, r) for i, f, r in places[m]] for m in masks}


def down_rows(places, refs, product, out_ref):
    first = 0
    for mask, place in places.items():
        rows = sum(r for _, _, r in place)
        out_ref[pl.ds(offset(mask, rows), rows), :] = product[first : first + rows].astype(
            jnp.bfloat16
        )
        first += rows


def fetch_kernel(count, *refs):
    sources, targets, sems = refs[:count], refs[count + 1 : -1], refs[-1]
    copies = start_all(
        [
            pltpu.make_async_copy(source, target, sems.at[n])
            for n, (source, target) in enumerate(zip(sources, targets))
        ]
    )
    for copy in copies:
        copy.wait()


def fetch(after, *weights):
    count = len(weights)
    return call(
        functools.partial(fetch_kernel, count),
        tuple(sds(w.shape, w.dtype) for w in weights),
        [pltpu.SemaphoreType.DMA((count,))],
        "h" * count + "v",
        *weights,
        after,
    )


def slice_copy(w_ref, mask, target, sem):
    columns = target.shape[1]
    return pltpu.make_async_copy(
        w_ref.at[:, pl.ds(offset(mask, columns), columns), :], target, sem
    )


def fetch_slices_kernel(masks, w_ref, _, kept_ref, sems):
    copies = start_all(
        [slice_copy(w_ref, m, kept_ref.at[n], sems.at[n]) for n, m in enumerate(masks)]
    )
    for copy in copies:
        copy.wait()


def down_early(places, count, *refs):
    blocks, (w_ref, later_ref, out_ref, kept_ref, sem) = refs[:count], refs[count:]
    copy = pltpu.make_async_copy(later_ref, kept_ref, sem)
    copy.start()
    rows = jnp.concatenate([rows_of(blocks, place) for place in places.values()], axis=0)
    down_rows(places, blocks, dot(rows, w_ref[...]), out_ref)
    copy.wait()


def down_late(places, count, *refs):
    blocks, w_ref, _, out_ref = refs[:count], *refs[count:]
    rows = jnp.concatenate([rows_of(blocks, place) for place in places.values()], axis=0)
    down_rows(places, blocks, dot(rows, w_ref[...]), out_ref)


def qkv_steps(places, blocks, gain_ref, weights, totals, squares):
    for step, (mask, place) in enumerate(places.items()):
        block = rows_of(blocks, place).astype(jnp.float32)
        columns = block.shape[1]
        part = jnp.sum(block * block, axis=1, keepdims=True)
        squares = part if squares is None else squares + part
        gained = (block * gain_ref[:, pl.ds(offset(mask, columns), columns)]).astype(jnp.bfloat16)
        held = weights(step)
        products = [dot(gained, held[which]) for which in range(3)]
        totals = products if totals is None else [t + p for t, p in zip(totals, products)]
    return totals, squares


def qkv_early(places, kept_masks, count, *refs):
    blocks, (gain_ref, w_ref, kept_ref, totals_ref, squares_ref, held, sems) = (
        refs[:count],
        refs[count:],
    )
    order = list(places)
    streamed = [m for m in order if m not in kept_masks]
    copies = start_all(
        [slice_copy(w_ref, m, held.at[n], sems.at[n]) for n, m in enumerate(streamed)]
    )

    def weights(step):
        mask = order[step]
        if mask in kept_masks:
            return kept_ref.at[kept_masks.index(mask)]
        copies[streamed.index(mask)].wait()
        return held.at[streamed.index(mask)]

    totals, squares = qkv_steps(places, blocks, gain_ref, weights, None, None)
    for which in range(3):
        totals_ref[which] = totals[which]
    squares_ref[...] = jnp.broadcast_to(squares, squares_ref.shape)


def qkv_late(places, features, count, *refs):
    blocks = refs[:count]
    gain_ref, kept_ref, totals_ref, squares_ref, q_ref, kv_ref = refs[count:]
    totals, squares = qkv_steps(
        places,
        blocks,
        gain_ref,
        lambda step: kept_ref.at[step],
        [totals_ref[which] for which in range(3)],
        squares_ref[:, :1],
    )
    scale = lax.rsqrt(squares / features + epsilon)
    q_ref[...] = (totals[0] * scale).astype(jnp.bfloat16)
    kv_ref[0] = (totals[1] * scale).astype(jnp.bfloat16)
    kv_ref[1] = (totals[2] * scale).astype(jnp.bfloat16)


def write_chunks(plan, attended_ref, w_ref, out_refs):
    columns = attended_ref.shape[1]
    for mask in dict.fromkeys(m for _, parts, _ in plan for m, _, _ in parts):
        chunk = dot(attended_ref[...], w_ref[:, pl.ds(offset(mask, columns), columns)])
        write_parts(plan, mask, lambda first, last: chunk[first:last], out_refs, slice(None))


def write_parts(plan, mask, rows, out_refs, columns):
    for (_, parts, _), ref in zip(plan, out_refs):
        at = 0
        for m, first, last in parts:
            if m == mask:
                ref[at : at + last - first, columns] = rows(first, last).astype(ref.dtype)
            at += last - first


def attend_kernel(plan, q_ref, own_ref, other_ref, w_ref, attended_ref, *out_refs):
    columns = q_ref.shape[1]
    contract = (((1,), (1,)), ((), ()))
    for head in range(columns // HD):
        here = slice(head * HD, (head + 1) * HD)
        query = q_ref[:, here]
        scores = [
            lax.dot_general(query, kv[0, :, here], contract, preferred_element_type=jnp.float32)
            * (1.0 / math.sqrt(HD))
            for kv in (own_ref, other_ref)
        ]
        peak = jnp.maximum(*[jnp.max(s, axis=1, keepdims=True) for s in scores])
        weights = [jnp.exp(s - peak) for s in scores]
        norm = sum(jnp.sum(w, axis=1, keepdims=True) for w in weights)
        attended_ref[:, here] = sum(
            dot((w / norm).astype(jnp.bfloat16), kv[1, :, here])
            for w, kv in zip(weights, (own_ref, other_ref))
        ).astype(jnp.bfloat16)
    write_chunks(plan, attended_ref, w_ref, out_refs)


def out_kernel(plan, attended_ref, w_ref, *out_refs):
    write_chunks(plan, attended_ref, w_ref, out_refs)


def up_kernel(size, plan, places, pieces, coarse_ref, own_ref, *refs):
    count = len(places)
    arrived, w_ref, out_refs, (mixed_ref, sums) = (
        refs[:count],
        refs[count],
        refs[count + 1 : -2],
        refs[-2:],
    )
    width = w_ref.shape[1] // pieces
    mixed_ref[...] = own_ref[...]
    for value, (source, target, rows) in zip(arrived, places):
        mixed_ref[target : target + rows, :] += value[source : source + rows].astype(jnp.float32)
    mixed = (coarse_ref[...].astype(jnp.float32) + mixed_ref[...]).astype(jnp.bfloat16)
    own_tokens = mixed.shape[0] // size
    for p in range(pieces):
        here = slice(p * width, (p + 1) * width)
        sums[...] = dot(mixed, w_ref[:, here])
        for mask in range(size):
            chunk = sums[pl.ds(offset(mask, own_tokens), own_tokens), :]
            write_parts(plan, mask, lambda first, last: chunk[first:last], out_refs, here)


def scaled(rows, gain):
    mean = jnp.mean(rows * rows, axis=1, keepdims=True)
    return (rows * lax.rsqrt(mean + epsilon) * gain).astype(jnp.bfloat16).astype(jnp.float32)


def norm_kernel(frames_ref, gain_ref, taps_ref, normed_ref, kept_ref, wide_ref, held, taps, sems):
    copies = start_all(
        [
            pltpu.make_async_copy(source, target, sems.at[n])
            for n, (source, target) in enumerate(
                [(frames_ref, held), (gain_ref, kept_ref), (taps_ref, taps)]
            )
        ]
    )
    for copy in copies:
        copy.wait()
    wide_ref[...] = taps[...].astype(jnp.float32)
    normed_ref[...] = scaled(held[...].astype(jnp.float32), kept_ref[...])


def conv_kernel(before_ref, after_ref, normed_ref, gain_ref, taps_ref, out_ref, padded):
    frame_rows = normed_ref.shape[0]
    edge = KW // 2
    padded[8 - edge : 8, :] = scaled(before_ref[...].astype(jnp.float32), gain_ref[...])
    padded[8 : 8 + frame_rows, :] = normed_ref[...]
    padded[8 + frame_rows : 8 + frame_rows + edge, :] = scaled(
        after_ref[...].astype(jnp.float32), gain_ref[...]
    )
    total = None
    for tap in range(KW):
        first = 8 - edge + tap
        part = padded[first : first + frame_rows, :] * taps_ref[tap : tap + 1, :]
        total = part if total is None else total + part
    out_ref[...] = total.astype(jnp.bfloat16)


def edge_rows(frames, width):
    size, inner = lax.axis_size("seq"), lax.axis_size("sub")
    position = lax.axis_index("seq") * inner + lax.axis_index("sub")
    total = size * inner
    first, last = frames[:width], frames[-width:]
    even = (position & 1) == 0
    inside = [(i, i ^ 1) for i in range(total)]
    across = [(i, ((i + 1) ^ 1) - 1) for i in range(1, total - 1)]
    near = lax.ppermute(jnp.where(even, last, first), ("seq", "sub"), inside)
    far = lax.ppermute(jnp.where(even, first, last), ("seq", "sub"), across)
    return jnp.where(even, far, near), jnp.where(even, near, far)


def per_device(frames, fine_gain, dw_kernel, w_down, coarse_gain, w_qkv, w_out, w_up):
    frame_rows = frames.shape[0]
    columns = w_qkv.shape[2]
    size = lax.axis_size("seq")
    features = columns * size
    own_tokens = frame_rows // 4
    tokens = own_tokens * size
    bf16, f32 = jnp.bfloat16, jnp.float32

    before, after = edge_rows(frames, KW // 2)
    frames_f32 = frames.astype(f32)

    normed, gain_kept, taps = call(
        norm_kernel,
        (sds(frames.shape, f32), sds((1, DF), f32), sds(dw_kernel.shape, f32)),
        [VMEM(frames.shape, bf16), VMEM(dw_kernel.shape, bf16), pltpu.SemaphoreType.DMA((3,))],
        "hhh",
        frames,
        fine_gain.reshape(1, DF),
        dw_kernel,
    )
    patches = call(
        conv_kernel,
        sds(frames.shape, bf16),
        [VMEM((frame_rows + 16, DF), f32)],
        "vvvvv",
        before,
        after,
        normed,
        gain_kept,
        taps,
    ).reshape(own_tokens, 4 * DF)

    pieces = 8
    early, late = early_masks(size), late_masks(size)

    w_down_kept, w_out_kept = fetch(patches, w_down, w_out)
    arrays, places = gather_flips(patches, "seq", (w_down_kept, w_out_kept))
    which, here = needed(places, early)
    coarse, w_up_kept = call(
        functools.partial(down_early, here, len(which)),
        (sds((tokens, columns), bf16), sds(w_up.shape, bf16)),
        [pltpu.SemaphoreType.DMA],
        "v" * len(which) + "vh",
        *[arrays[i] for i in which],
        w_down_kept,
        w_up,
    )
    which, here = needed(places, late)
    coarse = call(
        functools.partial(down_late, here, len(which)),
        sds((tokens, columns), bf16),
        [],
        "v" * len(which) + "vv",
        *[arrays[i] for i in which],
        w_down_kept,
        coarse,
        aliases={len(which) + 1: 0},
    )

    kept_masks = late + early[: len(early) // 2]
    streamed = [m for m in early if m not in kept_masks]
    kept = call(
        functools.partial(fetch_slices_kernel, kept_masks),
        sds((len(kept_masks), 3, columns, columns), bf16),
        [pltpu.SemaphoreType.DMA((len(kept_masks),))],
        "hv",
        w_qkv,
        coarse,
    )
    arrays, places = gather_flips(coarse, "seq", (kept,))
    gain_row = coarse_gain.reshape(1, features)
    which, here = needed(places, early)
    totals, squares = call(
        functools.partial(qkv_early, here, kept_masks, len(which)),
        (sds((3, tokens, columns), f32), sds((tokens, 128), f32)),
        [
            VMEM((len(streamed), 3, columns, columns), bf16),
            pltpu.SemaphoreType.DMA((len(streamed),)),
        ],
        "v" * len(which) + "vhv",
        *[arrays[i] for i in which],
        gain_row,
        w_qkv,
        kept,
    )
    which, here = needed(places, late)
    queries, own_kv = call(
        functools.partial(qkv_late, here, features, len(which)),
        (sds((tokens, columns), bf16), sds((2, tokens, columns), bf16)),
        [],
        "v" * len(which) + "vvvv",
        *[arrays[i] for i in which],
        gain_row,
        kept,
        totals,
        squares,
    )
    other_kv = flip(own_kv, "sub", 1)

    def planned(plan, width):
        return tuple(
            sds((sum(last - first for _, first, last in parts), width), f32 if wide else bf16)
            for _, parts, wide in plan
        )

    first_plan, second_plan = scatter_plan(size, tokens)
    attended, *first = call(
        functools.partial(attend_kernel, first_plan),
        (sds((tokens, columns), bf16),) + planned(first_plan, columns),
        [],
        "vvvv",
        queries,
        own_kv,
        other_kv,
        w_out_kept,
    )
    second = call(
        functools.partial(out_kernel, second_plan),
        planned(second_plan, columns),
        [],
        "vv",
        attended,
        w_out_kept,
    )
    names = [name for name, _, _ in first_plan + second_plan]
    parts = dict(zip(names, [*first, *second]))
    arrived = scatter_flips(parts, "seq")
    first_plan, second_plan = scatter_plan(size, own_tokens)
    lifted = call(
        functools.partial(
            up_kernel, size, first_plan + second_plan, [a[1:] for a in arrived], pieces
        ),
        planned(first_plan + second_plan, 4 * DF),
        [VMEM((tokens, columns), f32), VMEM((tokens, 4 * DF // pieces), f32)],
        "vv" + "v" * len(arrived) + "v",
        coarse,
        parts["own"],
        *[a[0] for a in arrived],
        w_up_kept,
    )
    parts = dict(zip(names, lifted))
    total = parts["own"]
    for value, source, target, rows in scatter_flips(parts, "seq"):
        value = value[source : source + rows].astype(f32)
        total = total + jnp.pad(value, ((target, own_tokens - target - rows), (0, 0)))
    return (frames_f32 + total.reshape(frame_rows, DF)).astype(bf16)


def solution(mesh):
    placed = (
        P(("groups", "seq", "sub"), None),
        P(),
        P(),
        P(None, "seq"),
        P(),
        P(None, None, "seq"),
        P("seq", None),
        P("seq", None),
    )
    return jax.shard_map(
        per_device,
        mesh=mesh,
        in_specs=placed,
        out_specs=P(("groups", "seq", "sub"), None),
        check_vma=False,
    )
```

time: 105 us -> 95.8 us (0.912)
  waiting for transfers between devices: 39.6 us -> 24.7 us
  starting transfers between devices: 41 us -> 50.4 us
  other arithmetic: 5.73 us -> 1.66 us
  Pallas kernels: 15.4 us -> 18.2 us
  local copies, waits for them, and re-layouts: 2.37 us -> 0.17 us
    ppermute x29, waiting for transfers between devices: 39.6 us -> 24.7 us  [flip(): return lax.ppermute(value, axis, pairs)]
    ppermute x29, starting transfers between devices: 39.8 us -> 45.3 us  [flip(): return lax.ppermute(value, axis, pairs)]
    ppermute x1, starting transfers between devices: 0.52 us -> 4.39 us  [edge_rows(): near = lax.ppermute(jnp.where(even, last, first), ('seq', 'sub'), inside)]
    pallas_call x6 -> x11, Pallas kernels: 15.4 us -> 18.2 us  [call(): pl.pallas_call(body, out_shape=outs, in_specs=specs, out_specs=jax.tree.m...]
    unnamed x8 -> x4, local copies, waits for them, and re-layouts: 2.2 us -> 0.01 us
    convert_element_type x7 -> x4, other arithmetic: 2.07 us -> 0.11 us  [plus(): sum([o.astype(jnp.float32) for o in others], part).astype(jnp.bfloat16)]
    reduce_sum x2 -> x0, other arithmetic: 1.19 us -> none  [normed(): jnp.mean(rows * rows, axis=1, keepdims=True) + epsilon]
  transfers between devices with their start and end apart: 31 -> 31, of which waited for: 15 -> 11; matrix products, arithmetic and copies ran while one was open for 3% -> 0% of each run, Pallas kernels for 6% -> 15%
where the time goes in v3:
time: 95.8 us; the launch traced here: 95.4 us
  starting transfers between devices  50.4 us (53%)
  waiting for transfers between devices  24.7 us (26%)
  Pallas kernels  18.2 us (19%)
  other arithmetic  1.66 us (2%)
    ppermute x29, starting transfers between devices, flip(): return lax.ppermute(value, axis, pairs)  45.3 us
    ppermute x29, waiting for transfers between devices, flip(): return lax.ppermute(value, axis, pairs)  24.7 us
    pallas_call x11, Pallas kernels, call(): pl.pallas_call(body, out_shape=outs, in_specs=specs, out_specs=jax.tree.m...  18.2 us
    ppermute x1, starting transfers between devices, edge_rows(): near = lax.ppermute(jnp.where(even, last, first), ('seq', 'sub'), inside)  4.39 us
  transfers between devices with their start and end apart: 31, of which 11 were waited for; matrix products, arithmetic and copies ran while one was open for 0% of the time, Pallas kernels for 15%

profile of v3, /device:TPU:0, one launch (start us, length us, event | category | flops | bytes accessed | tf_op | source)
XLA Modules:
  0.0 95.4 jit_solution(3684413808889516966)
XLA Ops:
  0.0 0.7 broadcast_select_fusion.2
  0.8 0.7 collective-permute-start
  1.4 4.4 %collective-permute-start.1 = (bf16[2,1024]{1,0:T(2,128)(2,1)S(1)}, bf16[2,1024]{1,0:T(2,128)(2,1)S(1)}, u32[]{:S(2)}, u32[]{:S(2)}) collective-permute-start(bf16[2,1024]{1,0:T(2,128)(2,1)S(1)} %get-tuple-element.69), channel_id=1, source_target_pairs={{0,1},{1,0},{2,3},{3,2},{4,5},{5,4},{6,7},{7,6},{8,9},{9,8},{10,11... | collective-permute-start | bytes 12296 | tf_op jit(solution)/shard_map/ppermute | solution.py:355
  5.8 1.1 %shard_map.82 = (f32[64,1024]{1,0:T(8,128)S(1)}, f32[1,1024]{1,0:T(1,128)S(1)}, f32[5,1024]{1,0:T(8,128)S(1)}) custom-call(bf16[64,1024]{1,0:T(8,128)(2,1)} %frames_ref.1, f32[1,1024]{1,0:T(1,128)} %bitcast.4, bf16[5,1024]{1,0:T(8,128)(2,1)} %taps_ref.1), custom_call_target="tpu_custom_call" | custom-call | tf_op jit(solution)/shard_map/pallas_call | solution.py:85
  6.9 0.0 collective-permute-done
  6.9 0.0 collective-permute-done.1
  6.9 0.3 shard_map.83
  7.2 0.1 reshape.13.refs_2_.refs_0_
  7.3 4.8 %collective-permute-start.4 = (bf16[16,4096]{1,0:T(8,128)(2,1)S(1)}, bf16[16,4096]{1,0:T(8,128)(2,1)S(1)}, u32[]{:S(2)}, u32[]{:S(2)}) collective-permute-start(bf16[16,4096]{1,0:T(8,128)(2,1)S(1)} %reshape.13.refs_2_.refs_0_), channel_id=1, source_target_pairs={{0,12},{2,14},{4,8},{6,10},{8,4},{10,6},{12,0},{14,2},{1,13},{3,15... | collective-permute-start | bytes 393224 | tf_op jit(solution)/shard_map/ppermute | solution.py:22
  12.1 0.6 collective-permute-start.6
  12.7 0.8 collective-permute-start.7
  13.5 2.1 %collective-permute-start.8 = (bf16[16,4096]{1,0:T(8,128)(2,1)S(1)}, bf16[16,4096]{1,0:T(8,128)(2,1)S(1)}, u32[]{:S(2)}, u32[]{:S(2)}) collective-permute-start(bf16[16,4096]{1,0:T(8,128)(2,1)S(1)} %reshape.13.refs_2_.refs_0_), channel_id=1, source_target_pairs={{0,6},{2,4},{4,2},{6,0},{8,14},{10,12},{12,10},{14,8},{1,7},{3,5},... | collective-permute-start | bytes 393224 | tf_op jit(solution)/shard_map/ppermute | solution.py:22
  15.6 3.5 %shard_map.84 = (bf16[4096,512]{1,0:T(8,128)(2,1)S(1)}, bf16[512,4096]{1,0:T(8,128)(2,1)S(1)}) custom-call(bf16[4096,512]{1,0:T(8,128)(2,1)} %refs_0_.1, bf16[512,4096]{1,0:T(8,128)(2,1)} %refs_1_.1, bf16[16,4096]{1,0:T(8,128)(2,1)S(1)} %reshape.13.refs_2_.refs_0_), custom_call_target="tpu_custom_call" | custom-call | tf_op jit(solution)/shard_map/pallas_call | solution.py:85
  19.1 0.0 collective-permute-done.4.refs_5_
  19.1 0.7 collective-permute-start.5
  19.8 2.7 %collective-permute-done.2.refs_4_ = bf16[16,4096]{1,0:T(8,128)(2,1)S(1)} collective-permute-done((bf16[16,4096]{1,0:T(8,128)(2,1)S(1)}, bf16[16,4096]{1,0:T(8,128)(2,1)S(1)}, u32[]{:S(2)}, u32[]{:S(2)}) %collective-permute-start.2) | collective-permute-done | bytes 131104 | tf_op jit(solution)/shard_map/ppermute | solution.py:22
  22.5 2.4 %collective-permute-start.3 = (bf16[16,4096]{1,0:T(8,128)(2,1)S(1)}, bf16[16,4096]{1,0:T(8,128)(2,1)S(1)}, u32[]{:S(2)}, u32[]{:S(2)}) collective-permute-start(bf16[16,4096]{1,0:T(8,128)(2,1)S(1)} %collective-permute-done.2.refs_4_), channel_id=1, source_target_pairs={{0,2},{2,0},{4,6},{6,4},{8,10},{10,8},{12,14},{14,12},{1,3},{3,1},... | collective-permute-start | bytes 393224 | tf_op jit(solution)/shard_map/ppermute | solution.py:22
  24.8 0.0 collective-permute-done.6.refs_1_
  24.8 0.3 collective-permute-done.8.refs_3_
  25.1 2.2 %shard_map.85 = (bf16[128,512]{1,0:T(8,128)(2,1)S(1)}, bf16[512,4096]{1,0:T(8,128)(2,1)S(1)}) custom-call(bf16[16,4096]{1,0:T(8,128)(2,1)S(1)} %reshape.13.refs_2_.refs_0_, bf16[16,4096]{1,0:T(8,128)(2,1)S(1)} %collective-permute-done.6.refs_1_, bf16[16,4096]{1,0:T(8,128)(2,1)S(1)} %collective-permute-done.7.refs_2_, ...), custom_call_target="tpu_custom_call" | custom-call | tf_op jit(solution)/shard_map/pallas_call | solution.py:85
  27.3 0.0 collective-permute-done.5.refs_1_
  27.3 1.0 %collective-permute-done.3.refs_0_ = bf16[16,4096]{1,0:T(8,128)(2,1)S(1)} collective-permute-done((bf16[16,4096]{1,0:T(8,128)(2,1)S(1)}, bf16[16,4096]{1,0:T(8,128)(2,1)S(1)}, u32[]{:S(2)}, u32[]{:S(2)}) %collective-permute-start.3) | collective-permute-done | bytes 131104 | tf_op jit(solution)/shard_map/ppermute | solution.py:22
  28.3 0.8 shard_map.86._.refs_0_.coarse_ref
  29.1 2.6 %collective-permute-start.11 = (bf16[128,512]{1,0:T(8,128)(2,1)S(1)}, bf16[128,512]{1,0:T(8,128)(2,1)S(1)}, u32[]{:S(2)}, u32[]{:S(2)}) collective-permute-start(bf16[128,512]{1,0:T(8,128)(2,1)S(1)} %shard_map.86._.refs_0_.coarse_ref), channel_id=1, source_target_pairs={{0,12},{2,14},{4,8},{6,10},{8,4},{10,6},{12,0},{14,2},{1,13},{3,15... | collective-permute-start | bytes 393224 | tf_op jit(solution)/shard_map/ppermute | solution.py:22
  31.7 0.8 collective-permute-start.9
  32.5 1.7 %collective-permute-start.13 = (bf16[128,512]{1,0:T(8,128)(2,1)S(1)}, bf16[128,512]{1,0:T(8,128)(2,1)S(1)}, u32[]{:S(2)}, u32[]{:S(2)}) collective-permute-start(bf16[128,512]{1,0:T(8,128)(2,1)S(1)} %shard_map.86._.refs_0_.coarse_ref), channel_id=1, source_target_pairs={{0,2},{2,0},{4,6},{6,4},{8,10},{10,8},{12,14},{14,12},{1,3},{3,1},... | collective-permute-start | bytes 393224 | tf_op jit(solution)/shard_map/ppermute | solution.py:22
  34.3 1.0 %collective-permute-start.14 = (bf16[128,512]{1,0:T(8,128)(2,1)S(1)}, bf16[128,512]{1,0:T(8,128)(2,1)S(1)}, u32[]{:S(2)}, u32[]{:S(2)}) collective-permute-start(bf16[128,512]{1,0:T(8,128)(2,1)S(1)} %shard_map.86._.refs_0_.coarse_ref), channel_id=1, source_target_pairs={{0,4},{2,6},{4,0},{6,2},{8,12},{10,14},{12,8},{14,10},{1,5},{3,7},... | collective-permute-start | bytes 393224 | tf_op jit(solution)/shard_map/ppermute | solution.py:22
  35.3 0.7 collective-permute-start.15
  36.0 3.3 %shard_map.87.refs_8_.refs_3_ = bf16[5,3,512,512]{3,2,1,0:T(8,128)(2,1)S(1)} custom-call(bf16[3,4096,512]{2,1,0:T(8,128)(2,1)} %refs_7_.3, bf16[128,512]{1,0:T(8,128)(2,1)S(1)} %shard_map.86._.refs_0_.coarse_ref), custom_call_target="tpu_custom_call" | custom-call | tf_op jit(solution)/shard_map/pallas_call | solution.py:85
  39.3 0.0 collective-permute-done.11.refs_5_
  39.4 1.8 %collective-permute-start.12 = (bf16[128,512]{1,0:T(8,128)(2,1)S(1)}, bf16[128,512]{1,0:T(8,128)(2,1)S(1)}, u32[]{:S(2)}, u32[]{:S(2)}) collective-permute-start(bf16[128,512]{1,0:T(8,128)(2,1)S(1)} %collective-permute-done.11.refs_5_), channel_id=1, source_target_pairs={{0,2},{2,0},{4,6},{6,4},{8,10},{10,8},{12,14},{14,12},{1,3},{3,1},... | collective-permute-start | bytes 393224 | tf_op jit(solution)/shard_map/ppermute | solution.py:22
  41.2 3.0 %collective-permute-done.9.refs_4_ = bf16[128,512]{1,0:T(8,128)(2,1)S(1)} collective-permute-done((bf16[128,512]{1,0:T(8,128)(2,1)S(1)}, bf16[128,512]{1,0:T(8,128)(2,1)S(1)}, u32[]{:S(2)}, u32[]{:S(2)}) %collective-permute-start.9) | collective-permute-done | bytes 131104 | tf_op jit(solution)/shard_map/ppermute | solution.py:22
  44.1 1.4 %collective-permute-start.10 = (bf16[128,512]{1,0:T(8,128)(2,1)S(1)}, bf16[128,512]{1,0:T(8,128)(2,1)S(1)}, u32[]{:S(2)}, u32[]{:S(2)}) collective-permute-start(bf16[128,512]{1,0:T(8,128)(2,1)S(1)} %collective-permute-done.9.refs_4_), channel_id=1, source_target_pairs={{0,2},{2,0},{4,6},{6,4},{8,10},{10,8},{12,14},{14,12},{1,3},{3,1},... | collective-permute-start | bytes 393224 | tf_op jit(solution)/shard_map/ppermute | solution.py:22
  45.5 0.0 collective-permute-done.13.refs_1_
  45.6 3.3 %shard_map.88 = (f32[3,128,512]{2,1,0:T(8,128)S(1)}, f32[128,128]{1,0:T(8,128)S(1)}) custom-call(bf16[128,512]{1,0:T(8,128)(2,1)S(1)} %shard_map.86._.refs_0_.coarse_ref, bf16[128,512]{1,0:T(8,128)(2,1)S(1)} %collective-permute-done.13.refs_1_, bf16[128,512]{1,0:T(8,128)(2,1)S(1)} %collective-permute-done.14.refs_2_, ...), custom_call_target="tpu_custom_call" | custom-call | tf_op jit(solution)/shard_map/pallas_call | solution.py:85
  48.9 0.6 collective-permute-done.10.refs_0_
  49.5 0.6 shard_map.89
  50.1 0.1 collective-permute-start.16
  50.2 1.5 %collective-permute-done.16.other_ref = bf16[2,128,512]{2,1,0:T(8,128)(2,1)S(1)} collective-permute-done((bf16[2,128,512]{2,1,0:T(8,128)(2,1)S(1)}, bf16[2,128,512]{2,1,0:T(8,128)(2,1)S(1)}, u32[]{:S(2)}, u32[]{:S(2)}) %collective-permute-start.16) | collective-permute-done | bytes 262176 | tf_op jit(solution)/shard_map/ppermute | solution.py:22
  51.7 1.8 %shard_map.90 = (bf16[128,512]{1,0:T(8,128)(2,1)S(1)}, bf16[128,512]{1,0:T(8,128)(2,1)S(1)}, bf16[128,512]{1,0:T(8,128)(2,1)S(1)}) custom-call(bf16[128,512]{1,0:T(8,128)(2,1)S(1)} %get-tuple-element.49.q_ref, bf16[2,128,512]{2,1,0:T(8,128)(2,1)S(1)} %get-tuple-element.50.own_ref, bf16[2,128,512]{2,1,0:T(8,128)(2,1)S(1)} %collective-permute-done.16.other_ref, ...), custom_call_target="tpu_custom_call" | custom-call | tf_op jit(solution)/shard_map/pallas_call | solution.py:85
  53.5 1.5 %collective-permute-start.19 = (bf16[128,512]{1,0:T(8,128)(2,1)S(1)}, bf16[128,512]{1,0:T(8,128)(2,1)S(1)}, u32[]{:S(2)}, u32[]{:S(2)}) collective-permute-start(bf16[128,512]{1,0:T(8,128)(2,1)S(1)} %get-tuple-element.56), channel_id=1, source_target_pairs={{0,2},{2,0},{4,6},{6,4},{8,10},{10,8},{12,14},{14,12},{1,3},{3,1},... | collective-permute-start | bytes 393224 | tf_op jit(solution)/shard_map/ppermute | solution.py:22
  55.0 0.6 shard_map.91
  55.6 0.7 collective-permute-start.17
  56.2 2.1 %collective-permute-start.21 = (bf16[128,512]{1,0:T(8,128)(2,1)S(1)}, bf16[128,512]{1,0:T(8,128)(2,1)S(1)}, u32[]{:S(2)}, u32[]{:S(2)}) collective-permute-start(bf16[128,512]{1,0:T(8,128)(2,1)S(1)} %get-tuple-element.57), channel_id=1, source_target_pairs={{0,6},{2,4},{4,2},{6,0},{8,14},{10,12},{12,10},{14,8},{1,7},{3,5},... | collective-permute-start | bytes 393224 | tf_op jit(solution)/shard_map/ppermute | solution.py:22
  58.3 0.8 collective-permute-start.22
  59.1 0.6 collective-permute-start.23
  59.7 2.3 %collective-permute-done.19 = bf16[128,512]{1,0:T(8,128)(2,1)S(1)} collective-permute-done((bf16[128,512]{1,0:T(8,128)(2,1)S(1)}, bf16[128,512]{1,0:T(8,128)(2,1)S(1)}, u32[]{:S(2)}, u32[]{:S(2)}) %collective-permute-start.19) | collective-permute-done | bytes 131104 | tf_op jit(solution)/shard_map/ppermute | solution.py:22
  62.1 1.5 %collective-permute-start.20 = (bf16[128,512]{1,0:T(8,128)(2,1)S(1)}, bf16[128,512]{1,0:T(8,128)(2,1)S(1)}, u32[]{:S(2)}, u32[]{:S(2)}) collective-permute-start(bf16[128,512]{1,0:T(8,128)(2,1)S(1)} %add_convert_fusion.3), channel_id=1, source_target_pairs={{0,8},{2,10},{4,12},{6,14},{8,0},{10,2},{12,4},{14,6},{1,9},{3,11}... | collective-permute-start | bytes 393224 | tf_op jit(solution)/shard_map/ppermute | solution.py:22
  63.6 1.9 %collective-permute-done.17 = bf16[128,512]{1,0:T(8,128)(2,1)S(1)} collective-permute-done((bf16[128,512]{1,0:T(8,128)(2,1)S(1)}, bf16[128,512]{1,0:T(8,128)(2,1)S(1)}, u32[]{:S(2)}, u32[]{:S(2)}) %collective-permute-start.17) | collective-permute-done | bytes 131104 | tf_op jit(solution)/shard_map/ppermute | solution.py:22
  65.5 1.9 %collective-permute-start.18 = (bf16[128,512]{1,0:T(8,128)(2,1)S(1)}, bf16[128,512]{1,0:T(8,128)(2,1)S(1)}, u32[]{:S(2)}, u32[]{:S(2)}) collective-permute-start(bf16[128,512]{1,0:T(8,128)(2,1)S(1)} %add_convert_fusion.4), channel_id=1, source_target_pairs={{0,12},{2,14},{4,8},{6,10},{8,4},{10,6},{12,0},{14,2},{1,13},{3,15... | collective-permute-start | bytes 393224 | tf_op jit(solution)/shard_map/ppermute | solution.py:22
  67.5 0.0 collective-permute-done.23.refs_4_
  67.5 5.0 %collective-permute-done.20.refs_1_ = bf16[128,512]{1,0:T(8,128)(2,1)S(1)} collective-permute-done((bf16[128,512]{1,0:T(8,128)(2,1)S(1)}, bf16[128,512]{1,0:T(8,128)(2,1)S(1)}, u32[]{:S(2)}, u32[]{:S(2)}) %collective-permute-start.20) | collective-permute-done | bytes 131104 | tf_op jit(solution)/shard_map/ppermute | solution.py:22
  72.5 0.8 shard_map.92
  73.3 1.8 %collective-permute-start.24 = (bf16[16,4096]{1,0:T(8,128)(2,1)S(1)}, bf16[16,4096]{1,0:T(8,128)(2,1)S(1)}, u32[]{:S(2)}, u32[]{:S(2)}) collective-permute-start(bf16[16,4096]{1,0:T(8,128)(2,1)S(1)} %get-tuple-element.63), channel_id=1, source_target_pairs={{0,2},{2,0},{4,6},{6,4},{8,10},{10,8},{12,14},{14,12},{1,3},{3,1},... | collective-permute-start | bytes 393224 | tf_op jit(solution)/shard_map/ppermute | solution.py:22
  75.1 0.3 collective-permute-start.26
  75.4 3.8 %collective-permute-start.28 = (bf16[16,4096]{1,0:T(8,128)(2,1)S(1)}, bf16[16,4096]{1,0:T(8,128)(2,1)S(1)}, u32[]{:S(2)}, u32[]{:S(2)}) collective-permute-start(bf16[16,4096]{1,0:T(8,128)(2,1)S(1)} %get-tuple-element.66), channel_id=1, source_target_pairs={{0,6},{2,4},{4,2},{6,0},{8,14},{10,12},{12,10},{14,8},{1,7},{3,5},... | collective-permute-start | bytes 393224 | tf_op jit(solution)/shard_map/ppermute | solution.py:22
  79.2 0.8 collective-permute-start.30
  80.1 3.0 %collective-permute-start.25 = (bf16[16,4096]{1,0:T(8,128)(2,1)S(1)}, bf16[16,4096]{1,0:T(8,128)(2,1)S(1)}, u32[]{:S(2)}, u32[]{:S(2)}) collective-permute-start(bf16[16,4096]{1,0:T(8,128)(2,1)S(1)} %add_convert_fusion.2), channel_id=1, source_target_pairs={{0,12},{2,14},{4,8},{6,10},{8,4},{10,6},{12,0},{14,2},{1,13},{3,15... | collective-permute-start | bytes 393224 | tf_op jit(solution)/shard_map/ppermute | solution.py:22
  83.1 0.9 collective-permute-done.26
  84.0 4.9 %collective-permute-start.27 = (bf16[16,4096]{1,0:T(8,128)(2,1)S(1)}, bf16[16,4096]{1,0:T(8,128)(2,1)S(1)}, u32[]{:S(2)}, u32[]{:S(2)}) collective-permute-start(bf16[16,4096]{1,0:T(8,128)(2,1)S(1)} %add_convert_fusion.1), channel_id=1, source_target_pairs={{0,8},{2,10},{4,12},{6,14},{8,0},{10,2},{12,4},{14,6},{1,9},{3,11}... | collective-permute-start | bytes 393224 | tf_op jit(solution)/shard_map/ppermute | solution.py:22
  88.9 5.6 %collective-permute-done.27 = bf16[16,4096]{1,0:T(8,128)(2,1)S(1)} collective-permute-done((bf16[16,4096]{1,0:T(8,128)(2,1)S(1)}, bf16[16,4096]{1,0:T(8,128)(2,1)S(1)}, u32[]{:S(2)}, u32[]{:S(2)}) %collective-permute-start.27) | collective-permute-done | bytes 131104 | tf_op jit(solution)/shard_map/ppermute | solution.py:22
  94.5 0.1 convert_add_fusion
  94.6 0.1 reshape.15
  94.7 0.7 add_convert_fusion
  (23 shorter events, 0.2 us)
Async XLA Ops:
  0.8 6.1 %collective-permute-start = (bf16[2,1024]{1,0:T(2,128)(2,1)S(1)}, bf16[2,1024]{1,0:T(2,128)(2,1)S(1)}, u32[]{:S(2)}, u32[]{:S(2)}) collective-permute-start(bf16[2,1024]{1,0:T(2,128)(2,1)S(1)} %get-tuple-element.70), channel_id=1, source_target_pairs={{1,2},{2,1},{3,4},{4,3},{5,6},{6,5},{7,8},{8,7},{9,10},{10,9},{11,... | collective-permute-start | bytes 12296 | tf_op jit(solution)/shard_map/ppermute | solution.py:356
  1.4 5.5 %collective-permute-start.1 = (bf16[2,1024]{1,0:T(2,128)(2,1)S(1)}, bf16[2,1024]{1,0:T(2,128)(2,1)S(1)}, u32[]{:S(2)}, u32[]{:S(2)}) collective-permute-start(bf16[2,1024]{1,0:T(2,128)(2,1)S(1)} %get-tuple-element.69), channel_id=1, source_target_pairs={{0,1},{1,0},{2,3},{3,2},{4,5},{5,4},{6,7},{7,6},{8,9},{9,8},{10,11... | collective-permute-start | bytes 12296 | tf_op jit(solution)/shard_map/ppermute | solution.py:355
  7.3 11.8 %collective-permute-start.4 = (bf16[16,4096]{1,0:T(8,128)(2,1)S(1)}, bf16[16,4096]{1,0:T(8,128)(2,1)S(1)}, u32[]{:S(2)}, u32[]{:S(2)}) collective-permute-start(bf16[16,4096]{1,0:T(8,128)(2,1)S(1)} %reshape.13.refs_2_.refs_0_), channel_id=1, source_target_pairs={{0,12},{2,14},{4,8},{6,10},{8,4},{10,6},{12,0},{14,2},{1,13},{3,15... | collective-permute-start | bytes 393224 | tf_op jit(solution)/shard_map/ppermute | solution.py:22
  12.1 10.3 %collective-permute-start.2 = (bf16[16,4096]{1,0:T(8,128)(2,1)S(1)}, bf16[16,4096]{1,0:T(8,128)(2,1)S(1)}, u32[]{:S(2)}, u32[]{:S(2)}) collective-permute-start(bf16[16,4096]{1,0:T(8,128)(2,1)S(1)} %reshape.13.refs_2_.refs_0_), channel_id=1, source_target_pairs={{0,8},{2,10},{4,12},{6,14},{8,0},{10,2},{12,4},{14,6},{1,9},{3,11}... | collective-permute-start | bytes 393224 | tf_op jit(solution)/shard_map/ppermute | solution.py:22
  12.1 12.7 %collective-permute-start.6 = (bf16[16,4096]{1,0:T(8,128)(2,1)S(1)}, bf16[16,4096]{1,0:T(8,128)(2,1)S(1)}, u32[]{:S(2)}, u32[]{:S(2)}) collective-permute-start(bf16[16,4096]{1,0:T(8,128)(2,1)S(1)} %reshape.13.refs_2_.refs_0_), channel_id=1, source_target_pairs={{0,2},{2,0},{4,6},{6,4},{8,10},{10,8},{12,14},{14,12},{1,3},{3,1},... | collective-permute-start | bytes 393224 | tf_op jit(solution)/shard_map/ppermute | solution.py:22
  12.7 12.1 %collective-permute-start.7 = (bf16[16,4096]{1,0:T(8,128)(2,1)S(1)}, bf16[16,4096]{1,0:T(8,128)(2,1)S(1)}, u32[]{:S(2)}, u32[]{:S(2)}) collective-permute-start(bf16[16,4096]{1,0:T(8,128)(2,1)S(1)} %reshape.13.refs_2_.refs_0_), channel_id=1, source_target_pairs={{0,4},{2,6},{4,0},{6,2},{8,12},{10,14},{12,8},{14,10},{1,5},{3,7},... | collective-permute-start | bytes 393224 | tf_op jit(solution)/shard_map/ppermute | solution.py:22
  13.5 11.6 %collective-permute-start.8 = (bf16[16,4096]{1,0:T(8,128)(2,1)S(1)}, bf16[16,4096]{1,0:T(8,128)(2,1)S(1)}, u32[]{:S(2)}, u32[]{:S(2)}) collective-permute-start(bf16[16,4096]{1,0:T(8,128)(2,1)S(1)} %reshape.13.refs_2_.refs_0_), channel_id=1, source_target_pairs={{0,6},{2,4},{4,2},{6,0},{8,14},{10,12},{12,10},{14,8},{1,7},{3,5},... | collective-permute-start | bytes 393224 | tf_op jit(solution)/shard_map/ppermute | solution.py:22
  19.1 8.2 %collective-permute-start.5 = (bf16[16,4096]{1,0:T(8,128)(2,1)S(1)}, bf16[16,4096]{1,0:T(8,128)(2,1)S(1)}, u32[]{:S(2)}, u32[]{:S(2)}) collective-permute-start(bf16[16,4096]{1,0:T(8,128)(2,1)S(1)} %collective-permute-done.4.refs_5_), channel_id=1, source_target_pairs={{0,2},{2,0},{4,6},{6,4},{8,10},{10,8},{12,14},{14,12},{1,3},{3,1},... | collective-permute-start | bytes 393224 | tf_op jit(solution)/shard_map/ppermute | solution.py:22
  22.5 5.8 %collective-permute-start.3 = (bf16[16,4096]{1,0:T(8,128)(2,1)S(1)}, bf16[16,4096]{1,0:T(8,128)(2,1)S(1)}, u32[]{:S(2)}, u32[]{:S(2)}) collective-permute-start(bf16[16,4096]{1,0:T(8,128)(2,1)S(1)} %collective-permute-done.2.refs_4_), channel_id=1, source_target_pairs={{0,2},{2,0},{4,6},{6,4},{8,10},{10,8},{12,14},{14,12},{1,3},{3,1},... | collective-permute-start | bytes 393224 | tf_op jit(solution)/shard_map/ppermute | solution.py:22
  29.1 16.5 %copy-start = (f32[4096]{0:T(1024)S(1)}, f32[4096]{0:T(1024)}, u32[]{:S(2)}) copy-start(f32[4096]{0:T(1024)} %param.12) | copy-start | bytes 49156
  29.1 10.2 %collective-permute-start.11 = (bf16[128,512]{1,0:T(8,128)(2,1)S(1)}, bf16[128,512]{1,0:T(8,128)(2,1)S(1)}, u32[]{:S(2)}, u32[]{:S(2)}) collective-permute-start(bf16[128,512]{1,0:T(8,128)(2,1)S(1)} %shard_map.86._.refs_0_.coarse_ref), channel_id=1, source_target_pairs={{0,12},{2,14},{4,8},{6,10},{8,4},{10,6},{12,0},{14,2},{1,13},{3,15... | collective-permute-start | bytes 393224 | tf_op jit(solution)/shard_map/ppermute | solution.py:22
  31.7 12.4 %collective-permute-start.9 = (bf16[128,512]{1,0:T(8,128)(2,1)S(1)}, bf16[128,512]{1,0:T(8,128)(2,1)S(1)}, u32[]{:S(2)}, u32[]{:S(2)}) collective-permute-start(bf16[128,512]{1,0:T(8,128)(2,1)S(1)} %shard_map.86._.refs_0_.coarse_ref), channel_id=1, source_target_pairs={{0,8},{2,10},{4,12},{6,14},{8,0},{10,2},{12,4},{14,6},{1,9},{3,11}... | collective-permute-start | bytes 393224 | tf_op jit(solution)/shard_map/ppermute | solution.py:22
  32.5 13.0 %collective-permute-start.13 = (bf16[128,512]{1,0:T(8,128)(2,1)S(1)}, bf16[128,512]{1,0:T(8,128)(2,1)S(1)}, u32[]{:S(2)}, u32[]{:S(2)}) collective-permute-start(bf16[128,512]{1,0:T(8,128)(2,1)S(1)} %shard_map.86._.refs_0_.coarse_ref), channel_id=1, source_target_pairs={{0,2},{2,0},{4,6},{6,4},{8,10},{10,8},{12,14},{14,12},{1,3},{3,1},... | collective-permute-start | bytes 393224 | tf_op jit(solution)/shard_map/ppermute | solution.py:22
  34.3 11.3 %collective-permute-start.14 = (bf16[128,512]{1,0:T(8,128)(2,1)S(1)}, bf16[128,512]{1,0:T(8,128)(2,1)S(1)}, u32[]{:S(2)}, u32[]{:S(2)}) collective-permute-start(bf16[128,512]{1,0:T(8,128)(2,1)S(1)} %shard_map.86._.refs_0_.coarse_ref), channel_id=1, source_target_pairs={{0,4},{2,6},{4,0},{6,2},{8,12},{10,14},{12,8},{14,10},{1,5},{3,7},... | collective-permute-start | bytes 393224 | tf_op jit(solution)/shard_map/ppermute | solution.py:22
  35.3 10.3 %collective-permute-start.15 = (bf16[128,512]{1,0:T(8,128)(2,1)S(1)}, bf16[128,512]{1,0:T(8,128)(2,1)S(1)}, u32[]{:S(2)}, u32[]{:S(2)}) collective-permute-start(bf16[128,512]{1,0:T(8,128)(2,1)S(1)} %shard_map.86._.refs_0_.coarse_ref), channel_id=1, source_target_pairs={{0,6},{2,4},{4,2},{6,0},{8,14},{10,12},{12,10},{14,8},{1,7},{3,5},... | collective-permute-start | bytes 393224 | tf_op jit(solution)/shard_map/ppermute | solution.py:22
  39.4 9.5 %collective-permute-start.12 = (bf16[128,512]{1,0:T(8,128)(2,1)S(1)}, bf16[128,512]{1,0:T(8,128)(2,1)S(1)}, u32[]{:S(2)}, u32[]{:S(2)}) collective-permute-start(bf16[128,512]{1,0:T(8,128)(2,1)S(1)} %collective-permute-done.11.refs_5_), channel_id=1, source_target_pairs={{0,2},{2,0},{4,6},{6,4},{8,10},{10,8},{12,14},{14,12},{1,3},{3,1},... | collective-permute-start | bytes 393224 | tf_op jit(solution)/shard_map/ppermute | solution.py:22
  44.1 5.4 %collective-permute-start.10 = (bf16[128,512]{1,0:T(8,128)(2,1)S(1)}, bf16[128,512]{1,0:T(8,128)(2,1)S(1)}, u32[]{:S(2)}, u32[]{:S(2)}) collective-permute-start(bf16[128,512]{1,0:T(8,128)(2,1)S(1)} %collective-permute-done.9.refs_4_), channel_id=1, source_target_pairs={{0,2},{2,0},{4,6},{6,4},{8,10},{10,8},{12,14},{14,12},{1,3},{3,1},... | collective-permute-start | bytes 393224 | tf_op jit(solution)/shard_map/ppermute | solution.py:22
  50.1 1.6 %collective-permute-start.16 = (bf16[2,128,512]{2,1,0:T(8,128)(2,1)S(1)}, bf16[2,128,512]{2,1,0:T(8,128)(2,1)S(1)}, u32[]{:S(2)}, u32[]{:S(2)}) collective-permute-start(bf16[2,128,512]{2,1,0:T(8,128)(2,1)S(1)} %get-tuple-element.50.own_ref), channel_id=1, source_target_pairs={{0,1},{1,0},{2,3},{3,2},{4,5},{5,4},{6,7},{7,6},{8,9},{9,8},{10,11... | collective-permute-start | bytes 786440 | tf_op jit(solution)/shard_map/ppermute | solution.py:22
  53.5 8.6 %collective-permute-start.19 = (bf16[128,512]{1,0:T(8,128)(2,1)S(1)}, bf16[128,512]{1,0:T(8,128)(2,1)S(1)}, u32[]{:S(2)}, u32[]{:S(2)}) collective-permute-start(bf16[128,512]{1,0:T(8,128)(2,1)S(1)} %get-tuple-element.56), channel_id=1, source_target_pairs={{0,2},{2,0},{4,6},{6,4},{8,10},{10,8},{12,14},{14,12},{1,3},{3,1},... | collective-permute-start | bytes 393224 | tf_op jit(solution)/shard_map/ppermute | solution.py:22
  55.6 9.9 %collective-permute-start.17 = (bf16[128,512]{1,0:T(8,128)(2,1)S(1)}, bf16[128,512]{1,0:T(8,128)(2,1)S(1)}, u32[]{:S(2)}, u32[]{:S(2)}) collective-permute-start(bf16[128,512]{1,0:T(8,128)(2,1)S(1)} %get-tuple-element.54), channel_id=1, source_target_pairs={{0,2},{2,0},{4,6},{6,4},{8,10},{10,8},{12,14},{14,12},{1,3},{3,1},... | collective-permute-start | bytes 393224 | tf_op jit(solution)/shard_map/ppermute | solution.py:22
  56.2 11.2 %collective-permute-start.21 = (bf16[128,512]{1,0:T(8,128)(2,1)S(1)}, bf16[128,512]{1,0:T(8,128)(2,1)S(1)}, u32[]{:S(2)}, u32[]{:S(2)}) collective-permute-start(bf16[128,512]{1,0:T(8,128)(2,1)S(1)} %get-tuple-element.57), channel_id=1, source_target_pairs={{0,6},{2,4},{4,2},{6,0},{8,14},{10,12},{12,10},{14,8},{1,7},{3,5},... | collective-permute-start | bytes 393224 | tf_op jit(solution)/shard_map/ppermute | solution.py:22
  58.3 9.1 %collective-permute-start.22 = (bf16[128,512]{1,0:T(8,128)(2,1)S(1)}, bf16[128,512]{1,0:T(8,128)(2,1)S(1)}, u32[]{:S(2)}, u32[]{:S(2)}) collective-permute-start(bf16[128,512]{1,0:T(8,128)(2,1)S(1)} %get-tuple-element.58), channel_id=1, source_target_pairs={{0,4},{2,6},{4,0},{6,2},{8,12},{10,14},{12,8},{14,10},{1,5},{3,7},... | collective-permute-start | bytes 393224 | tf_op jit(solution)/shard_map/ppermute | solution.py:22
  59.1 8.4 %collective-permute-start.23 = (bf16[128,512]{1,0:T(8,128)(2,1)S(1)}, bf16[128,512]{1,0:T(8,128)(2,1)S(1)}, u32[]{:S(2)}, u32[]{:S(2)}) collective-permute-start(bf16[128,512]{1,0:T(8,128)(2,1)S(1)} %get-tuple-element.59), channel_id=1, source_target_pairs={{0,2},{2,0},{4,6},{6,4},{8,10},{10,8},{12,14},{14,12},{1,3},{3,1},... | collective-permute-start | bytes 393224 | tf_op jit(solution)/shard_map/ppermute | solution.py:22
  62.1 10.4 %collective-permute-start.20 = (bf16[128,512]{1,0:T(8,128)(2,1)S(1)}, bf16[128,512]{1,0:T(8,128)(2,1)S(1)}, u32[]{:S(2)}, u32[]{:S(2)}) collective-permute-start(bf16[128,512]{1,0:T(8,128)(2,1)S(1)} %add_convert_fusion.3), channel_id=1, source_target_pairs={{0,8},{2,10},{4,12},{6,14},{8,0},{10,2},{12,4},{14,6},{1,9},{3,11}... | collective-permute-start | bytes 393224 | tf_op jit(solution)/shard_map/ppermute | solution.py:22
  65.5 29.2 %copy-start.1 = (bf16[64,1024]{1,0:T(8,128)(2,1)S(1)}, bf16[64,1024]{1,0:T(8,128)(2,1)}, u32[]{:S(2)}) copy-start(bf16[64,1024]{1,0:T(8,128)(2,1)} %frames_ref.1) | copy-start | bytes 393220
  65.5 7.0 %collective-permute-start.18 = (bf16[128,512]{1,0:T(8,128)(2,1)S(1)}, bf16[128,512]{1,0:T(8,128)(2,1)S(1)}, u32[]{:S(2)}, u32[]{:S(2)}) collective-permute-start(bf16[128,512]{1,0:T(8,128)(2,1)S(1)} %add_convert_fusion.4), channel_id=1, source_target_pairs={{0,12},{2,14},{4,8},{6,10},{8,4},{10,6},{12,0},{14,2},{1,13},{3,15... | collective-permute-start | bytes 393224 | tf_op jit(solution)/shard_map/ppermute | solution.py:22
  73.3 6.8 %collective-permute-start.24 = (bf16[16,4096]{1,0:T(8,128)(2,1)S(1)}, bf16[16,4096]{1,0:T(8,128)(2,1)S(1)}, u32[]{:S(2)}, u32[]{:S(2)}) collective-permute-start(bf16[16,4096]{1,0:T(8,128)(2,1)S(1)} %get-tuple-element.63), channel_id=1, source_target_pairs={{0,2},{2,0},{4,6},{6,4},{8,10},{10,8},{12,14},{14,12},{1,3},{3,1},... | collective-permute-start | bytes 393224 | tf_op jit(solution)/shard_map/ppermute | solution.py:22
  75.1 8.9 %collective-permute-start.26 = (bf16[16,4096]{1,0:T(8,128)(2,1)S(1)}, bf16[16,4096]{1,0:T(8,128)(2,1)S(1)}, u32[]{:S(2)}, u32[]{:S(2)}) collective-permute-start(bf16[16,4096]{1,0:T(8,128)(2,1)S(1)} %get-tuple-element.65), channel_id=1, source_target_pairs={{0,2},{2,0},{4,6},{6,4},{8,10},{10,8},{12,14},{14,12},{1,3},{3,1},... | collective-permute-start | bytes 393224 | tf_op jit(solution)/shard_map/ppermute | solution.py:22
  75.4 13.5 %collective-permute-start.28 = (bf16[16,4096]{1,0:T(8,128)(2,1)S(1)}, bf16[16,4096]{1,0:T(8,128)(2,1)S(1)}, u32[]{:S(2)}, u32[]{:S(2)}) collective-permute-start(bf16[16,4096]{1,0:T(8,128)(2,1)S(1)} %get-tuple-element.66), channel_id=1, source_target_pairs={{0,6},{2,4},{4,2},{6,0},{8,14},{10,12},{12,10},{14,8},{1,7},{3,5},... | collective-permute-start | bytes 393224 | tf_op jit(solution)/shard_map/ppermute | solution.py:22
  79.2 9.7 %collective-permute-start.29 = (bf16[16,4096]{1,0:T(8,128)(2,1)S(1)}, bf16[16,4096]{1,0:T(8,128)(2,1)S(1)}, u32[]{:S(2)}, u32[]{:S(2)}) collective-permute-start(bf16[16,4096]{1,0:T(8,128)(2,1)S(1)} %get-tuple-element.67), channel_id=1, source_target_pairs={{0,4},{2,6},{4,0},{6,2},{8,12},{10,14},{12,8},{14,10},{1,5},{3,7},... | collective-permute-start | bytes 393224 | tf_op jit(solution)/shard_map/ppermute | solution.py:22
  79.2 9.7 %collective-permute-start.30 = (bf16[16,4096]{1,0:T(8,128)(2,1)S(1)}, bf16[16,4096]{1,0:T(8,128)(2,1)S(1)}, u32[]{:S(2)}, u32[]{:S(2)}) collective-permute-start(bf16[16,4096]{1,0:T(8,128)(2,1)S(1)} %get-tuple-element.68), channel_id=1, source_target_pairs={{0,2},{2,0},{4,6},{6,4},{8,10},{10,8},{12,14},{14,12},{1,3},{3,1},... | collective-permute-start | bytes 393224 | tf_op jit(solution)/shard_map/ppermute | solution.py:22
  80.1 8.9 %collective-permute-start.25 = (bf16[16,4096]{1,0:T(8,128)(2,1)S(1)}, bf16[16,4096]{1,0:T(8,128)(2,1)S(1)}, u32[]{:S(2)}, u32[]{:S(2)}) collective-permute-start(bf16[16,4096]{1,0:T(8,128)(2,1)S(1)} %add_convert_fusion.2), channel_id=1, source_target_pairs={{0,12},{2,14},{4,8},{6,10},{8,4},{10,6},{12,0},{14,2},{1,13},{3,15... | collective-permute-start | bytes 393224 | tf_op jit(solution)/shard_map/ppermute | solution.py:22
  84.0 10.5 %collective-permute-start.27 = (bf16[16,4096]{1,0:T(8,128)(2,1)S(1)}, bf16[16,4096]{1,0:T(8,128)(2,1)S(1)}, u32[]{:S(2)}, u32[]{:S(2)}) collective-permute-start(bf16[16,4096]{1,0:T(8,128)(2,1)S(1)} %add_convert_fusion.1), channel_id=1, source_target_pairs={{0,8},{2,10},{4,12},{6,14},{8,0},{10,2},{12,4},{14,6},{1,9},{3,11}... | collective-permute-start | bytes 393224 | tf_op jit(solution)/shard_map/ppermute | solution.py:22

commit v4 on v3

--- a/solution.py
+++ b/solution.py
@@ -40,9 +40,10 @@
     for mask in far_first(size):
         if not relayed(mask, size):
             arrays[mask] = flip(value, axis, mask)
-    for mask in far_first(size):
-        if relayed(mask, size):
-            arrays[mask] = flip(after_all((arrays[mask ^ 1],), fetched)[0], axis, 1)
+    near = [arrays[m] for m in range(1, size) if arrays[m] is not None and m == 3]
+    for n, mask in enumerate(m for m in far_first(size) if relayed(m, size)):
+        ready = (*fetched, *near) if n else fetched
+        arrays[mask] = flip(after_all((arrays[mask ^ 1],), ready)[0], axis, 1)
     return arrays, {mask: [(mask, 0, rows)] for mask in range(size)}
 
 
@@ -69,12 +70,17 @@
     def plus(part, *others):
         return sum([o.astype(jnp.float32) for o in others], part).astype(jnp.bfloat16)
 
-    arrived = []
     passed = {m ^ 1: flip(parts[m], axis, 1) for m in far_first(size) if relayed(m, size)}
+    beside = flip(parts[2], axis, 2)
+    arrived = [(beside, 0, 0, rows)]
     for mask in far_first(size):
-        if not relayed(mask, size):
-            part = plus(parts[mask], passed[mask]) if mask in passed else parts[mask]
-            arrived.append((flip(part, axis, mask), 0, 0, rows))
+        if mask in passed:
+            part = plus(parts[mask], passed[mask])
+        elif mask == 2 or relayed(mask, size):
+            continue
+        else:
+            part = after_all((parts[mask],), (beside, *passed.values()))[0]
+        arrived.append((flip(part, axis, mask), 0, 0, rows))
     return arrived
 
 
@@ -484,7 +490,7 @@
     )
     names = [name for name, _, _ in first_plan + second_plan]
     parts = dict(zip(names, [*first, *second]))
-    arrived = scatter_flips(parts, "seq")
+    arrived = scatter_flips(parts, "seq")[::-1]
     first_plan, second_plan = scatter_plan(size, own_tokens)
     lifted = call(
         functools.partial(

time: 95.8 us -> 89.6 us (0.935)
  starting transfers between devices: 50.4 us -> 42 us
  waiting for transfers between devices: 24.7 us -> 27 us
    ppermute x29, starting transfers between devices: 45.3 us -> 36.9 us  [flip(): return lax.ppermute(value, axis, pairs)]
    ppermute x29, waiting for transfers between devices: 24.7 us -> 27 us  [flip(): return lax.ppermute(value, axis, pairs)]
  transfers between devices with their start and end apart: 31 -> 31, of which waited for: 11 -> 14; matrix products, arithmetic and copies ran while one was open for 0% -> 0% of each run, Pallas kernels for 15% -> 16%
where the time goes in v4:
time: 89.6 us; the launch traced here: 89.3 us
  starting transfers between devices  42 us (47%)
  waiting for transfers between devices  27 us (30%)
  Pallas kernels  18.2 us (20%)
  other arithmetic  1.65 us (2%)
    ppermute x29, starting transfers between devices, flip(): return lax.ppermute(value, axis, pairs)  36.9 us
    ppermute x29, waiting for transfers between devices, flip(): return lax.ppermute(value, axis, pairs)  27 us
    pallas_call x11, Pallas kernels, call(): pl.pallas_call(body, out_shape=outs, in_specs=specs, out_specs=jax.tree.m...  18.2 us
    ppermute x1, starting transfers between devices, edge_rows(): near = lax.ppermute(jnp.where(even, last, first), ('seq', 'sub'), inside)  4.39 us
  transfers between devices with their start and end apart: 31, of which 14 were waited for; matrix products, arithmetic and copies ran while one was open for 0% of the time, Pallas kernels for 16%

profile of v4, /device:TPU:0, one launch (start us, length us, event | category | flops | bytes accessed | tf_op | source)
XLA Modules:
  0.0 89.3 jit_solution(9841093216923366505)
XLA Ops:
  0.0 0.7 broadcast_select_fusion.2
  0.8 0.7 collective-permute-start
  1.4 4.4 %collective-permute-start.1 = (bf16[2,1024]{1,0:T(2,128)(2,1)S(1)}, bf16[2,1024]{1,0:T(2,128)(2,1)S(1)}, u32[]{:S(2)}, u32[]{:S(2)}) collective-permute-start(bf16[2,1024]{1,0:T(2,128)(2,1)S(1)} %get-tuple-element.77), channel_id=1, source_target_pairs={{0,1},{1,0},{2,3},{3,2},{4,5},{5,4},{6,7},{7,6},{8,9},{9,8},{10,11... | collective-permute-start | bytes 12296 | tf_op jit(solution)/shard_map/ppermute | solution.py:361
  5.8 1.1 %shard_map.82 = (f32[64,1024]{1,0:T(8,128)S(1)}, f32[1,1024]{1,0:T(1,128)S(1)}, f32[5,1024]{1,0:T(8,128)S(1)}) custom-call(bf16[64,1024]{1,0:T(8,128)(2,1)} %frames_ref.1, f32[1,1024]{1,0:T(1,128)} %bitcast.4, bf16[5,1024]{1,0:T(8,128)(2,1)} %taps_ref.1), custom_call_target="tpu_custom_call" | custom-call | tf_op jit(solution)/shard_map/pallas_call | solution.py:91
  6.9 0.0 collective-permute-done
  6.9 0.3 shard_map.83
  7.2 0.1 reshape.13.refs_2_.refs_0_
  7.3 3.8 %collective-permute-start.2 = (bf16[16,4096]{1,0:T(8,128)(2,1)S(1)}, bf16[16,4096]{1,0:T(8,128)(2,1)S(1)}, u32[]{:S(2)}, u32[]{:S(2)}) collective-permute-start(bf16[16,4096]{1,0:T(8,128)(2,1)S(1)} %reshape.13.refs_2_.refs_0_), channel_id=1, source_target_pairs={{0,8},{2,10},{4,12},{6,14},{8,0},{10,2},{12,4},{14,6},{1,9},{3,11}... | collective-permute-start | bytes 393224 | tf_op jit(solution)/shard_map/ppermute | solution.py:22
  11.1 1.6 %collective-permute-start.3 = (bf16[16,4096]{1,0:T(8,128)(2,1)S(1)}, bf16[16,4096]{1,0:T(8,128)(2,1)S(1)}, u32[]{:S(2)}, u32[]{:S(2)}) collective-permute-start(bf16[16,4096]{1,0:T(8,128)(2,1)S(1)} %reshape.13.refs_2_.refs_0_), channel_id=1, source_target_pairs={{0,6},{2,4},{4,2},{6,0},{8,14},{10,12},{12,10},{14,8},{1,7},{3,5},... | collective-permute-start | bytes 393224 | tf_op jit(solution)/shard_map/ppermute | solution.py:22
  12.7 0.2 collective-permute-start.5
  13.0 1.2 %collective-permute-start.7 = (bf16[16,4096]{1,0:T(8,128)(2,1)S(1)}, bf16[16,4096]{1,0:T(8,128)(2,1)S(1)}, u32[]{:S(2)}, u32[]{:S(2)}) collective-permute-start(bf16[16,4096]{1,0:T(8,128)(2,1)S(1)} %reshape.13.refs_2_.refs_0_), channel_id=1, source_target_pairs={{0,2},{2,0},{4,6},{6,4},{8,10},{10,8},{12,14},{14,12},{1,3},{3,1},... | collective-permute-start | bytes 393224 | tf_op jit(solution)/shard_map/ppermute | solution.py:22
  14.2 0.9 %collective-permute-start.8 = (bf16[16,4096]{1,0:T(8,128)(2,1)S(1)}, bf16[16,4096]{1,0:T(8,128)(2,1)S(1)}, u32[]{:S(2)}, u32[]{:S(2)}) collective-permute-start(bf16[16,4096]{1,0:T(8,128)(2,1)S(1)} %reshape.13.refs_2_.refs_0_), channel_id=1, source_target_pairs={{0,4},{2,6},{4,0},{6,2},{8,12},{10,14},{12,8},{14,10},{1,5},{3,7},... | collective-permute-start | bytes 393224 | tf_op jit(solution)/shard_map/ppermute | solution.py:22
  15.0 3.5 %shard_map.84 = (bf16[4096,512]{1,0:T(8,128)(2,1)S(1)}, bf16[512,4096]{1,0:T(8,128)(2,1)S(1)}) custom-call(bf16[4096,512]{1,0:T(8,128)(2,1)} %refs_0_.1, bf16[512,4096]{1,0:T(8,128)(2,1)} %refs_1_.1, bf16[16,4096]{1,0:T(8,128)(2,1)S(1)} %reshape.13.refs_2_.refs_0_), custom_call_target="tpu_custom_call" | custom-call | tf_op jit(solution)/shard_map/pallas_call | solution.py:91
  18.5 0.5 collective-permute-done.3.refs_3_
  19.0 2.4 %collective-permute-start.4 = (bf16[16,4096]{1,0:T(8,128)(2,1)S(1)}, bf16[16,4096]{1,0:T(8,128)(2,1)S(1)}, u32[]{:S(2)}, u32[]{:S(2)}) collective-permute-start(bf16[16,4096]{1,0:T(8,128)(2,1)S(1)} %collective-permute-done.2.refs_4_), channel_id=1, source_target_pairs={{0,2},{2,0},{4,6},{6,4},{8,10},{10,8},{12,14},{14,12},{1,3},{3,1},... | collective-permute-start | bytes 393224 | tf_op jit(solution)/shard_map/ppermute | solution.py:22
  21.5 0.9 %collective-permute-done.5.refs_5_ = bf16[16,4096]{1,0:T(8,128)(2,1)S(1)} collective-permute-done((bf16[16,4096]{1,0:T(8,128)(2,1)S(1)}, bf16[16,4096]{1,0:T(8,128)(2,1)S(1)}, u32[]{:S(2)}, u32[]{:S(2)}) %collective-permute-start.5) | collective-permute-done | bytes 131104 | tf_op jit(solution)/shard_map/ppermute | solution.py:22
  22.4 0.8 collective-permute-start.6
  23.2 0.0 collective-permute-done.7.refs_1_
  23.2 0.6 collective-permute-done.8.refs_2_
  23.8 2.2 %shard_map.85 = (bf16[128,512]{1,0:T(8,128)(2,1)S(1)}, bf16[512,4096]{1,0:T(8,128)(2,1)S(1)}) custom-call(bf16[16,4096]{1,0:T(8,128)(2,1)S(1)} %reshape.13.refs_2_.refs_0_, bf16[16,4096]{1,0:T(8,128)(2,1)S(1)} %collective-permute-done.7.refs_1_, bf16[16,4096]{1,0:T(8,128)(2,1)S(1)} %collective-permute-done.8.refs_2_, ...), custom_call_target="tpu_custom_call" | custom-call | tf_op jit(solution)/shard_map/pallas_call | solution.py:91
  26.0 1.4 %collective-permute-done.6.refs_1_ = bf16[16,4096]{1,0:T(8,128)(2,1)S(1)} collective-permute-done((bf16[16,4096]{1,0:T(8,128)(2,1)S(1)}, bf16[16,4096]{1,0:T(8,128)(2,1)S(1)}, u32[]{:S(2)}, u32[]{:S(2)}) %collective-permute-start.6) | collective-permute-done | bytes 131104 | tf_op jit(solution)/shard_map/ppermute | solution.py:22
  27.4 0.8 shard_map.86._.refs_0_.coarse_ref
  28.2 3.0 %collective-permute-start.12 = (bf16[128,512]{1,0:T(8,128)(2,1)S(1)}, bf16[128,512]{1,0:T(8,128)(2,1)S(1)}, u32[]{:S(2)}, u32[]{:S(2)}) collective-permute-start(bf16[128,512]{1,0:T(8,128)(2,1)S(1)} %shard_map.86._.refs_0_.coarse_ref), channel_id=1, source_target_pairs={{0,12},{2,14},{4,8},{6,10},{8,4},{10,6},{12,0},{14,2},{1,13},{3,15... | collective-permute-start | bytes 393224 | tf_op jit(solution)/shard_map/ppermute | solution.py:22
  31.2 0.1 collective-permute-start.10
  31.3 2.6 %collective-permute-start.9 = (bf16[128,512]{1,0:T(8,128)(2,1)S(1)}, bf16[128,512]{1,0:T(8,128)(2,1)S(1)}, u32[]{:S(2)}, u32[]{:S(2)}) collective-permute-start(bf16[128,512]{1,0:T(8,128)(2,1)S(1)} %shard_map.86._.refs_0_.coarse_ref), channel_id=1, source_target_pairs={{0,8},{2,10},{4,12},{6,14},{8,0},{10,2},{12,4},{14,6},{1,9},{3,11}... | collective-permute-start | bytes 393224 | tf_op jit(solution)/shard_map/ppermute | solution.py:22
  33.9 0.2 collective-permute-start.14
  34.1 0.6 collective-permute-start.15
  34.7 3.3 %shard_map.87.refs_8_.refs_3_ = bf16[5,3,512,512]{3,2,1,0:T(8,128)(2,1)S(1)} custom-call(bf16[3,4096,512]{2,1,0:T(8,128)(2,1)} %refs_7_.3, bf16[128,512]{1,0:T(8,128)(2,1)S(1)} %shard_map.86._.refs_0_.coarse_ref), custom_call_target="tpu_custom_call" | custom-call | tf_op jit(solution)/shard_map/pallas_call | solution.py:91
  38.0 0.0 collective-permute-done.12.refs_5_
  38.0 1.8 %collective-permute-start.13 = (bf16[128,512]{1,0:T(8,128)(2,1)S(1)}, bf16[128,512]{1,0:T(8,128)(2,1)S(1)}, u32[]{:S(2)}, u32[]{:S(2)}) collective-permute-start(bf16[128,512]{1,0:T(8,128)(2,1)S(1)} %collective-permute-done.12.refs_5_), channel_id=1, source_target_pairs={{0,2},{2,0},{4,6},{6,4},{8,10},{10,8},{12,14},{14,12},{1,3},{3,1},... | collective-permute-start | bytes 393224 | tf_op jit(solution)/shard_map/ppermute | solution.py:22
  39.8 1.7 %collective-permute-done.10.refs_3_ = bf16[128,512]{1,0:T(8,128)(2,1)S(1)} collective-permute-done((bf16[128,512]{1,0:T(8,128)(2,1)S(1)}, bf16[128,512]{1,0:T(8,128)(2,1)S(1)}, u32[]{:S(2)}, u32[]{:S(2)}) %collective-permute-start.10) | collective-permute-done | bytes 131104 | tf_op jit(solution)/shard_map/ppermute | solution.py:22
  41.6 0.7 collective-permute-done.9.refs_4_
  42.2 1.4 %collective-permute-start.11 = (bf16[128,512]{1,0:T(8,128)(2,1)S(1)}, bf16[128,512]{1,0:T(8,128)(2,1)S(1)}, u32[]{:S(2)}, u32[]{:S(2)}) collective-permute-start(bf16[128,512]{1,0:T(8,128)(2,1)S(1)} %collective-permute-done.9.refs_4_), channel_id=1, source_target_pairs={{0,2},{2,0},{4,6},{6,4},{8,10},{10,8},{12,14},{14,12},{1,3},{3,1},... | collective-permute-start | bytes 393224 | tf_op jit(solution)/shard_map/ppermute | solution.py:22
  43.7 0.0 collective-permute-done.14.refs_1_
  43.7 3.3 %shard_map.88 = (f32[3,128,512]{2,1,0:T(8,128)S(1)}, f32[128,128]{1,0:T(8,128)S(1)}) custom-call(bf16[128,512]{1,0:T(8,128)(2,1)S(1)} %shard_map.86._.refs_0_.coarse_ref, bf16[128,512]{1,0:T(8,128)(2,1)S(1)} %collective-permute-done.14.refs_1_, bf16[128,512]{1,0:T(8,128)(2,1)S(1)} %collective-permute-done.15.refs_2_, ...), custom_call_target="tpu_custom_call" | custom-call | tf_op jit(solution)/shard_map/pallas_call | solution.py:91
  47.0 0.4 collective-permute-done.11.refs_0_
  47.3 0.6 shard_map.89
  47.9 0.1 collective-permute-start.16
  48.0 1.5 %collective-permute-done.16.other_ref = bf16[2,128,512]{2,1,0:T(8,128)(2,1)S(1)} collective-permute-done((bf16[2,128,512]{2,1,0:T(8,128)(2,1)S(1)}, bf16[2,128,512]{2,1,0:T(8,128)(2,1)S(1)}, u32[]{:S(2)}, u32[]{:S(2)}) %collective-permute-start.16) | collective-permute-done | bytes 262176 | tf_op jit(solution)/shard_map/ppermute | solution.py:22
  49.5 1.8 %shard_map.90 = (bf16[128,512]{1,0:T(8,128)(2,1)S(1)}, bf16[128,512]{1,0:T(8,128)(2,1)S(1)}, bf16[128,512]{1,0:T(8,128)(2,1)S(1)}) custom-call(bf16[128,512]{1,0:T(8,128)(2,1)S(1)} %get-tuple-element.53.q_ref, bf16[2,128,512]{2,1,0:T(8,128)(2,1)S(1)} %get-tuple-element.54.own_ref, bf16[2,128,512]{2,1,0:T(8,128)(2,1)S(1)} %collective-permute-done.16.other_ref, ...), custom_call_target="tpu_custom_call" | custom-call | tf_op jit(solution)/shard_map/pallas_call | solution.py:91
  51.3 1.3 %collective-permute-start.18 = (bf16[128,512]{1,0:T(8,128)(2,1)S(1)}, bf16[128,512]{1,0:T(8,128)(2,1)S(1)}, u32[]{:S(2)}, u32[]{:S(2)}) collective-permute-start(bf16[128,512]{1,0:T(8,128)(2,1)S(1)} %get-tuple-element.59), channel_id=1, source_target_pairs={{0,2},{2,0},{4,6},{6,4},{8,10},{10,8},{12,14},{14,12},{1,3},{3,1},... | collective-permute-start | bytes 393224 | tf_op jit(solution)/shard_map/ppermute | solution.py:22
  52.7 0.6 shard_map.91
  53.3 0.8 collective-permute-start.19
  54.1 0.0 collective-permute-start.17
  54.1 3.6 %collective-permute-done.18 = bf16[128,512]{1,0:T(8,128)(2,1)S(1)} collective-permute-done((bf16[128,512]{1,0:T(8,128)(2,1)S(1)}, bf16[128,512]{1,0:T(8,128)(2,1)S(1)}, u32[]{:S(2)}, u32[]{:S(2)}) %collective-permute-start.18) | collective-permute-done | bytes 131104 | tf_op jit(solution)/shard_map/ppermute | solution.py:22
  57.8 2.0 %collective-permute-start.23 = (bf16[128,512]{1,0:T(8,128)(2,1)S(1)}, bf16[128,512]{1,0:T(8,128)(2,1)S(1)}, u32[]{:S(2)}, u32[]{:S(2)}) collective-permute-start(bf16[128,512]{1,0:T(8,128)(2,1)S(1)} %add_convert_fusion.3), channel_id=1, source_target_pairs={{0,12},{2,14},{4,8},{6,10},{8,4},{10,6},{12,0},{14,2},{1,13},{3,15... | collective-permute-start | bytes 393224 | tf_op jit(solution)/shard_map/ppermute | solution.py:22
  59.8 0.9 collective-permute-start.22
  60.7 2.4 %collective-permute-start.21 = (bf16[128,512]{1,0:T(8,128)(2,1)S(1)}, bf16[128,512]{1,0:T(8,128)(2,1)S(1)}, u32[]{:S(2)}, u32[]{:S(2)}) collective-permute-start(bf16[128,512]{1,0:T(8,128)(2,1)S(1)} %get-tuple-element.63), channel_id=1, source_target_pairs={{0,6},{2,4},{4,2},{6,0},{8,14},{10,12},{12,10},{14,8},{1,7},{3,5},... | collective-permute-start | bytes 393224 | tf_op jit(solution)/shard_map/ppermute | solution.py:22
  63.0 0.7 collective-permute-start.20
  63.8 1.6 %collective-permute-done.23.refs_3_ = bf16[128,512]{1,0:T(8,128)(2,1)S(1)} collective-permute-done((bf16[128,512]{1,0:T(8,128)(2,1)S(1)}, bf16[128,512]{1,0:T(8,128)(2,1)S(1)}, u32[]{:S(2)}, u32[]{:S(2)}) %collective-permute-start.23) | collective-permute-done | bytes 131104 | tf_op jit(solution)/shard_map/ppermute | solution.py:22
  65.4 5.2 %collective-permute-done.22.refs_2_ = bf16[128,512]{1,0:T(8,128)(2,1)S(1)} collective-permute-done((bf16[128,512]{1,0:T(8,128)(2,1)S(1)}, bf16[128,512]{1,0:T(8,128)(2,1)S(1)}, u32[]{:S(2)}, u32[]{:S(2)}) %collective-permute-start.22) | collective-permute-done | bytes 131104 | tf_op jit(solution)/shard_map/ppermute | solution.py:22
  70.6 0.8 shard_map.92
  71.4 1.3 %collective-permute-start.25 = (bf16[16,4096]{1,0:T(8,128)(2,1)S(1)}, bf16[16,4096]{1,0:T(8,128)(2,1)S(1)}, u32[]{:S(2)}, u32[]{:S(2)}) collective-permute-start(bf16[16,4096]{1,0:T(8,128)(2,1)S(1)} %get-tuple-element.70), channel_id=1, source_target_pairs={{0,2},{2,0},{4,6},{6,4},{8,10},{10,8},{12,14},{14,12},{1,3},{3,1},... | collective-permute-start | bytes 393224 | tf_op jit(solution)/shard_map/ppermute | solution.py:22
  72.7 0.7 collective-permute-start.27
  73.5 3.6 %collective-permute-done.25 = bf16[16,4096]{1,0:T(8,128)(2,1)S(1)} collective-permute-done((bf16[16,4096]{1,0:T(8,128)(2,1)S(1)}, bf16[16,4096]{1,0:T(8,128)(2,1)S(1)}, u32[]{:S(2)}, u32[]{:S(2)}) %collective-permute-start.25) | collective-permute-done | bytes 131104 | tf_op jit(solution)/shard_map/ppermute | solution.py:22
  77.1 2.2 %collective-permute-start.26 = (bf16[16,4096]{1,0:T(8,128)(2,1)S(1)}, bf16[16,4096]{1,0:T(8,128)(2,1)S(1)}, u32[]{:S(2)}, u32[]{:S(2)}) collective-permute-start(bf16[16,4096]{1,0:T(8,128)(2,1)S(1)} %add_convert_fusion.2), channel_id=1, source_target_pairs={{0,12},{2,14},{4,8},{6,10},{8,4},{10,6},{12,0},{14,2},{1,13},{3,15... | collective-permute-start | bytes 393224 | tf_op jit(solution)/shard_map/ppermute | solution.py:22
  79.3 0.1 collective-permute-start.28
  79.4 3.2 %collective-permute-start.29 = (bf16[16,4096]{1,0:T(8,128)(2,1)S(1)}, bf16[16,4096]{1,0:T(8,128)(2,1)S(1)}, u32[]{:S(2)}, u32[]{:S(2)}) collective-permute-start(bf16[16,4096]{1,0:T(8,128)(2,1)S(1)} %get-tuple-element.74), channel_id=1, source_target_pairs={{0,6},{2,4},{4,2},{6,0},{8,14},{10,12},{12,10},{14,8},{1,7},{3,5},... | collective-permute-start | bytes 393224 | tf_op jit(solution)/shard_map/ppermute | solution.py:22
  82.6 0.5 collective-permute-start.30
  83.1 2.1 %collective-permute-done.26 = bf16[16,4096]{1,0:T(8,128)(2,1)S(1)} collective-permute-done((bf16[16,4096]{1,0:T(8,128)(2,1)S(1)}, bf16[16,4096]{1,0:T(8,128)(2,1)S(1)}, u32[]{:S(2)}, u32[]{:S(2)}) %collective-permute-start.26) | collective-permute-done | bytes 131104 | tf_op jit(solution)/shard_map/ppermute | solution.py:22
  85.2 3.1 %collective-permute-done.28 = bf16[16,4096]{1,0:T(8,128)(2,1)S(1)} collective-permute-done((bf16[16,4096]{1,0:T(8,128)(2,1)S(1)}, bf16[16,4096]{1,0:T(8,128)(2,1)S(1)}, u32[]{:S(2)}, u32[]{:S(2)}) %collective-permute-start.28) | collective-permute-done | bytes 131104 | tf_op jit(solution)/shard_map/ppermute | solution.py:22
  88.4 0.1 convert_add_fusion
  88.5 0.1 reshape.15
  88.6 0.7 add_convert_fusion
  (23 shorter events, 0.2 us)
Async XLA Ops:
  0.8 6.1 %collective-permute-start = (bf16[2,1024]{1,0:T(2,128)(2,1)S(1)}, bf16[2,1024]{1,0:T(2,128)(2,1)S(1)}, u32[]{:S(2)}, u32[]{:S(2)}) collective-permute-start(bf16[2,1024]{1,0:T(2,128)(2,1)S(1)} %get-tuple-element.78), channel_id=1, source_target_pairs={{1,2},{2,1},{3,4},{4,3},{5,6},{6,5},{7,8},{8,7},{9,10},{10,9},{11,... | collective-permute-start | bytes 12296 | tf_op jit(solution)/shard_map/ppermute | solution.py:362
  1.4 5.5 %collective-permute-start.1 = (bf16[2,1024]{1,0:T(2,128)(2,1)S(1)}, bf16[2,1024]{1,0:T(2,128)(2,1)S(1)}, u32[]{:S(2)}, u32[]{:S(2)}) collective-permute-start(bf16[2,1024]{1,0:T(2,128)(2,1)S(1)} %get-tuple-element.77), channel_id=1, source_target_pairs={{0,1},{1,0},{2,3},{3,2},{4,5},{5,4},{6,7},{7,6},{8,9},{9,8},{10,11... | collective-permute-start | bytes 12296 | tf_op jit(solution)/shard_map/ppermute | solution.py:361
  7.3 11.2 %collective-permute-start.2 = (bf16[16,4096]{1,0:T(8,128)(2,1)S(1)}, bf16[16,4096]{1,0:T(8,128)(2,1)S(1)}, u32[]{:S(2)}, u32[]{:S(2)}) collective-permute-start(bf16[16,4096]{1,0:T(8,128)(2,1)S(1)} %reshape.13.refs_2_.refs_0_), channel_id=1, source_target_pairs={{0,8},{2,10},{4,12},{6,14},{8,0},{10,2},{12,4},{14,6},{1,9},{3,11}... | collective-permute-start | bytes 393224 | tf_op jit(solution)/shard_map/ppermute | solution.py:22
  11.1 7.9 %collective-permute-start.3 = (bf16[16,4096]{1,0:T(8,128)(2,1)S(1)}, bf16[16,4096]{1,0:T(8,128)(2,1)S(1)}, u32[]{:S(2)}, u32[]{:S(2)}) collective-permute-start(bf16[16,4096]{1,0:T(8,128)(2,1)S(1)} %reshape.13.refs_2_.refs_0_), channel_id=1, source_target_pairs={{0,6},{2,4},{4,2},{6,0},{8,14},{10,12},{12,10},{14,8},{1,7},{3,5},... | collective-permute-start | bytes 393224 | tf_op jit(solution)/shard_map/ppermute | solution.py:22
  12.7 9.7 %collective-permute-start.5 = (bf16[16,4096]{1,0:T(8,128)(2,1)S(1)}, bf16[16,4096]{1,0:T(8,128)(2,1)S(1)}, u32[]{:S(2)}, u32[]{:S(2)}) collective-permute-start(bf16[16,4096]{1,0:T(8,128)(2,1)S(1)} %reshape.13.refs_2_.refs_0_), channel_id=1, source_target_pairs={{0,12},{2,14},{4,8},{6,10},{8,4},{10,6},{12,0},{14,2},{1,13},{3,15... | collective-permute-start | bytes 393224 | tf_op jit(solution)/shard_map/ppermute | solution.py:22
  13.0 10.2 %collective-permute-start.7 = (bf16[16,4096]{1,0:T(8,128)(2,1)S(1)}, bf16[16,4096]{1,0:T(8,128)(2,1)S(1)}, u32[]{:S(2)}, u32[]{:S(2)}) collective-permute-start(bf16[16,4096]{1,0:T(8,128)(2,1)S(1)} %reshape.13.refs_2_.refs_0_), channel_id=1, source_target_pairs={{0,2},{2,0},{4,6},{6,4},{8,10},{10,8},{12,14},{14,12},{1,3},{3,1},... | collective-permute-start | bytes 393224 | tf_op jit(solution)/shard_map/ppermute | solution.py:22
  14.2 9.6 %collective-permute-start.8 = (bf16[16,4096]{1,0:T(8,128)(2,1)S(1)}, bf16[16,4096]{1,0:T(8,128)(2,1)S(1)}, u32[]{:S(2)}, u32[]{:S(2)}) collective-permute-start(bf16[16,4096]{1,0:T(8,128)(2,1)S(1)} %reshape.13.refs_2_.refs_0_), channel_id=1, source_target_pairs={{0,4},{2,6},{4,0},{6,2},{8,12},{10,14},{12,8},{14,10},{1,5},{3,7},... | collective-permute-start | bytes 393224 | tf_op jit(solution)/shard_map/ppermute | solution.py:22
  19.0 6.9 %collective-permute-start.4 = (bf16[16,4096]{1,0:T(8,128)(2,1)S(1)}, bf16[16,4096]{1,0:T(8,128)(2,1)S(1)}, u32[]{:S(2)}, u32[]{:S(2)}) collective-permute-start(bf16[16,4096]{1,0:T(8,128)(2,1)S(1)} %collective-permute-done.2.refs_4_), channel_id=1, source_target_pairs={{0,2},{2,0},{4,6},{6,4},{8,10},{10,8},{12,14},{14,12},{1,3},{3,1},... | collective-permute-start | bytes 393224 | tf_op jit(solution)/shard_map/ppermute | solution.py:22
  22.4 5.0 %collective-permute-start.6 = (bf16[16,4096]{1,0:T(8,128)(2,1)S(1)}, bf16[16,4096]{1,0:T(8,128)(2,1)S(1)}, u32[]{:S(2)}, u32[]{:S(2)}) collective-permute-start(bf16[16,4096]{1,0:T(8,128)(2,1)S(1)} %collective-permute-done.5.refs_5_), channel_id=1, source_target_pairs={{0,2},{2,0},{4,6},{6,4},{8,10},{10,8},{12,14},{14,12},{1,3},{3,1},... | collective-permute-start | bytes 393224 | tf_op jit(solution)/shard_map/ppermute | solution.py:22
  28.2 15.5 %copy-start = (f32[4096]{0:T(1024)S(1)}, f32[4096]{0:T(1024)}, u32[]{:S(2)}) copy-start(f32[4096]{0:T(1024)} %param.12) | copy-start | bytes 49156
  28.2 9.8 %collective-permute-start.12 = (bf16[128,512]{1,0:T(8,128)(2,1)S(1)}, bf16[128,512]{1,0:T(8,128)(2,1)S(1)}, u32[]{:S(2)}, u32[]{:S(2)}) collective-permute-start(bf16[128,512]{1,0:T(8,128)(2,1)S(1)} %shard_map.86._.refs_0_.coarse_ref), channel_id=1, source_target_pairs={{0,12},{2,14},{4,8},{6,10},{8,4},{10,6},{12,0},{14,2},{1,13},{3,15... | collective-permute-start | bytes 393224 | tf_op jit(solution)/shard_map/ppermute | solution.py:22
  31.2 10.4 %collective-permute-start.10 = (bf16[128,512]{1,0:T(8,128)(2,1)S(1)}, bf16[128,512]{1,0:T(8,128)(2,1)S(1)}, u32[]{:S(2)}, u32[]{:S(2)}) collective-permute-start(bf16[128,512]{1,0:T(8,128)(2,1)S(1)} %shard_map.86._.refs_0_.coarse_ref), channel_id=1, source_target_pairs={{0,6},{2,4},{4,2},{6,0},{8,14},{10,12},{12,10},{14,8},{1,7},{3,5},... | collective-permute-start | bytes 393224 | tf_op jit(solution)/shard_map/ppermute | solution.py:22
  31.3 10.9 %collective-permute-start.9 = (bf16[128,512]{1,0:T(8,128)(2,1)S(1)}, bf16[128,512]{1,0:T(8,128)(2,1)S(1)}, u32[]{:S(2)}, u32[]{:S(2)}) collective-permute-start(bf16[128,512]{1,0:T(8,128)(2,1)S(1)} %shard_map.86._.refs_0_.coarse_ref), channel_id=1, source_target_pairs={{0,8},{2,10},{4,12},{6,14},{8,0},{10,2},{12,4},{14,6},{1,9},{3,11}... | collective-permute-start | bytes 393224 | tf_op jit(solution)/shard_map/ppermute | solution.py:22
  33.9 9.7 %collective-permute-start.14 = (bf16[128,512]{1,0:T(8,128)(2,1)S(1)}, bf16[128,512]{1,0:T(8,128)(2,1)S(1)}, u32[]{:S(2)}, u32[]{:S(2)}) collective-permute-start(bf16[128,512]{1,0:T(8,128)(2,1)S(1)} %shard_map.86._.refs_0_.coarse_ref), channel_id=1, source_target_pairs={{0,2},{2,0},{4,6},{6,4},{8,10},{10,8},{12,14},{14,12},{1,3},{3,1},... | collective-permute-start | bytes 393224 | tf_op jit(solution)/shard_map/ppermute | solution.py:22
  34.1 9.6 %collective-permute-start.15 = (bf16[128,512]{1,0:T(8,128)(2,1)S(1)}, bf16[128,512]{1,0:T(8,128)(2,1)S(1)}, u32[]{:S(2)}, u32[]{:S(2)}) collective-permute-start(bf16[128,512]{1,0:T(8,128)(2,1)S(1)} %shard_map.86._.refs_0_.coarse_ref), channel_id=1, source_target_pairs={{0,4},{2,6},{4,0},{6,2},{8,12},{10,14},{12,8},{14,10},{1,5},{3,7},... | collective-permute-start | bytes 393224 | tf_op jit(solution)/shard_map/ppermute | solution.py:22
  38.0 8.9 %collective-permute-start.13 = (bf16[128,512]{1,0:T(8,128)(2,1)S(1)}, bf16[128,512]{1,0:T(8,128)(2,1)S(1)}, u32[]{:S(2)}, u32[]{:S(2)}) collective-permute-start(bf16[128,512]{1,0:T(8,128)(2,1)S(1)} %collective-permute-done.12.refs_5_), channel_id=1, source_target_pairs={{0,2},{2,0},{4,6},{6,4},{8,10},{10,8},{12,14},{14,12},{1,3},{3,1},... | collective-permute-start | bytes 393224 | tf_op jit(solution)/shard_map/ppermute | solution.py:22
  42.2 5.1 %collective-permute-start.11 = (bf16[128,512]{1,0:T(8,128)(2,1)S(1)}, bf16[128,512]{1,0:T(8,128)(2,1)S(1)}, u32[]{:S(2)}, u32[]{:S(2)}) collective-permute-start(bf16[128,512]{1,0:T(8,128)(2,1)S(1)} %collective-permute-done.9.refs_4_), channel_id=1, source_target_pairs={{0,2},{2,0},{4,6},{6,4},{8,10},{10,8},{12,14},{14,12},{1,3},{3,1},... | collective-permute-start | bytes 393224 | tf_op jit(solution)/shard_map/ppermute | solution.py:22
  47.9 1.6 %collective-permute-start.16 = (bf16[2,128,512]{2,1,0:T(8,128)(2,1)S(1)}, bf16[2,128,512]{2,1,0:T(8,128)(2,1)S(1)}, u32[]{:S(2)}, u32[]{:S(2)}) collective-permute-start(bf16[2,128,512]{2,1,0:T(8,128)(2,1)S(1)} %get-tuple-element.54.own_ref), channel_id=1, source_target_pairs={{0,1},{1,0},{2,3},{3,2},{4,5},{5,4},{6,7},{7,6},{8,9},{9,8},{10,11... | collective-permute-start | bytes 786440 | tf_op jit(solution)/shard_map/ppermute | solution.py:22
  51.3 6.4 %collective-permute-start.18 = (bf16[128,512]{1,0:T(8,128)(2,1)S(1)}, bf16[128,512]{1,0:T(8,128)(2,1)S(1)}, u32[]{:S(2)}, u32[]{:S(2)}) collective-permute-start(bf16[128,512]{1,0:T(8,128)(2,1)S(1)} %get-tuple-element.59), channel_id=1, source_target_pairs={{0,2},{2,0},{4,6},{6,4},{8,10},{10,8},{12,14},{14,12},{1,3},{3,1},... | collective-permute-start | bytes 393224 | tf_op jit(solution)/shard_map/ppermute | solution.py:22
  53.3 6.5 %collective-permute-start.19 = (bf16[128,512]{1,0:T(8,128)(2,1)S(1)}, bf16[128,512]{1,0:T(8,128)(2,1)S(1)}, u32[]{:S(2)}, u32[]{:S(2)}) collective-permute-start(bf16[128,512]{1,0:T(8,128)(2,1)S(1)} %get-tuple-element.60), channel_id=1, source_target_pairs={{0,2},{2,0},{4,6},{6,4},{8,10},{10,8},{12,14},{14,12},{1,3},{3,1},... | collective-permute-start | bytes 393224 | tf_op jit(solution)/shard_map/ppermute | solution.py:22
  54.1 6.6 %collective-permute-start.17 = (bf16[128,512]{1,0:T(8,128)(2,1)S(1)}, bf16[128,512]{1,0:T(8,128)(2,1)S(1)}, u32[]{:S(2)}, u32[]{:S(2)}) collective-permute-start(bf16[128,512]{1,0:T(8,128)(2,1)S(1)} %get-tuple-element.58), channel_id=1, source_target_pairs={{0,4},{2,6},{4,0},{6,2},{8,12},{10,14},{12,8},{14,10},{1,5},{3,7},... | collective-permute-start | bytes 393224 | tf_op jit(solution)/shard_map/ppermute | solution.py:22
  57.8 7.6 %collective-permute-start.23 = (bf16[128,512]{1,0:T(8,128)(2,1)S(1)}, bf16[128,512]{1,0:T(8,128)(2,1)S(1)}, u32[]{:S(2)}, u32[]{:S(2)}) collective-permute-start(bf16[128,512]{1,0:T(8,128)(2,1)S(1)} %add_convert_fusion.3), channel_id=1, source_target_pairs={{0,12},{2,14},{4,8},{6,10},{8,4},{10,6},{12,0},{14,2},{1,13},{3,15... | collective-permute-start | bytes 393224 | tf_op jit(solution)/shard_map/ppermute | solution.py:22
  59.7 28.8 %copy-start.1 = (bf16[64,1024]{1,0:T(8,128)(2,1)S(1)}, bf16[64,1024]{1,0:T(8,128)(2,1)}, u32[]{:S(2)}) copy-start(bf16[64,1024]{1,0:T(8,128)(2,1)} %frames_ref.1) | copy-start | bytes 393220
  59.8 10.8 %collective-permute-start.22 = (bf16[128,512]{1,0:T(8,128)(2,1)S(1)}, bf16[128,512]{1,0:T(8,128)(2,1)S(1)}, u32[]{:S(2)}, u32[]{:S(2)}) collective-permute-start(bf16[128,512]{1,0:T(8,128)(2,1)S(1)} %add_convert_fusion.4), channel_id=1, source_target_pairs={{0,8},{2,10},{4,12},{6,14},{8,0},{10,2},{12,4},{14,6},{1,9},{3,11}... | collective-permute-start | bytes 393224 | tf_op jit(solution)/shard_map/ppermute | solution.py:22
  60.7 9.9 %collective-permute-start.21 = (bf16[128,512]{1,0:T(8,128)(2,1)S(1)}, bf16[128,512]{1,0:T(8,128)(2,1)S(1)}, u32[]{:S(2)}, u32[]{:S(2)}) collective-permute-start(bf16[128,512]{1,0:T(8,128)(2,1)S(1)} %get-tuple-element.63), channel_id=1, source_target_pairs={{0,6},{2,4},{4,2},{6,0},{8,14},{10,12},{12,10},{14,8},{1,7},{3,5},... | collective-permute-start | bytes 393224 | tf_op jit(solution)/shard_map/ppermute | solution.py:22
  63.0 7.5 %collective-permute-start.20 = (bf16[128,512]{1,0:T(8,128)(2,1)S(1)}, bf16[128,512]{1,0:T(8,128)(2,1)S(1)}, u32[]{:S(2)}, u32[]{:S(2)}) collective-permute-start(bf16[128,512]{1,0:T(8,128)(2,1)S(1)} %get-tuple-element.61), channel_id=1, source_target_pairs={{0,2},{2,0},{4,6},{6,4},{8,10},{10,8},{12,14},{14,12},{1,3},{3,1},... | collective-permute-start | bytes 393224 | tf_op jit(solution)/shard_map/ppermute | solution.py:22
  71.4 5.7 %collective-permute-start.25 = (bf16[16,4096]{1,0:T(8,128)(2,1)S(1)}, bf16[16,4096]{1,0:T(8,128)(2,1)S(1)}, u32[]{:S(2)}, u32[]{:S(2)}) collective-permute-start(bf16[16,4096]{1,0:T(8,128)(2,1)S(1)} %get-tuple-element.70), channel_id=1, source_target_pairs={{0,2},{2,0},{4,6},{6,4},{8,10},{10,8},{12,14},{14,12},{1,3},{3,1},... | collective-permute-start | bytes 393224 | tf_op jit(solution)/shard_map/ppermute | solution.py:22
  72.7 6.6 %collective-permute-start.27 = (bf16[16,4096]{1,0:T(8,128)(2,1)S(1)}, bf16[16,4096]{1,0:T(8,128)(2,1)S(1)}, u32[]{:S(2)}, u32[]{:S(2)}) collective-permute-start(bf16[16,4096]{1,0:T(8,128)(2,1)S(1)} %get-tuple-element.72), channel_id=1, source_target_pairs={{0,2},{2,0},{4,6},{6,4},{8,10},{10,8},{12,14},{14,12},{1,3},{3,1},... | collective-permute-start | bytes 393224 | tf_op jit(solution)/shard_map/ppermute | solution.py:22
  73.5 5.9 %collective-permute-start.24 = (bf16[16,4096]{1,0:T(8,128)(2,1)S(1)}, bf16[16,4096]{1,0:T(8,128)(2,1)S(1)}, u32[]{:S(2)}, u32[]{:S(2)}) collective-permute-start(bf16[16,4096]{1,0:T(8,128)(2,1)S(1)} %get-tuple-element.68), channel_id=1, source_target_pairs={{0,4},{2,6},{4,0},{6,2},{8,12},{10,14},{12,8},{14,10},{1,5},{3,7},... | collective-permute-start | bytes 393224 | tf_op jit(solution)/shard_map/ppermute | solution.py:22
  77.1 8.2 %collective-permute-start.26 = (bf16[16,4096]{1,0:T(8,128)(2,1)S(1)}, bf16[16,4096]{1,0:T(8,128)(2,1)S(1)}, u32[]{:S(2)}, u32[]{:S(2)}) collective-permute-start(bf16[16,4096]{1,0:T(8,128)(2,1)S(1)} %add_convert_fusion.2), channel_id=1, source_target_pairs={{0,12},{2,14},{4,8},{6,10},{8,4},{10,6},{12,0},{14,2},{1,13},{3,15... | collective-permute-start | bytes 393224 | tf_op jit(solution)/shard_map/ppermute | solution.py:22
  79.3 9.1 %collective-permute-start.28 = (bf16[16,4096]{1,0:T(8,128)(2,1)S(1)}, bf16[16,4096]{1,0:T(8,128)(2,1)S(1)}, u32[]{:S(2)}, u32[]{:S(2)}) collective-permute-start(bf16[16,4096]{1,0:T(8,128)(2,1)S(1)} %add_convert_fusion.1), channel_id=1, source_target_pairs={{0,8},{2,10},{4,12},{6,14},{8,0},{10,2},{12,4},{14,6},{1,9},{3,11}... | collective-permute-start | bytes 393224 | tf_op jit(solution)/shard_map/ppermute | solution.py:22
  79.4 9.0 %collective-permute-start.29 = (bf16[16,4096]{1,0:T(8,128)(2,1)S(1)}, bf16[16,4096]{1,0:T(8,128)(2,1)S(1)}, u32[]{:S(2)}, u32[]{:S(2)}) collective-permute-start(bf16[16,4096]{1,0:T(8,128)(2,1)S(1)} %get-tuple-element.74), channel_id=1, source_target_pairs={{0,6},{2,4},{4,2},{6,0},{8,14},{10,12},{12,10},{14,8},{1,7},{3,5},... | collective-permute-start | bytes 393224 | tf_op jit(solution)/shard_map/ppermute | solution.py:22
  82.6 5.8 %collective-permute-start.30 = (bf16[16,4096]{1,0:T(8,128)(2,1)S(1)}, bf16[16,4096]{1,0:T(8,128)(2,1)S(1)}, u32[]{:S(2)}, u32[]{:S(2)}) collective-permute-start(bf16[16,4096]{1,0:T(8,128)(2,1)S(1)} %get-tuple-element.76), channel_id=1, source_target_pairs={{0,2},{2,0},{4,6},{6,4},{8,10},{10,8},{12,14},{14,12},{1,3},{3,1},... | collective-permute-start | bytes 393224 | tf_op jit(solution)/shard_map/ppermute | solution.py:22

commit v5 on v4

--- a/solution.py
+++ b/solution.py
@@ -267,24 +267,33 @@
             at += last - first
 
 
-def attend_kernel(plan, q_ref, own_ref, other_ref, w_ref, attended_ref, *out_refs):
+def head_scores(query, keys):
+    return lax.dot_general(
+        query, keys, (((1,), (1,)), ((), ())), preferred_element_type=jnp.float32
+    ) * (1.0 / math.sqrt(HD))
+
+
+def own_scores_kernel(q_ref, own_ref, scores_ref):
+    for head in range(scores_ref.shape[0]):
+        here = slice(head * HD, (head + 1) * HD)
+        scores_ref[head] = head_scores(q_ref[:, here], own_ref[0, :, here])
+
+
+def attend_kernel(
+    plan, q_ref, scores_ref, own_ref, other_ref, w_ref, attended_ref, *out_refs
+):
     columns = q_ref.shape[1]
-    contract = (((1,), (1,)), ((), ()))
     for head in range(columns // HD):
         here = slice(head * HD, (head + 1) * HD)
-        query = q_ref[:, here]
-        scores = [
-            lax.dot_general(query, kv[0, :, here], contract, preferred_element_type=jnp.float32)
-            * (1.0 / math.sqrt(HD))
-            for kv in (own_ref, other_ref)
-        ]
+        scores = [scores_ref[head], head_scores(q_ref[:, here], other_ref[0, :, here])]
         peak = jnp.maximum(*[jnp.max(s, axis=1, keepdims=True) for s in scores])
         weights = [jnp.exp(s - peak) for s in scores]
         norm = sum(jnp.sum(w, axis=1, keepdims=True) for w in weights)
-        attended_ref[:, here] = sum(
-            dot((w / norm).astype(jnp.bfloat16), kv[1, :, here])
+        mixed = sum(
+            dot(w.astype(jnp.bfloat16), kv[1, :, here])
             for w, kv in zip(weights, (own_ref, other_ref))
-        ).astype(jnp.bfloat16)
+        )
+        attended_ref[:, here] = (mixed * (1.0 / norm)).astype(jnp.bfloat16)
     write_chunks(plan, attended_ref, w_ref, out_refs)
 
 
@@ -462,6 +471,14 @@
         squares,
     )
     other_kv = flip(own_kv, "sub", 1)
+    own_scores = call(
+        own_scores_kernel,
+        sds((columns // HD, tokens, tokens), f32),
+        [],
+        "vv",
+        queries,
+        own_kv,
+    )
 
     def planned(plan, width):
         return tuple(
@@ -474,8 +491,9 @@
         functools.partial(attend_kernel, first_plan),
         (sds((tokens, columns), bf16),) + planned(first_plan, columns),
         [],
-        "vvvv",
+        "vvvvv",
         queries,
+        own_scores,
         own_kv,
         other_kv,
         w_out_kept,

time: 89.6 us -> 88.6 us (0.989)
    pallas_call x11 -> x12, Pallas kernels: 18.2 us -> 17.4 us  [call(): pl.pallas_call(body, out_shape=outs, in_specs=specs, out_specs=jax.tree.m...]
where the time goes in v5:
time: 88.6 us; the launch traced here: 88.2 us
  starting transfers between devices  42 us (47%)
  waiting for transfers between devices  26.8 us (30%)
  Pallas kernels  17.4 us (20%)
  other arithmetic  1.65 us (2%)
    ppermute x29, starting transfers between devices, flip(): return lax.ppermute(value, axis, pairs)  36.9 us
    ppermute x29, waiting for transfers between devices, flip(): return lax.ppermute(value, axis, pairs)  26.8 us
    pallas_call x12, Pallas kernels, call(): pl.pallas_call(body, out_shape=outs, in_specs=specs, out_specs=jax.tree.m...  17.4 us
    ppermute x1, starting transfers between devices, edge_rows(): near = lax.ppermute(jnp.where(even, last, first), ('seq', 'sub'), inside)  4.39 us
  transfers between devices with their start and end apart: 31, of which 14 were waited for; matrix products, arithmetic and copies ran while one was open for 0% of the time, Pallas kernels for 16%

profile of v5, /device:TPU:0, one launch (start us, length us, event | category | flops | bytes accessed | tf_op | source)
XLA Modules:
  0.0 88.2 jit_solution(10096225217595257245)
XLA Ops:
  0.0 0.7 broadcast_select_fusion.2
  0.8 0.7 collective-permute-start
  1.4 4.4 %collective-permute-start.1 = (bf16[2,1024]{1,0:T(2,128)(2,1)S(1)}, bf16[2,1024]{1,0:T(2,128)(2,1)S(1)}, u32[]{:S(2)}, u32[]{:S(2)}) collective-permute-start(bf16[2,1024]{1,0:T(2,128)(2,1)S(1)} %get-tuple-element.77), channel_id=1, source_target_pairs={{0,1},{1,0},{2,3},{3,2},{4,5},{5,4},{6,7},{7,6},{8,9},{9,8},{10,11... | collective-permute-start | bytes 12296 | tf_op jit(solution)/shard_map/ppermute | solution.py:370
  5.8 1.1 %shard_map.82 = (f32[64,1024]{1,0:T(8,128)S(1)}, f32[1,1024]{1,0:T(1,128)S(1)}, f32[5,1024]{1,0:T(8,128)S(1)}) custom-call(bf16[64,1024]{1,0:T(8,128)(2,1)} %frames_ref.1, f32[1,1024]{1,0:T(1,128)} %bitcast.4, bf16[5,1024]{1,0:T(8,128)(2,1)} %taps_ref.1), custom_call_target="tpu_custom_call" | custom-call | tf_op jit(solution)/shard_map/pallas_call | solution.py:91
  6.9 0.0 collective-permute-done.1
  6.9 0.3 shard_map.83
  7.2 0.1 reshape.13.refs_2_.refs_0_
  7.3 3.8 %collective-permute-start.2 = (bf16[16,4096]{1,0:T(8,128)(2,1)S(1)}, bf16[16,4096]{1,0:T(8,128)(2,1)S(1)}, u32[]{:S(2)}, u32[]{:S(2)}) collective-permute-start(bf16[16,4096]{1,0:T(8,128)(2,1)S(1)} %reshape.13.refs_2_.refs_0_), channel_id=1, source_target_pairs={{0,8},{2,10},{4,12},{6,14},{8,0},{10,2},{12,4},{14,6},{1,9},{3,11}... | collective-permute-start | bytes 393224 | tf_op jit(solution)/shard_map/ppermute | solution.py:22
  11.1 1.6 %collective-permute-start.3 = (bf16[16,4096]{1,0:T(8,128)(2,1)S(1)}, bf16[16,4096]{1,0:T(8,128)(2,1)S(1)}, u32[]{:S(2)}, u32[]{:S(2)}) collective-permute-start(bf16[16,4096]{1,0:T(8,128)(2,1)S(1)} %reshape.13.refs_2_.refs_0_), channel_id=1, source_target_pairs={{0,6},{2,4},{4,2},{6,0},{8,14},{10,12},{12,10},{14,8},{1,7},{3,5},... | collective-permute-start | bytes 393224 | tf_op jit(solution)/shard_map/ppermute | solution.py:22
  12.7 0.2 collective-permute-start.5
  13.0 1.2 %collective-permute-start.7 = (bf16[16,4096]{1,0:T(8,128)(2,1)S(1)}, bf16[16,4096]{1,0:T(8,128)(2,1)S(1)}, u32[]{:S(2)}, u32[]{:S(2)}) collective-permute-start(bf16[16,4096]{1,0:T(8,128)(2,1)S(1)} %reshape.13.refs_2_.refs_0_), channel_id=1, source_target_pairs={{0,2},{2,0},{4,6},{6,4},{8,10},{10,8},{12,14},{14,12},{1,3},{3,1},... | collective-permute-start | bytes 393224 | tf_op jit(solution)/shard_map/ppermute | solution.py:22
  14.2 0.9 %collective-permute-start.8 = (bf16[16,4096]{1,0:T(8,128)(2,1)S(1)}, bf16[16,4096]{1,0:T(8,128)(2,1)S(1)}, u32[]{:S(2)}, u32[]{:S(2)}) collective-permute-start(bf16[16,4096]{1,0:T(8,128)(2,1)S(1)} %reshape.13.refs_2_.refs_0_), channel_id=1, source_target_pairs={{0,4},{2,6},{4,0},{6,2},{8,12},{10,14},{12,8},{14,10},{1,5},{3,7},... | collective-permute-start | bytes 393224 | tf_op jit(solution)/shard_map/ppermute | solution.py:22
  15.0 3.5 %shard_map.84 = (bf16[4096,512]{1,0:T(8,128)(2,1)S(1)}, bf16[512,4096]{1,0:T(8,128)(2,1)S(1)}) custom-call(bf16[4096,512]{1,0:T(8,128)(2,1)} %refs_0_.1, bf16[512,4096]{1,0:T(8,128)(2,1)} %refs_1_.1, bf16[16,4096]{1,0:T(8,128)(2,1)S(1)} %reshape.13.refs_2_.refs_0_), custom_call_target="tpu_custom_call" | custom-call | tf_op jit(solution)/shard_map/pallas_call | solution.py:91
  18.5 0.0 collective-permute-done.2.refs_4_
  18.5 0.5 collective-permute-done.3.refs_3_
  19.0 2.4 %collective-permute-start.4 = (bf16[16,4096]{1,0:T(8,128)(2,1)S(1)}, bf16[16,4096]{1,0:T(8,128)(2,1)S(1)}, u32[]{:S(2)}, u32[]{:S(2)}) collective-permute-start(bf16[16,4096]{1,0:T(8,128)(2,1)S(1)} %collective-permute-done.2.refs_4_), channel_id=1, source_target_pairs={{0,2},{2,0},{4,6},{6,4},{8,10},{10,8},{12,14},{14,12},{1,3},{3,1},... | collective-permute-start | bytes 393224 | tf_op jit(solution)/shard_map/ppermute | solution.py:22
  21.5 0.9 %collective-permute-done.5.refs_5_ = bf16[16,4096]{1,0:T(8,128)(2,1)S(1)} collective-permute-done((bf16[16,4096]{1,0:T(8,128)(2,1)S(1)}, bf16[16,4096]{1,0:T(8,128)(2,1)S(1)}, u32[]{:S(2)}, u32[]{:S(2)}) %collective-permute-start.5) | collective-permute-done | bytes 131104 | tf_op jit(solution)/shard_map/ppermute | solution.py:22
  22.4 0.8 collective-permute-start.6
  23.2 0.0 collective-permute-done.7.refs_1_
  23.2 0.6 collective-permute-done.8.refs_2_
  23.8 2.2 %shard_map.85 = (bf16[128,512]{1,0:T(8,128)(2,1)S(1)}, bf16[512,4096]{1,0:T(8,128)(2,1)S(1)}) custom-call(bf16[16,4096]{1,0:T(8,128)(2,1)S(1)} %reshape.13.refs_2_.refs_0_, bf16[16,4096]{1,0:T(8,128)(2,1)S(1)} %collective-permute-done.7.refs_1_, bf16[16,4096]{1,0:T(8,128)(2,1)S(1)} %collective-permute-done.8.refs_2_, ...), custom_call_target="tpu_custom_call" | custom-call | tf_op jit(solution)/shard_map/pallas_call | solution.py:91
  26.0 1.4 %collective-permute-done.6.refs_1_ = bf16[16,4096]{1,0:T(8,128)(2,1)S(1)} collective-permute-done((bf16[16,4096]{1,0:T(8,128)(2,1)S(1)}, bf16[16,4096]{1,0:T(8,128)(2,1)S(1)}, u32[]{:S(2)}, u32[]{:S(2)}) %collective-permute-start.6) | collective-permute-done | bytes 131104 | tf_op jit(solution)/shard_map/ppermute | solution.py:22
  27.4 0.8 shard_map.86._.refs_0_.coarse_ref
  28.2 3.0 %collective-permute-start.12 = (bf16[128,512]{1,0:T(8,128)(2,1)S(1)}, bf16[128,512]{1,0:T(8,128)(2,1)S(1)}, u32[]{:S(2)}, u32[]{:S(2)}) collective-permute-start(bf16[128,512]{1,0:T(8,128)(2,1)S(1)} %shard_map.86._.refs_0_.coarse_ref), channel_id=1, source_target_pairs={{0,12},{2,14},{4,8},{6,10},{8,4},{10,6},{12,0},{14,2},{1,13},{3,15... | collective-permute-start | bytes 393224 | tf_op jit(solution)/shard_map/ppermute | solution.py:22
  31.2 0.1 collective-permute-start.10
  31.3 2.6 %collective-permute-start.9 = (bf16[128,512]{1,0:T(8,128)(2,1)S(1)}, bf16[128,512]{1,0:T(8,128)(2,1)S(1)}, u32[]{:S(2)}, u32[]{:S(2)}) collective-permute-start(bf16[128,512]{1,0:T(8,128)(2,1)S(1)} %shard_map.86._.refs_0_.coarse_ref), channel_id=1, source_target_pairs={{0,8},{2,10},{4,12},{6,14},{8,0},{10,2},{12,4},{14,6},{1,9},{3,11}... | collective-permute-start | bytes 393224 | tf_op jit(solution)/shard_map/ppermute | solution.py:22
  33.9 0.2 collective-permute-start.14
  34.1 0.6 collective-permute-start.15
  34.7 3.3 %shard_map.87.refs_8_.refs_3_ = bf16[5,3,512,512]{3,2,1,0:T(8,128)(2,1)S(1)} custom-call(bf16[3,4096,512]{2,1,0:T(8,128)(2,1)} %refs_7_.3, bf16[128,512]{1,0:T(8,128)(2,1)S(1)} %shard_map.86._.refs_0_.coarse_ref), custom_call_target="tpu_custom_call" | custom-call | tf_op jit(solution)/shard_map/pallas_call | solution.py:91
  38.0 1.8 %collective-permute-start.13 = (bf16[128,512]{1,0:T(8,128)(2,1)S(1)}, bf16[128,512]{1,0:T(8,128)(2,1)S(1)}, u32[]{:S(2)}, u32[]{:S(2)}) collective-permute-start(bf16[128,512]{1,0:T(8,128)(2,1)S(1)} %collective-permute-done.12.refs_5_), channel_id=1, source_target_pairs={{0,2},{2,0},{4,6},{6,4},{8,10},{10,8},{12,14},{14,12},{1,3},{3,1},... | collective-permute-start | bytes 393224 | tf_op jit(solution)/shard_map/ppermute | solution.py:22
  39.8 1.7 %collective-permute-done.10.refs_3_ = bf16[128,512]{1,0:T(8,128)(2,1)S(1)} collective-permute-done((bf16[128,512]{1,0:T(8,128)(2,1)S(1)}, bf16[128,512]{1,0:T(8,128)(2,1)S(1)}, u32[]{:S(2)}, u32[]{:S(2)}) %collective-permute-start.10) | collective-permute-done | bytes 131104 | tf_op jit(solution)/shard_map/ppermute | solution.py:22
  41.6 0.7 collective-permute-done.9.refs_4_
  42.2 1.4 %collective-permute-start.11 = (bf16[128,512]{1,0:T(8,128)(2,1)S(1)}, bf16[128,512]{1,0:T(8,128)(2,1)S(1)}, u32[]{:S(2)}, u32[]{:S(2)}) collective-permute-start(bf16[128,512]{1,0:T(8,128)(2,1)S(1)} %collective-permute-done.9.refs_4_), channel_id=1, source_target_pairs={{0,2},{2,0},{4,6},{6,4},{8,10},{10,8},{12,14},{14,12},{1,3},{3,1},... | collective-permute-start | bytes 393224 | tf_op jit(solution)/shard_map/ppermute | solution.py:22
  43.7 3.3 %shard_map.88 = (f32[3,128,512]{2,1,0:T(8,128)S(1)}, f32[128,128]{1,0:T(8,128)S(1)}) custom-call(bf16[128,512]{1,0:T(8,128)(2,1)S(1)} %shard_map.86._.refs_0_.coarse_ref, bf16[128,512]{1,0:T(8,128)(2,1)S(1)} %collective-permute-done.14.refs_1_, bf16[128,512]{1,0:T(8,128)(2,1)S(1)} %collective-permute-done.15.refs_2_, ...), custom_call_target="tpu_custom_call" | custom-call | tf_op jit(solution)/shard_map/pallas_call | solution.py:91
  47.0 0.4 collective-permute-done.11.refs_0_
  47.3 0.6 shard_map.89
  47.9 0.1 collective-permute-start.16
  48.0 0.2 shard_map.90.scores_ref
  48.2 1.3 %collective-permute-done.16.other_ref = bf16[2,128,512]{2,1,0:T(8,128)(2,1)S(1)} collective-permute-done((bf16[2,128,512]{2,1,0:T(8,128)(2,1)S(1)}, bf16[2,128,512]{2,1,0:T(8,128)(2,1)S(1)}, u32[]{:S(2)}, u32[]{:S(2)}) %collective-permute-start.16) | collective-permute-done | bytes 262176 | tf_op jit(solution)/shard_map/ppermute | solution.py:22
  49.5 0.8 shard_map.91
  50.3 1.3 %collective-permute-start.18 = (bf16[128,512]{1,0:T(8,128)(2,1)S(1)}, bf16[128,512]{1,0:T(8,128)(2,1)S(1)}, u32[]{:S(2)}, u32[]{:S(2)}) collective-permute-start(bf16[128,512]{1,0:T(8,128)(2,1)S(1)} %get-tuple-element.59), channel_id=1, source_target_pairs={{0,2},{2,0},{4,6},{6,4},{8,10},{10,8},{12,14},{14,12},{1,3},{3,1},... | collective-permute-start | bytes 393224 | tf_op jit(solution)/shard_map/ppermute | solution.py:22
  51.6 0.6 shard_map.92
  52.2 0.8 collective-permute-start.19
  53.0 0.0 collective-permute-start.17
  53.1 3.6 %collective-permute-done.18 = bf16[128,512]{1,0:T(8,128)(2,1)S(1)} collective-permute-done((bf16[128,512]{1,0:T(8,128)(2,1)S(1)}, bf16[128,512]{1,0:T(8,128)(2,1)S(1)}, u32[]{:S(2)}, u32[]{:S(2)}) %collective-permute-start.18) | collective-permute-done | bytes 131104 | tf_op jit(solution)/shard_map/ppermute | solution.py:22
  56.7 2.0 %collective-permute-start.23 = (bf16[128,512]{1,0:T(8,128)(2,1)S(1)}, bf16[128,512]{1,0:T(8,128)(2,1)S(1)}, u32[]{:S(2)}, u32[]{:S(2)}) collective-permute-start(bf16[128,512]{1,0:T(8,128)(2,1)S(1)} %add_convert_fusion.3), channel_id=1, source_target_pairs={{0,12},{2,14},{4,8},{6,10},{8,4},{10,6},{12,0},{14,2},{1,13},{3,15... | collective-permute-start | bytes 393224 | tf_op jit(solution)/shard_map/ppermute | solution.py:22
  58.7 0.9 collective-permute-start.22
  59.6 2.4 %collective-permute-start.21 = (bf16[128,512]{1,0:T(8,128)(2,1)S(1)}, bf16[128,512]{1,0:T(8,128)(2,1)S(1)}, u32[]{:S(2)}, u32[]{:S(2)}) collective-permute-start(bf16[128,512]{1,0:T(8,128)(2,1)S(1)} %get-tuple-element.63), channel_id=1, source_target_pairs={{0,6},{2,4},{4,2},{6,0},{8,14},{10,12},{12,10},{14,8},{1,7},{3,5},... | collective-permute-start | bytes 393224 | tf_op jit(solution)/shard_map/ppermute | solution.py:22
  62.0 0.7 collective-permute-start.20
  62.8 1.6 %collective-permute-done.23.refs_3_ = bf16[128,512]{1,0:T(8,128)(2,1)S(1)} collective-permute-done((bf16[128,512]{1,0:T(8,128)(2,1)S(1)}, bf16[128,512]{1,0:T(8,128)(2,1)S(1)}, u32[]{:S(2)}, u32[]{:S(2)}) %collective-permute-start.23) | collective-permute-done | bytes 131104 | tf_op jit(solution)/shard_map/ppermute | solution.py:22
  64.4 5.2 %collective-permute-done.22.refs_2_ = bf16[128,512]{1,0:T(8,128)(2,1)S(1)} collective-permute-done((bf16[128,512]{1,0:T(8,128)(2,1)S(1)}, bf16[128,512]{1,0:T(8,128)(2,1)S(1)}, u32[]{:S(2)}, u32[]{:S(2)}) %collective-permute-start.22) | collective-permute-done | bytes 131104 | tf_op jit(solution)/shard_map/ppermute | solution.py:22
  69.5 0.8 shard_map.93
  70.3 1.3 %collective-permute-start.25 = (bf16[16,4096]{1,0:T(8,128)(2,1)S(1)}, bf16[16,4096]{1,0:T(8,128)(2,1)S(1)}, u32[]{:S(2)}, u32[]{:S(2)}) collective-permute-start(bf16[16,4096]{1,0:T(8,128)(2,1)S(1)} %get-tuple-element.70), channel_id=1, source_target_pairs={{0,2},{2,0},{4,6},{6,4},{8,10},{10,8},{12,14},{14,12},{1,3},{3,1},... | collective-permute-start | bytes 393224 | tf_op jit(solution)/shard_map/ppermute | solution.py:22
  71.7 0.7 collective-permute-start.27
  72.4 3.6 %collective-permute-done.25 = bf16[16,4096]{1,0:T(8,128)(2,1)S(1)} collective-permute-done((bf16[16,4096]{1,0:T(8,128)(2,1)S(1)}, bf16[16,4096]{1,0:T(8,128)(2,1)S(1)}, u32[]{:S(2)}, u32[]{:S(2)}) %collective-permute-start.25) | collective-permute-done | bytes 131104 | tf_op jit(solution)/shard_map/ppermute | solution.py:22
  76.0 2.2 %collective-permute-start.26 = (bf16[16,4096]{1,0:T(8,128)(2,1)S(1)}, bf16[16,4096]{1,0:T(8,128)(2,1)S(1)}, u32[]{:S(2)}, u32[]{:S(2)}) collective-permute-start(bf16[16,4096]{1,0:T(8,128)(2,1)S(1)} %add_convert_fusion.2), channel_id=1, source_target_pairs={{0,12},{2,14},{4,8},{6,10},{8,4},{10,6},{12,0},{14,2},{1,13},{3,15... | collective-permute-start | bytes 393224 | tf_op jit(solution)/shard_map/ppermute | solution.py:22
  78.3 0.1 collective-permute-start.28
  78.4 3.3 %collective-permute-start.29 = (bf16[16,4096]{1,0:T(8,128)(2,1)S(1)}, bf16[16,4096]{1,0:T(8,128)(2,1)S(1)}, u32[]{:S(2)}, u32[]{:S(2)}) collective-permute-start(bf16[16,4096]{1,0:T(8,128)(2,1)S(1)} %get-tuple-element.74), channel_id=1, source_target_pairs={{0,6},{2,4},{4,2},{6,0},{8,14},{10,12},{12,10},{14,8},{1,7},{3,5},... | collective-permute-start | bytes 393224 | tf_op jit(solution)/shard_map/ppermute | solution.py:22
  81.6 0.4 collective-permute-start.30
  82.1 2.2 %collective-permute-done.26 = bf16[16,4096]{1,0:T(8,128)(2,1)S(1)} collective-permute-done((bf16[16,4096]{1,0:T(8,128)(2,1)S(1)}, bf16[16,4096]{1,0:T(8,128)(2,1)S(1)}, u32[]{:S(2)}, u32[]{:S(2)}) %collective-permute-start.26) | collective-permute-done | bytes 131104 | tf_op jit(solution)/shard_map/ppermute | solution.py:22
  84.3 3.0 %collective-permute-done.28 = bf16[16,4096]{1,0:T(8,128)(2,1)S(1)} collective-permute-done((bf16[16,4096]{1,0:T(8,128)(2,1)S(1)}, bf16[16,4096]{1,0:T(8,128)(2,1)S(1)}, u32[]{:S(2)}, u32[]{:S(2)}) %collective-permute-start.28) | collective-permute-done | bytes 131104 | tf_op jit(solution)/shard_map/ppermute | solution.py:22
  87.3 0.1 convert_add_fusion
  87.4 0.1 reshape.15
  87.5 0.7 add_convert_fusion
  (24 shorter events, 0.2 us)
Async XLA Ops:
  0.8 6.1 %collective-permute-start = (bf16[2,1024]{1,0:T(2,128)(2,1)S(1)}, bf16[2,1024]{1,0:T(2,128)(2,1)S(1)}, u32[]{:S(2)}, u32[]{:S(2)}) collective-permute-start(bf16[2,1024]{1,0:T(2,128)(2,1)S(1)} %get-tuple-element.78), channel_id=1, source_target_pairs={{1,2},{2,1},{3,4},{4,3},{5,6},{6,5},{7,8},{8,7},{9,10},{10,9},{11,... | collective-permute-start | bytes 12296 | tf_op jit(solution)/shard_map/ppermute | solution.py:371
  1.4 5.5 %collective-permute-start.1 = (bf16[2,1024]{1,0:T(2,128)(2,1)S(1)}, bf16[2,1024]{1,0:T(2,128)(2,1)S(1)}, u32[]{:S(2)}, u32[]{:S(2)}) collective-permute-start(bf16[2,1024]{1,0:T(2,128)(2,1)S(1)} %get-tuple-element.77), channel_id=1, source_target_pairs={{0,1},{1,0},{2,3},{3,2},{4,5},{5,4},{6,7},{7,6},{8,9},{9,8},{10,11... | collective-permute-start | bytes 12296 | tf_op jit(solution)/shard_map/ppermute | solution.py:370
  7.3 11.2 %collective-permute-start.2 = (bf16[16,4096]{1,0:T(8,128)(2,1)S(1)}, bf16[16,4096]{1,0:T(8,128)(2,1)S(1)}, u32[]{:S(2)}, u32[]{:S(2)}) collective-permute-start(bf16[16,4096]{1,0:T(8,128)(2,1)S(1)} %reshape.13.refs_2_.refs_0_), channel_id=1, source_target_pairs={{0,8},{2,10},{4,12},{6,14},{8,0},{10,2},{12,4},{14,6},{1,9},{3,11}... | collective-permute-start | bytes 393224 | tf_op jit(solution)/shard_map/ppermute | solution.py:22
  11.1 7.9 %collective-permute-start.3 = (bf16[16,4096]{1,0:T(8,128)(2,1)S(1)}, bf16[16,4096]{1,0:T(8,128)(2,1)S(1)}, u32[]{:S(2)}, u32[]{:S(2)}) collective-permute-start(bf16[16,4096]{1,0:T(8,128)(2,1)S(1)} %reshape.13.refs_2_.refs_0_), channel_id=1, source_target_pairs={{0,6},{2,4},{4,2},{6,0},{8,14},{10,12},{12,10},{14,8},{1,7},{3,5},... | collective-permute-start | bytes 393224 | tf_op jit(solution)/shard_map/ppermute | solution.py:22
  12.7 9.7 %collective-permute-start.5 = (bf16[16,4096]{1,0:T(8,128)(2,1)S(1)}, bf16[16,4096]{1,0:T(8,128)(2,1)S(1)}, u32[]{:S(2)}, u32[]{:S(2)}) collective-permute-start(bf16[16,4096]{1,0:T(8,128)(2,1)S(1)} %reshape.13.refs_2_.refs_0_), channel_id=1, source_target_pairs={{0,12},{2,14},{4,8},{6,10},{8,4},{10,6},{12,0},{14,2},{1,13},{3,15... | collective-permute-start | bytes 393224 | tf_op jit(solution)/shard_map/ppermute | solution.py:22
  13.0 10.2 %collective-permute-start.7 = (bf16[16,4096]{1,0:T(8,128)(2,1)S(1)}, bf16[16,4096]{1,0:T(8,128)(2,1)S(1)}, u32[]{:S(2)}, u32[]{:S(2)}) collective-permute-start(bf16[16,4096]{1,0:T(8,128)(2,1)S(1)} %reshape.13.refs_2_.refs_0_), channel_id=1, source_target_pairs={{0,2},{2,0},{4,6},{6,4},{8,10},{10,8},{12,14},{14,12},{1,3},{3,1},... | collective-permute-start | bytes 393224 | tf_op jit(solution)/shard_map/ppermute | solution.py:22
  14.2 9.6 %collective-permute-start.8 = (bf16[16,4096]{1,0:T(8,128)(2,1)S(1)}, bf16[16,4096]{1,0:T(8,128)(2,1)S(1)}, u32[]{:S(2)}, u32[]{:S(2)}) collective-permute-start(bf16[16,4096]{1,0:T(8,128)(2,1)S(1)} %reshape.13.refs_2_.refs_0_), channel_id=1, source_target_pairs={{0,4},{2,6},{4,0},{6,2},{8,12},{10,14},{12,8},{14,10},{1,5},{3,7},... | collective-permute-start | bytes 393224 | tf_op jit(solution)/shard_map/ppermute | solution.py:22
  19.0 6.9 %collective-permute-start.4 = (bf16[16,4096]{1,0:T(8,128)(2,1)S(1)}, bf16[16,4096]{1,0:T(8,128)(2,1)S(1)}, u32[]{:S(2)}, u32[]{:S(2)}) collective-permute-start(bf16[16,4096]{1,0:T(8,128)(2,1)S(1)} %collective-permute-done.2.refs_4_), channel_id=1, source_target_pairs={{0,2},{2,0},{4,6},{6,4},{8,10},{10,8},{12,14},{14,12},{1,3},{3,1},... | collective-permute-start | bytes 393224 | tf_op jit(solution)/shard_map/ppermute | solution.py:22
  22.4 5.0 %collective-permute-start.6 = (bf16[16,4096]{1,0:T(8,128)(2,1)S(1)}, bf16[16,4096]{1,0:T(8,128)(2,1)S(1)}, u32[]{:S(2)}, u32[]{:S(2)}) collective-permute-start(bf16[16,4096]{1,0:T(8,128)(2,1)S(1)} %collective-permute-done.5.refs_5_), channel_id=1, source_target_pairs={{0,2},{2,0},{4,6},{6,4},{8,10},{10,8},{12,14},{14,12},{1,3},{3,1},... | collective-permute-start | bytes 393224 | tf_op jit(solution)/shard_map/ppermute | solution.py:22
  28.2 15.5 %copy-start = (f32[4096]{0:T(1024)S(1)}, f32[4096]{0:T(1024)}, u32[]{:S(2)}) copy-start(f32[4096]{0:T(1024)} %param.12) | copy-start | bytes 49156
  28.2 9.8 %collective-permute-start.12 = (bf16[128,512]{1,0:T(8,128)(2,1)S(1)}, bf16[128,512]{1,0:T(8,128)(2,1)S(1)}, u32[]{:S(2)}, u32[]{:S(2)}) collective-permute-start(bf16[128,512]{1,0:T(8,128)(2,1)S(1)} %shard_map.86._.refs_0_.coarse_ref), channel_id=1, source_target_pairs={{0,12},{2,14},{4,8},{6,10},{8,4},{10,6},{12,0},{14,2},{1,13},{3,15... | collective-permute-start | bytes 393224 | tf_op jit(solution)/shard_map/ppermute | solution.py:22
  31.2 10.4 %collective-permute-start.10 = (bf16[128,512]{1,0:T(8,128)(2,1)S(1)}, bf16[128,512]{1,0:T(8,128)(2,1)S(1)}, u32[]{:S(2)}, u32[]{:S(2)}) collective-permute-start(bf16[128,512]{1,0:T(8,128)(2,1)S(1)} %shard_map.86._.refs_0_.coarse_ref), channel_id=1, source_target_pairs={{0,6},{2,4},{4,2},{6,0},{8,14},{10,12},{12,10},{14,8},{1,7},{3,5},... | collective-permute-start | bytes 393224 | tf_op jit(solution)/shard_map/ppermute | solution.py:22
  31.3 10.9 %collective-permute-start.9 = (bf16[128,512]{1,0:T(8,128)(2,1)S(1)}, bf16[128,512]{1,0:T(8,128)(2,1)S(1)}, u32[]{:S(2)}, u32[]{:S(2)}) collective-permute-start(bf16[128,512]{1,0:T(8,128)(2,1)S(1)} %shard_map.86._.refs_0_.coarse_ref), channel_id=1, source_target_pairs={{0,8},{2,10},{4,12},{6,14},{8,0},{10,2},{12,4},{14,6},{1,9},{3,11}... | collective-permute-start | bytes 393224 | tf_op jit(solution)/shard_map/ppermute | solution.py:22
  33.9 9.7 %collective-permute-start.14 = (bf16[128,512]{1,0:T(8,128)(2,1)S(1)}, bf16[128,512]{1,0:T(8,128)(2,1)S(1)}, u32[]{:S(2)}, u32[]{:S(2)}) collective-permute-start(bf16[128,512]{1,0:T(8,128)(2,1)S(1)} %shard_map.86._.refs_0_.coarse_ref), channel_id=1, source_target_pairs={{0,2},{2,0},{4,6},{6,4},{8,10},{10,8},{12,14},{14,12},{1,3},{3,1},... | collective-permute-start | bytes 393224 | tf_op jit(solution)/shard_map/ppermute | solution.py:22
  34.1 9.6 %collective-permute-start.15 = (bf16[128,512]{1,0:T(8,128)(2,1)S(1)}, bf16[128,512]{1,0:T(8,128)(2,1)S(1)}, u32[]{:S(2)}, u32[]{:S(2)}) collective-permute-start(bf16[128,512]{1,0:T(8,128)(2,1)S(1)} %shard_map.86._.refs_0_.coarse_ref), channel_id=1, source_target_pairs={{0,4},{2,6},{4,0},{6,2},{8,12},{10,14},{12,8},{14,10},{1,5},{3,7},... | collective-permute-start | bytes 393224 | tf_op jit(solution)/shard_map/ppermute | solution.py:22
  38.0 8.9 %collective-permute-start.13 = (bf16[128,512]{1,0:T(8,128)(2,1)S(1)}, bf16[128,512]{1,0:T(8,128)(2,1)S(1)}, u32[]{:S(2)}, u32[]{:S(2)}) collective-permute-start(bf16[128,512]{1,0:T(8,128)(2,1)S(1)} %collective-permute-done.12.refs_5_), channel_id=1, source_target_pairs={{0,2},{2,0},{4,6},{6,4},{8,10},{10,8},{12,14},{14,12},{1,3},{3,1},... | collective-permute-start | bytes 393224 | tf_op jit(solution)/shard_map/ppermute | solution.py:22
  42.2 5.1 %collective-permute-start.11 = (bf16[128,512]{1,0:T(8,128)(2,1)S(1)}, bf16[128,512]{1,0:T(8,128)(2,1)S(1)}, u32[]{:S(2)}, u32[]{:S(2)}) collective-permute-start(bf16[128,512]{1,0:T(8,128)(2,1)S(1)} %collective-permute-done.9.refs_4_), channel_id=1, source_target_pairs={{0,2},{2,0},{4,6},{6,4},{8,10},{10,8},{12,14},{14,12},{1,3},{3,1},... | collective-permute-start | bytes 393224 | tf_op jit(solution)/shard_map/ppermute | solution.py:22
  47.9 1.6 %collective-permute-start.16 = (bf16[2,128,512]{2,1,0:T(8,128)(2,1)S(1)}, bf16[2,128,512]{2,1,0:T(8,128)(2,1)S(1)}, u32[]{:S(2)}, u32[]{:S(2)}) collective-permute-start(bf16[2,128,512]{2,1,0:T(8,128)(2,1)S(1)} %get-tuple-element.54.own_ref), channel_id=1, source_target_pairs={{0,1},{1,0},{2,3},{3,2},{4,5},{5,4},{6,7},{7,6},{8,9},{9,8},{10,11... | collective-permute-start | bytes 786440 | tf_op jit(solution)/shard_map/ppermute | solution.py:22
  50.3 6.4 %collective-permute-start.18 = (bf16[128,512]{1,0:T(8,128)(2,1)S(1)}, bf16[128,512]{1,0:T(8,128)(2,1)S(1)}, u32[]{:S(2)}, u32[]{:S(2)}) collective-permute-start(bf16[128,512]{1,0:T(8,128)(2,1)S(1)} %get-tuple-element.59), channel_id=1, source_target_pairs={{0,2},{2,0},{4,6},{6,4},{8,10},{10,8},{12,14},{14,12},{1,3},{3,1},... | collective-permute-start | bytes 393224 | tf_op jit(solution)/shard_map/ppermute | solution.py:22
  52.2 6.5 %collective-permute-start.19 = (bf16[128,512]{1,0:T(8,128)(2,1)S(1)}, bf16[128,512]{1,0:T(8,128)(2,1)S(1)}, u32[]{:S(2)}, u32[]{:S(2)}) collective-permute-start(bf16[128,512]{1,0:T(8,128)(2,1)S(1)} %get-tuple-element.60), channel_id=1, source_target_pairs={{0,2},{2,0},{4,6},{6,4},{8,10},{10,8},{12,14},{14,12},{1,3},{3,1},... | collective-permute-start | bytes 393224 | tf_op jit(solution)/shard_map/ppermute | solution.py:22
  53.0 6.6 %collective-permute-start.17 = (bf16[128,512]{1,0:T(8,128)(2,1)S(1)}, bf16[128,512]{1,0:T(8,128)(2,1)S(1)}, u32[]{:S(2)}, u32[]{:S(2)}) collective-permute-start(bf16[128,512]{1,0:T(8,128)(2,1)S(1)} %get-tuple-element.58), channel_id=1, source_target_pairs={{0,4},{2,6},{4,0},{6,2},{8,12},{10,14},{12,8},{14,10},{1,5},{3,7},... | collective-permute-start | bytes 393224 | tf_op jit(solution)/shard_map/ppermute | solution.py:22
  56.7 7.6 %collective-permute-start.23 = (bf16[128,512]{1,0:T(8,128)(2,1)S(1)}, bf16[128,512]{1,0:T(8,128)(2,1)S(1)}, u32[]{:S(2)}, u32[]{:S(2)}) collective-permute-start(bf16[128,512]{1,0:T(8,128)(2,1)S(1)} %add_convert_fusion.3), channel_id=1, source_target_pairs={{0,12},{2,14},{4,8},{6,10},{8,4},{10,6},{12,0},{14,2},{1,13},{3,15... | collective-permute-start | bytes 393224 | tf_op jit(solution)/shard_map/ppermute | solution.py:22
  58.7 28.8 %copy-start.1 = (bf16[64,1024]{1,0:T(8,128)(2,1)S(1)}, bf16[64,1024]{1,0:T(8,128)(2,1)}, u32[]{:S(2)}) copy-start(bf16[64,1024]{1,0:T(8,128)(2,1)} %frames_ref.1) | copy-start | bytes 393220
  58.7 10.8 %collective-permute-start.22 = (bf16[128,512]{1,0:T(8,128)(2,1)S(1)}, bf16[128,512]{1,0:T(8,128)(2,1)S(1)}, u32[]{:S(2)}, u32[]{:S(2)}) collective-permute-start(bf16[128,512]{1,0:T(8,128)(2,1)S(1)} %add_convert_fusion.4), channel_id=1, source_target_pairs={{0,8},{2,10},{4,12},{6,14},{8,0},{10,2},{12,4},{14,6},{1,9},{3,11}... | collective-permute-start | bytes 393224 | tf_op jit(solution)/shard_map/ppermute | solution.py:22
  59.6 9.9 %collective-permute-start.21 = (bf16[128,512]{1,0:T(8,128)(2,1)S(1)}, bf16[128,512]{1,0:T(8,128)(2,1)S(1)}, u32[]{:S(2)}, u32[]{:S(2)}) collective-permute-start(bf16[128,512]{1,0:T(8,128)(2,1)S(1)} %get-tuple-element.63), channel_id=1, source_target_pairs={{0,6},{2,4},{4,2},{6,0},{8,14},{10,12},{12,10},{14,8},{1,7},{3,5},... | collective-permute-start | bytes 393224 | tf_op jit(solution)/shard_map/ppermute | solution.py:22
  62.0 7.5 %collective-permute-start.20 = (bf16[128,512]{1,0:T(8,128)(2,1)S(1)}, bf16[128,512]{1,0:T(8,128)(2,1)S(1)}, u32[]{:S(2)}, u32[]{:S(2)}) collective-permute-start(bf16[128,512]{1,0:T(8,128)(2,1)S(1)} %get-tuple-element.61), channel_id=1, source_target_pairs={{0,2},{2,0},{4,6},{6,4},{8,10},{10,8},{12,14},{14,12},{1,3},{3,1},... | collective-permute-start | bytes 393224 | tf_op jit(solution)/shard_map/ppermute | solution.py:22
  70.3 5.7 %collective-permute-start.25 = (bf16[16,4096]{1,0:T(8,128)(2,1)S(1)}, bf16[16,4096]{1,0:T(8,128)(2,1)S(1)}, u32[]{:S(2)}, u32[]{:S(2)}) collective-permute-start(bf16[16,4096]{1,0:T(8,128)(2,1)S(1)} %get-tuple-element.70), channel_id=1, source_target_pairs={{0,2},{2,0},{4,6},{6,4},{8,10},{10,8},{12,14},{14,12},{1,3},{3,1},... | collective-permute-start | bytes 393224 | tf_op jit(solution)/shard_map/ppermute | solution.py:22
  71.7 6.6 %collective-permute-start.27 = (bf16[16,4096]{1,0:T(8,128)(2,1)S(1)}, bf16[16,4096]{1,0:T(8,128)(2,1)S(1)}, u32[]{:S(2)}, u32[]{:S(2)}) collective-permute-start(bf16[16,4096]{1,0:T(8,128)(2,1)S(1)} %get-tuple-element.72), channel_id=1, source_target_pairs={{0,2},{2,0},{4,6},{6,4},{8,10},{10,8},{12,14},{14,12},{1,3},{3,1},... | collective-permute-start | bytes 393224 | tf_op jit(solution)/shard_map/ppermute | solution.py:22
  72.4 5.9 %collective-permute-start.24 = (bf16[16,4096]{1,0:T(8,128)(2,1)S(1)}, bf16[16,4096]{1,0:T(8,128)(2,1)S(1)}, u32[]{:S(2)}, u32[]{:S(2)}) collective-permute-start(bf16[16,4096]{1,0:T(8,128)(2,1)S(1)} %get-tuple-element.68), channel_id=1, source_target_pairs={{0,4},{2,6},{4,0},{6,2},{8,12},{10,14},{12,8},{14,10},{1,5},{3,7},... | collective-permute-start | bytes 393224 | tf_op jit(solution)/shard_map/ppermute | solution.py:22
  76.0 8.3 %collective-permute-start.26 = (bf16[16,4096]{1,0:T(8,128)(2,1)S(1)}, bf16[16,4096]{1,0:T(8,128)(2,1)S(1)}, u32[]{:S(2)}, u32[]{:S(2)}) collective-permute-start(bf16[16,4096]{1,0:T(8,128)(2,1)S(1)} %add_convert_fusion.2), channel_id=1, source_target_pairs={{0,12},{2,14},{4,8},{6,10},{8,4},{10,6},{12,0},{14,2},{1,13},{3,15... | collective-permute-start | bytes 393224 | tf_op jit(solution)/shard_map/ppermute | solution.py:22
  78.3 9.1 %collective-permute-start.28 = (bf16[16,4096]{1,0:T(8,128)(2,1)S(1)}, bf16[16,4096]{1,0:T(8,128)(2,1)S(1)}, u32[]{:S(2)}, u32[]{:S(2)}) collective-permute-start(bf16[16,4096]{1,0:T(8,128)(2,1)S(1)} %add_convert_fusion.1), channel_id=1, source_target_pairs={{0,8},{2,10},{4,12},{6,14},{8,0},{10,2},{12,4},{14,6},{1,9},{3,11}... | collective-permute-start | bytes 393224 | tf_op jit(solution)/shard_map/ppermute | solution.py:22
  78.4 9.0 %collective-permute-start.29 = (bf16[16,4096]{1,0:T(8,128)(2,1)S(1)}, bf16[16,4096]{1,0:T(8,128)(2,1)S(1)}, u32[]{:S(2)}, u32[]{:S(2)}) collective-permute-start(bf16[16,4096]{1,0:T(8,128)(2,1)S(1)} %get-tuple-element.74), channel_id=1, source_target_pairs={{0,6},{2,4},{4,2},{6,0},{8,14},{10,12},{12,10},{14,8},{1,7},{3,5},... | collective-permute-start | bytes 393224 | tf_op jit(solution)/shard_map/ppermute | solution.py:22
  81.6 5.7 %collective-permute-start.30 = (bf16[16,4096]{1,0:T(8,128)(2,1)S(1)}, bf16[16,4096]{1,0:T(8,128)(2,1)S(1)}, u32[]{:S(2)}, u32[]{:S(2)}) collective-permute-start(bf16[16,4096]{1,0:T(8,128)(2,1)S(1)} %get-tuple-element.76), channel_id=1, source_target_pairs={{0,2},{2,0},{4,6},{6,4},{8,10},{10,8},{12,14},{14,12},{1,3},{3,1},... | collective-permute-start | bytes 393224 | tf_op jit(solution)/shard_map/ppermute | solution.py:22
